TPU v7x, 32 devices: a whole 2x2x4 slice. The times are simulated.
32 devices in a mesh: dp: 8 (over z, core), tensor: 4 (over y, x).
Axes of the slice: x: 2, y: 2, z: 4, core: 2. Of those that a mesh axis runs over, the one named last changes fastest.
Arguments:
- hidden_in: bfloat16 [2, 4096, 2048], P(None, ('dp', 'tensor')), may hold values from -6 to 6
- cotangent: bfloat16 [2, 4096, 2048], P(None, ('dp', 'tensor')), may hold values from -6 to 6
- segment_ids: int32 [2, 4096], P(None, 'dp'), may hold values from 0 to 8, as said below
- positions: int32 [2, 4096], P(None, 'dp'), may hold values from 0 to 399, as said below
- pad_mask: int32 [2, 4096], P(None, 'dp'), may hold values from 0 to 1, as said below
- attn_gain: bfloat16 [2048], P('dp'), may hold values from 0.5 to 1.5
- w_query: bfloat16 [2048, 2048], P('dp', 'tensor'), may hold values from -0.125 to 0.125
- key_weight: bfloat16 [2048, 1024], P('dp', 'tensor'), may hold values from -0.125 to 0.125
- value_weight: bfloat16 [2048, 1024], P('dp', 'tensor'), may hold values from -0.125 to 0.125
- query_norm_gain: bfloat16 [128], P('dp'), may hold values from 0.5 to 1.5
- key_gain: bfloat16 [128], P('dp'), may hold values from 0.5 to 1.5
- w_out: bfloat16 [2048, 2048], P('tensor', 'dp'), may hold values from -1 to 1
- ffn_gain: bfloat16 [2048], P('dp'), may hold values from 0.5 to 1.5
- w_gate: bfloat16 [2048, 6144], P('dp', 'tensor'), may hold values from -0.125 to 0.125
- w_up: bfloat16 [2048, 6144], P('dp', 'tensor'), may hold values from -0.125 to 0.125
- w_down: bfloat16 [6144, 2048], P('tensor', 'dp'), may hold values from -0.078125 to 0.078125
Outputs:
- layer_out: bfloat16 [2, 4096, 2048], P(None, ('dp', 'tensor'))
- input_grad: bfloat16 [2, 4096, 2048], P(None, ('dp', 'tensor'))
- grad_attn_gain: float32 [2048], P('dp')
- grad_query: float32 [2048, 2048], P('dp', 'tensor')
- grad_key: float32 [2048, 1024], P('dp', 'tensor')
- grad_value: float32 [2048, 1024], P('dp', 'tensor')
- grad_query_gain: float32 [128], P('dp')
- grad_key_gain: float32 [128], P('dp')
- grad_out: float32 [2048, 2048], P('tensor', 'dp')
- grad_ffn_gain: float32 [2048], P('dp')
- grad_gate: float32 [2048, 6144], P('dp', 'tensor')
- grad_up: float32 [2048, 6144], P('dp', 'tensor')
- grad_down: float32 [6144, 2048], P('tensor', 'dp')
Inputs may be any that keep to these rules, and one draw needn't show every extreme that they name: `segment_ids`: segment numbers start at 0 and never fall within a sequence; documents hold 60 to 400 tokens and are followed by one padding segment of 1 to 400 tokens. `positions`: positions count from 0 within each document and are 0 on padding. `pad_mask`: 0 exactly on the last segment of each sequence.
All inputs are finite; a program needn't handle non-finite values.
Results may differ from a plain program's by a relative error of at most 0.023.
Values may be sent and summed in bfloat16 or wider, within the bound.
A program may use at most 384 MiB of HBM per device.

v0:
```python
import math

import jax
import jax.numpy as jnp
from jax import lax
from jax.sharding import PartitionSpec as P

MODEL_WIDTH = 2048
HEAD_SIZE = 128


EPS = 1e-06
THETA = 1000000.0


def normalize(value_rows, gain):
    recip = lax.rsqrt(jnp.mean(value_rows * value_rows, axis=-1, keepdims=True) + EPS)
    unit = value_rows * recip
    return (unit * gain, unit, recip)


def norm_back(upstream, unit, recip, gain, axes):
    scaled = upstream * gain
    grad_in = recip * (scaled - unit * jnp.mean(scaled * unit, axis=-1, keepdims=True))
    return (grad_in, jnp.sum(upstream * unit, axis=axes))


def rotary(offsets):
    freqs = jnp.exp(
        jnp.arange(0, HEAD_SIZE, 2).astype(jnp.float32) * (-math.log(THETA) / HEAD_SIZE)
    )
    angles = offsets.astype(jnp.float32)[:, None] * freqs[None, :]
    return (jnp.cos(angles)[:, None, :], jnp.sin(angles)[:, None, :])


def rotary_apply(value_rows, cosine_table, sine_table):
    half = value_rows.shape[-1] // 2
    lower = value_rows[..., :half]
    higher = value_rows[..., half:]
    return jnp.concatenate(
        [lower * cosine_table - higher * sine_table, higher * cosine_table + lower * sine_table],
        axis=-1,
    )


def rotate_back(upstream, cosine_table, sine_table):
    half = upstream.shape[-1] // 2
    lower = upstream[..., :half]
    higher = upstream[..., half:]
    return jnp.concatenate(
        [lower * cosine_table + higher * sine_table, higher * cosine_table - lower * sine_table],
        axis=-1,
    )


def contract_rows(left, right):
    return lax.dot_general(
        left, right, (((0,), (0,)), ((), ())), preferred_element_type=jnp.float32
    )


def times_trans(left, right):
    return lax.dot_general(
        left, right, (((1,), (1,)), ((), ())), preferred_element_type=jnp.float32
    )


def block_mask(segment, valid_int, first_row, block):
    seq_len = segment.shape[0]
    columns = jnp.arange(seq_len)
    row_ids = first_row + jnp.arange(block)
    return (
        (segment[:, None] == segment[None, :])
        & (columns[None, :] <= row_ids[:, None])
        & ((valid_int[None, :] > 0) | (columns[None, :] == row_ids[:, None]))
    )


def block_scores(query_block, key_bf, scale):
    return scale * jnp.einsum(
        "qkgd,tkd->kgqt", query_block, key_bf, preferred_element_type=jnp.float32
    )


def on_device(
    hidden_in,
    cotangent,
    segment_ids,
    positions,
    pad_mask,
    attn_gain,
    w_query,
    key_weight,
    value_weight,
    query_norm_gain,
    key_gain,
    w_out,
    ffn_gain,
    w_gate,
    w_up,
    w_down,
):
    scale = 1.0 / math.sqrt(HEAD_SIZE)

    def micro_step(totals, items):
        rows_in, grad_out, segment, offsets, valid_int = items
        seq_len = segment.shape[0]
        own_rows = rows_in.shape[0]
        block = min(512, seq_len)
        attn_set = (
            lax.all_gather(attn_gain, "dp", axis=0, tiled=True),
            lax.all_gather(w_query, "dp", axis=0, tiled=True),
            lax.all_gather(key_weight, "dp", axis=0, tiled=True),
            lax.all_gather(value_weight, "dp", axis=0, tiled=True),
            lax.all_gather(query_norm_gain, "dp", axis=0, tiled=True),
            lax.all_gather(key_gain, "dp", axis=0, tiled=True),
            lax.all_gather(w_out, "dp", axis=1, tiled=True),
        )
        mlp_set = (
            lax.all_gather(ffn_gain, "dp", axis=0, tiled=True),
            lax.all_gather(w_gate, "dp", axis=0, tiled=True),
            lax.all_gather(w_up, "dp", axis=0, tiled=True),
            lax.all_gather(w_down, "dp", axis=1, tiled=True),
        )
        gain_attn, wq_full, wk_full, wv_full, gain_qbf, gain_kbf, wo_full = attn_set
        gain_ffnbf, wg_full, wu_full, wd_full = mlp_set
        gain_one = gain_attn.astype(jnp.float32)
        gain_two = gain_ffnbf.astype(jnp.float32)
        gain_query = gain_qbf.astype(jnp.float32)
        gain_key = gain_kbf.astype(jnp.float32)
        heads_q = wq_full.shape[1] // HEAD_SIZE
        heads_kv = wk_full.shape[1] // HEAD_SIZE
        head_groups = heads_q // heads_kv
        cosine_table, sine_table = rotary(offsets)
        valid_col = valid_int.astype(jnp.float32)[:, None]
        row_start = lax.axis_index("tensor") * own_rows
        x_all = lax.all_gather(rows_in, "tensor", axis=0, tiled=True).astype(jnp.float32)
        normed_all, unit_all, recip_all = normalize(x_all, gain_one)
        normalized_input = normed_all.astype(jnp.bfloat16)
        unit_one = lax.dynamic_slice_in_dim(unit_all, row_start, own_rows, 0)
        recip_one = lax.dynamic_slice_in_dim(recip_all, row_start, own_rows, 0)
        query_raw = jnp.dot(normalized_input, wq_full, preferred_element_type=jnp.float32).reshape(
            seq_len, heads_q, HEAD_SIZE
        )
        key_raw = jnp.dot(normalized_input, wk_full, preferred_element_type=jnp.float32).reshape(
            seq_len, heads_kv, HEAD_SIZE
        )
        value_bf = (
            jnp.dot(normalized_input, wv_full, preferred_element_type=jnp.float32)
            .astype(jnp.bfloat16)
            .reshape(seq_len, heads_kv, HEAD_SIZE)
        )
        query_normed, query_unit, query_recip = normalize(query_raw, gain_query)
        key_normed, key_unit, key_recip = normalize(key_raw, gain_key)
        query_bf = (
            rotary_apply(query_normed, cosine_table, sine_table)
            .astype(jnp.bfloat16)
            .reshape(seq_len, heads_kv, head_groups, HEAD_SIZE)
        )
        key_bf = rotary_apply(key_normed, cosine_table, sine_table).astype(jnp.bfloat16)
        first_row = 0
        query_block = query_bf
        allowed = block_mask(segment, valid_int, first_row, block)
        scores = block_scores(query_block, key_bf, scale)
        masked = jnp.where(allowed, scores, -1e30)
        totals_lse = jax.nn.logsumexp(masked, axis=-1, keepdims=True)
        probs_bf = jnp.where(allowed, jnp.exp(masked - totals_lse), 0.0).astype(jnp.bfloat16)
        mixed_blocks = [
            jnp.einsum("kgqt,tkd->qkgd", probs_bf, value_bf, preferred_element_type=jnp.float32)
        ]
        lse_blocks = [totals_lse]
        mixed = jnp.concatenate(mixed_blocks, axis=0).reshape(seq_len, heads_q * HEAD_SIZE)
        mixed_bf = (mixed * valid_col).astype(jnp.bfloat16)
        attn_all = lax.psum(
            jnp.dot(mixed_bf, wo_full, preferred_element_type=jnp.float32).astype(jnp.bfloat16),
            "tensor",
        ).astype(jnp.float32)
        resid_all = x_all + attn_all
        normed_two_all, unit_two_all, recip_two_all = normalize(resid_all, gain_two)
        normed_two = normed_two_all.astype(jnp.bfloat16)
        resid = lax.dynamic_slice_in_dim(resid_all, row_start, own_rows, 0)
        unit_two = lax.dynamic_slice_in_dim(unit_two_all, row_start, own_rows, 0)
        recip_two = lax.dynamic_slice_in_dim(recip_two_all, row_start, own_rows, 0)
        gate = jnp.dot(normed_two, wg_full, preferred_element_type=jnp.float32)
        upper = jnp.dot(normed_two, wu_full, preferred_element_type=jnp.float32)
        sigma = jax.nn.sigmoid(gate)
        swish = gate * sigma
        inner = (swish * upper).astype(jnp.bfloat16)
        mlp_own = lax.psum_scatter(
            jnp.dot(inner, wd_full, preferred_element_type=jnp.float32).astype(jnp.bfloat16),
            "tensor",
            scatter_dimension=0,
            tiled=True,
        ).astype(jnp.float32)
        layer_rows = (resid + mlp_own).astype(jnp.bfloat16)
        attn_set = (
            lax.all_gather(attn_gain, "dp", axis=0, tiled=True),
            lax.all_gather(w_query, "dp", axis=0, tiled=True),
            lax.all_gather(key_weight, "dp", axis=0, tiled=True),
            lax.all_gather(value_weight, "dp", axis=0, tiled=True),
            lax.all_gather(query_norm_gain, "dp", axis=0, tiled=True),
            lax.all_gather(key_gain, "dp", axis=0, tiled=True),
            lax.all_gather(w_out, "dp", axis=1, tiled=True),
        )
        mlp_set = (
            lax.all_gather(ffn_gain, "dp", axis=0, tiled=True),
            lax.all_gather(w_gate, "dp", axis=0, tiled=True),
            lax.all_gather(w_up, "dp", axis=0, tiled=True),
            lax.all_gather(w_down, "dp", axis=1, tiled=True),
        )
        gain_attn, wq_full, wk_full, wv_full, gain_qbf, gain_kbf, wo_full = attn_set
        gain_ffnbf, wg_full, wu_full, wd_full = mlp_set
        grad_rows = lax.all_gather(grad_out, "tensor", axis=0, tiled=True)
        d_inner = times_trans(grad_rows, wd_full)
        acc_down = contract_rows(inner, grad_rows)
        d_gate = (d_inner * upper * sigma * (1.0 + gate * (1.0 - sigma))).astype(jnp.bfloat16)
        d_upper = (d_inner * swish).astype(jnp.bfloat16)
        acc_gate = contract_rows(normed_two, d_gate)
        acc_up = contract_rows(normed_two, d_upper)
        d_normed_two = lax.psum_scatter(
            (times_trans(d_gate, wg_full) + times_trans(d_upper, wu_full)).astype(jnp.bfloat16),
            "tensor",
            scatter_dimension=0,
            tiled=True,
        ).astype(jnp.float32)
        d_resid_norm, acc_ffn_gain = norm_back(d_normed_two, unit_two, recip_two, gain_two, 0)
        d_resid = grad_out.astype(jnp.float32) + d_resid_norm
        d_resid_rows = lax.all_gather(d_resid.astype(jnp.bfloat16), "tensor", axis=0, tiled=True)
        d_mixed = times_trans(d_resid_rows, wo_full)
        acc_out = contract_rows(mixed_bf, d_resid_rows)
        d_mixed_bf = (d_mixed.astype(jnp.bfloat16) * valid_col.astype(jnp.bfloat16)).reshape(
            seq_len, heads_kv, head_groups, HEAD_SIZE
        )
        d_query_blocks = []
        d_key = jnp.zeros((seq_len, heads_kv, HEAD_SIZE), jnp.float32)
        d_value = jnp.zeros((seq_len, heads_kv, HEAD_SIZE), jnp.float32)
        for index, first_row in enumerate(range(0, seq_len, block)):
            query_block = query_bf
            allowed = block_mask(segment, valid_int, first_row, block)
            scores = block_scores(query_block, key_bf, scale)
            probs = jnp.where(allowed, jnp.exp(scores - lse_blocks[index]), 0.0)
            probs_bf = probs.astype(jnp.bfloat16)
            d_probs = jnp.einsum(
                "qkgd,tkd->kgqt", d_mixed_bf, value_bf, preferred_element_type=jnp.float32
            )
            delta = jnp.sum(probs * d_probs, axis=-1, keepdims=True)
            d_scores = (probs * (d_probs - delta)).astype(jnp.bfloat16)
            d_query_blocks.append(
                scale
                * jnp.einsum("kgqt,tkd->qkgd", d_scores, key_bf, preferred_element_type=jnp.float32)
            )
            d_key = d_key + scale * jnp.einsum(
                "kgqt,qkgd->tkd", d_scores, query_block, preferred_element_type=jnp.float32
            )
            d_value = d_value + jnp.einsum(
                "kgqt,qkgd->tkd", probs_bf, d_mixed_bf, preferred_element_type=jnp.float32
            )
        d_query = jnp.concatenate(d_query_blocks, axis=0).reshape(seq_len, heads_q, HEAD_SIZE)
        d_query_raw, acc_query_gain = norm_back(
            rotate_back(d_query, cosine_table, sine_table),
            query_unit,
            query_recip,
            gain_query,
            (0, 1),
        )
        d_key_raw, acc_key_gain = norm_back(
            rotate_back(d_key, cosine_table, sine_table), key_unit, key_recip, gain_key, (0, 1)
        )
        d_query_bf = d_query_raw.reshape(seq_len, heads_q * HEAD_SIZE).astype(jnp.bfloat16)
        d_key_bf = d_key_raw.reshape(seq_len, heads_kv * HEAD_SIZE).astype(jnp.bfloat16)
        d_value_bf = d_value.reshape(seq_len, heads_kv * HEAD_SIZE).astype(jnp.bfloat16)
        acc_query = contract_rows(normalized_input, d_query_bf)
        acc_key = contract_rows(normalized_input, d_key_bf)
        acc_value = contract_rows(normalized_input, d_value_bf)
        d_normed = lax.psum_scatter(
            (
                times_trans(d_query_bf, wq_full)
                + times_trans(d_key_bf, wk_full)
                + times_trans(d_value_bf, wv_full)
            ).astype(jnp.bfloat16),
            "tensor",
            scatter_dimension=0,
            tiled=True,
        ).astype(jnp.float32)
        d_input_norm, acc_attn_gain = norm_back(d_normed, unit_one, recip_one, gain_one, 0)
        input_rows = (d_resid + d_input_norm).astype(jnp.bfloat16)
        parts = (
            acc_attn_gain,
            acc_query,
            acc_key,
            acc_value,
            acc_query_gain,
            acc_key_gain,
            acc_out,
            acc_ffn_gain,
            acc_gate,
            acc_up,
            acc_down,
        )
        summed = tuple((total + part for total, part in zip(totals, parts)))
        return (summed, (layer_rows, input_rows))

    zeros = (
        jnp.zeros((MODEL_WIDTH,), jnp.float32),
        jnp.zeros((MODEL_WIDTH, w_query.shape[1]), jnp.float32),
        jnp.zeros((MODEL_WIDTH, key_weight.shape[1]), jnp.float32),
        jnp.zeros((MODEL_WIDTH, value_weight.shape[1]), jnp.float32),
        jnp.zeros((HEAD_SIZE,), jnp.float32),
        jnp.zeros((HEAD_SIZE,), jnp.float32),
        jnp.zeros((w_out.shape[0], MODEL_WIDTH), jnp.float32),
        jnp.zeros((MODEL_WIDTH,), jnp.float32),
        jnp.zeros((MODEL_WIDTH, w_gate.shape[1]), jnp.float32),
        jnp.zeros((MODEL_WIDTH, w_up.shape[1]), jnp.float32),
        jnp.zeros((w_down.shape[0], MODEL_WIDTH), jnp.float32),
    )
    totals, (layer_out, input_grad) = lax.scan(
        micro_step, zeros, (hidden_in, cotangent, segment_ids, positions, pad_mask)
    )
    gain_attn, gain_query, gain_key, gain_ffn = lax.psum(
        (totals[0], totals[4], totals[5], totals[7]), "tensor"
    )
    reduced = (
        lax.psum_scatter(
            gain_attn.astype(jnp.bfloat16), "dp", scatter_dimension=0, tiled=True
        ).astype(jnp.float32),
        lax.psum_scatter(
            totals[1].astype(jnp.bfloat16), "dp", scatter_dimension=0, tiled=True
        ).astype(jnp.float32),
        lax.psum_scatter(
            totals[2].astype(jnp.bfloat16), "dp", scatter_dimension=0, tiled=True
        ).astype(jnp.float32),
        lax.psum_scatter(
            totals[3].astype(jnp.bfloat16), "dp", scatter_dimension=0, tiled=True
        ).astype(jnp.float32),
        lax.psum_scatter(
            gain_query.astype(jnp.bfloat16), "dp", scatter_dimension=0, tiled=True
        ).astype(jnp.float32),
        lax.psum_scatter(
            gain_key.astype(jnp.bfloat16), "dp", scatter_dimension=0, tiled=True
        ).astype(jnp.float32),
        lax.psum_scatter(
            totals[6].astype(jnp.bfloat16), "dp", scatter_dimension=1, tiled=True
        ).astype(jnp.float32),
        lax.psum_scatter(
            gain_ffn.astype(jnp.bfloat16), "dp", scatter_dimension=0, tiled=True
        ).astype(jnp.float32),
        lax.psum_scatter(
            totals[8].astype(jnp.bfloat16), "dp", scatter_dimension=0, tiled=True
        ).astype(jnp.float32),
        lax.psum_scatter(
            totals[9].astype(jnp.bfloat16), "dp", scatter_dimension=0, tiled=True
        ).astype(jnp.float32),
        lax.psum_scatter(
            totals[10].astype(jnp.bfloat16), "dp", scatter_dimension=1, tiled=True
        ).astype(jnp.float32),
    )
    return (
        layer_out,
        input_grad,
        reduced[0],
        reduced[1],
        reduced[2],
        reduced[3],
        reduced[4],
        reduced[5],
        reduced[6],
        reduced[7],
        reduced[8],
        reduced[9],
        reduced[10],
    )


def solution(mesh):
    placed = (
        P(None, ("dp", "tensor"), None),
        P(None, ("dp", "tensor"), None),
        P(None, "dp"),
        P(None, "dp"),
        P(None, "dp"),
        P("dp"),
        P("dp", "tensor"),
        P("dp", "tensor"),
        P("dp", "tensor"),
        P("dp"),
        P("dp"),
        P("tensor", "dp"),
        P("dp"),
        P("dp", "tensor"),
        P("dp", "tensor"),
        P("tensor", "dp"),
    )
    return jax.shard_map(
        on_device,
        mesh=mesh,
        in_specs=placed,
        out_specs=(
            P(None, ("dp", "tensor"), None),
            P(None, ("dp", "tensor"), None),
            P("dp"),
            P("dp", "tensor"),
            P("dp", "tensor"),
            P("dp", "tensor"),
            P("dp"),
            P("dp"),
            P("tensor", "dp"),
            P("dp"),
            P("dp", "tensor"),
            P("dp", "tensor"),
            P("tensor", "dp"),
        ),
        check_vma=False,
    )
```

profile of v0, /device:TPU:8, one launch (start us, length us, event | category | flops | bytes accessed | tf_op | source)
XLA Modules:
  0.0 1641.6 jit_solution(12910806848978938666)
XLA Ops:
  8.1 1271.8 %while.35 = (s32[]{:T(128)}, f32[2048]{0:T(1024)}, f32[2048,512]{1,0:T(8,128)}, f32[2048,256]{1,0:T(8,128)}, f32[2048,256]{1,0:T(8,128)}, /*index=5*/f32[128]{0:...) while((s32[]{:T(128)}, f32[2048]{0:T(1024)}, ...), condition=%wide.region_22.23_spmd.clone, body=%wide.region_0.22_spmd.clone.sunk | while | flops 40405483520 | bytes 694621504 | solution.py:316
  50.1 21.9 %all-gather.33.cloned.1.call-done = bf16[2048,256]{1,0:T(8,128)(2,1)} async-done(((bf16[256,256]{1,0:T(8,128)(2,1)}), bf16[2048,256]{1,0:T(8,128)(2,1)}) %all-gather.33.cloned.1.call-update) | async-done | bytes 1048592 | tf_op jit(solution)/shard_map/while/body/eval_jaxpr/all_gather | solution.py:113
  98.3 27.3 %all-gather.31.cloned.1.call-done = bf16[2048,512]{1,0:T(8,128)(2,1)} async-done(((bf16[256,512]{1,0:T(8,128)(2,1)}), bf16[2048,512]{1,0:T(8,128)(2,1)}) %all-gather.31.cloned.1.call-update) | async-done | bytes 2097168 | tf_op jit(solution)/shard_map/while/body/eval_jaxpr/all_gather | solution.py:112
  175.1 55.1 %all-reduce.15.cloned.1.call-done = bf16[512,2048]{1,0:T(8,128)(2,1)} async-done(((bf16[512,2048]{1,0:T(8,128)(2,1)}), bf16[512,2048]{1,0:T(8,128)(2,1)}) %all-reduce.15.cloned.1.call-update) | async-done | bytes 2097168 | tf_op jit(solution)/shard_map/while/body/eval_jaxpr/psum | solution.py:174
  240.6 53.8 %all-gather.37.cloned.1.call-done = bf16[2048,1536]{1,0:T(8,128)(2,1)} async-done(((bf16[256,1536]{1,0:T(8,128)(2,1)}), bf16[2048,1536]{1,0:T(8,128)(2,1)}) %all-gather.37.cloned.1.call-update) | async-done | bytes 6291472 | tf_op jit(solution)/shard_map/while/body/eval_jaxpr/all_gather | solution.py:121
  302.9 29.8 %all-gather.41.cloned.1.call-done = bf16[1,512,2048]{2,1,0:T(8,128)(2,1)} async-done(((bf16[1,128,2048]{2,1,0:T(8,128)(2,1)}), bf16[1,512,2048]{2,1,0:T(8,128)(2,1)}) %all-gather.41.cloned.1.call-update) | async-done | bytes 2097168 | tf_op jit(solution)/shard_map/while/body/eval_jaxpr/all_gather | solution.py:213
  332.8 63.8 %all-gather.39.cloned.1.call-done = bf16[1536,2048]{1,0:T(8,128)(2,1)} async-done(((bf16[1536,256]{1,0:T(8,128)(2,1)}), bf16[1536,2048]{1,0:T(8,128)(2,1)}) %all-gather.39.cloned.1.call-update) | async-done | bytes 6291472 | tf_op jit(solution)/shard_map/while/body/eval_jaxpr/all_gather | solution.py:209
  405.2 56.7 %all-gather.43.cloned.1.call-done = bf16[2048,1536]{1,0:T(8,128)(2,1)} async-done(((bf16[256,1536]{1,0:T(8,128)(2,1)}), bf16[2048,1536]{1,0:T(8,128)(2,1)}) %all-gather.43.cloned.1.call-update) | async-done | bytes 6291472 | tf_op jit(solution)/shard_map/while/body/eval_jaxpr/all_gather | solution.py:122
  487.0 33.5 %reduce-scatter.25.cloned.1.call-done = bf16[128,2048]{1,0:T(8,128)(2,1)} async-done(((bf16[512,2048]{1,0:T(8,128)(2,1)}), bf16[128,2048]{1,0:T(8,128)(2,1)}) %reduce-scatter.25.cloned.1.call-update) | async-done | bytes 524304 | tf_op jit(solution)/shard_map/while/body/eval_jaxpr/reduce_scatter | solution.py:220
  614.4 23.2 %reduce-scatter.27.cloned.1.call-done = bf16[128,2048]{1,0:T(8,128)(2,1)} async-done(((bf16[512,2048]{1,0:T(8,128)(2,1)}), bf16[128,2048]{1,0:T(8,128)(2,1)}) %reduce-scatter.27.cloned.1.call-update) | async-done | bytes 524304 | tf_op jit(solution)/shard_map/while/body/eval_jaxpr/reduce_scatter | solution.py:275
  683.0 21.7 %all-gather.33.cloned.1.call-done = bf16[2048,256]{1,0:T(8,128)(2,1)} async-done(((bf16[256,256]{1,0:T(8,128)(2,1)}), bf16[2048,256]{1,0:T(8,128)(2,1)}) %all-gather.33.cloned.1.call-update) | async-done | bytes 1048592 | tf_op jit(solution)/shard_map/while/body/eval_jaxpr/all_gather | solution.py:113
  730.9 27.3 %all-gather.31.cloned.1.call-done = bf16[2048,512]{1,0:T(8,128)(2,1)} async-done(((bf16[256,512]{1,0:T(8,128)(2,1)}), bf16[2048,512]{1,0:T(8,128)(2,1)}) %all-gather.31.cloned.1.call-update) | async-done | bytes 2097168 | tf_op jit(solution)/shard_map/while/body/eval_jaxpr/all_gather | solution.py:112
  772.3 19.2 %all-gather.35.cloned.1.call-done = bf16[512,2048]{1,0:T(8,128)(2,1)} async-done(((bf16[512,256]{1,0:T(8,128)(2,1)}), bf16[512,2048]{1,0:T(8,128)(2,1)}) %all-gather.35.cloned.1.call-update) | async-done | bytes 2097168 | tf_op jit(solution)/shard_map/while/body/eval_jaxpr/all_gather | solution.py:117
  807.4 55.4 %all-reduce.15.cloned.1.call-done = bf16[512,2048]{1,0:T(8,128)(2,1)} async-done(((bf16[512,2048]{1,0:T(8,128)(2,1)}), bf16[512,2048]{1,0:T(8,128)(2,1)}) %all-reduce.15.cloned.1.call-update) | async-done | bytes 2097168 | tf_op jit(solution)/shard_map/while/body/eval_jaxpr/psum | solution.py:174
  873.3 53.8 %all-gather.37.cloned.1.call-done = bf16[2048,1536]{1,0:T(8,128)(2,1)} async-done(((bf16[256,1536]{1,0:T(8,128)(2,1)}), bf16[2048,1536]{1,0:T(8,128)(2,1)}) %all-gather.37.cloned.1.call-update) | async-done | bytes 6291472 | tf_op jit(solution)/shard_map/while/body/eval_jaxpr/all_gather | solution.py:121
  935.6 29.8 %all-gather.41.cloned.1.call-done = bf16[1,512,2048]{2,1,0:T(8,128)(2,1)} async-done(((bf16[1,128,2048]{2,1,0:T(8,128)(2,1)}), bf16[1,512,2048]{2,1,0:T(8,128)(2,1)}) %all-gather.41.cloned.1.call-update) | async-done | bytes 2097168 | tf_op jit(solution)/shard_map/while/body/eval_jaxpr/all_gather | solution.py:213
  965.5 63.8 %all-gather.39.cloned.1.call-done = bf16[1536,2048]{1,0:T(8,128)(2,1)} async-done(((bf16[1536,256]{1,0:T(8,128)(2,1)}), bf16[1536,2048]{1,0:T(8,128)(2,1)}) %all-gather.39.cloned.1.call-update) | async-done | bytes 6291472 | tf_op jit(solution)/shard_map/while/body/eval_jaxpr/all_gather | solution.py:209
  1037.9 56.7 %all-gather.43.cloned.1.call-done = bf16[2048,1536]{1,0:T(8,128)(2,1)} async-done(((bf16[256,1536]{1,0:T(8,128)(2,1)}), bf16[2048,1536]{1,0:T(8,128)(2,1)}) %all-gather.43.cloned.1.call-update) | async-done | bytes 6291472 | tf_op jit(solution)/shard_map/while/body/eval_jaxpr/all_gather | solution.py:122
  1120.1 33.5 %reduce-scatter.25.cloned.1.call-done = bf16[128,2048]{1,0:T(8,128)(2,1)} async-done(((bf16[512,2048]{1,0:T(8,128)(2,1)}), bf16[128,2048]{1,0:T(8,128)(2,1)}) %reduce-scatter.25.cloned.1.call-update) | async-done | bytes 524304 | tf_op jit(solution)/shard_map/while/body/eval_jaxpr/reduce_scatter | solution.py:220
  1350.0 32.8 %reduce-scatter.11.cloned.1.call-done = bf16[256,512]{1,0:T(8,128)(2,1)} async-done(((bf16[2048,512]{1,0:T(8,128)(2,1)}), bf16[256,512]{1,0:T(8,128)(2,1)}) %reduce-scatter.11.cloned.1.call-update) | async-done | bytes 262160 | tf_op jit(solution)/shard_map/reduce_scatter | solution.py:326
  1384.6 34.7 %reduce-scatter.17.cloned.1.call-done = bf16[512,256]{1,0:T(8,128)(2,1)} async-done(((bf16[512,2048]{1,0:T(8,128)(2,1)}), bf16[512,256]{1,0:T(8,128)(2,1)}) %reduce-scatter.17.cloned.1.call-update) | async-done | bytes 262160 | tf_op jit(solution)/shard_map/reduce_scatter | solution.py:341
  1421.1 69.7 %reduce-scatter.19.cloned.1.call-done = bf16[256,1536]{1,0:T(8,128)(2,1)} async-done(((bf16[2048,1536]{1,0:T(8,128)(2,1)}), bf16[256,1536]{1,0:T(8,128)(2,1)}) %reduce-scatter.19.cloned.1.call-update) | async-done | bytes 786448 | tf_op jit(solution)/shard_map/reduce_scatter | solution.py:347
  1493.3 68.0 %reduce-scatter.21.cloned.1.call-done = bf16[256,1536]{1,0:T(8,128)(2,1)} async-done(((bf16[2048,1536]{1,0:T(8,128)(2,1)}), bf16[256,1536]{1,0:T(8,128)(2,1)}) %reduce-scatter.21.cloned.1.call-update) | async-done | bytes 786448 | tf_op jit(solution)/shard_map/reduce_scatter | solution.py:350
  1563.7 67.9 %reduce-scatter.23.cloned.1.call-done = bf16[1536,256]{1,0:T(8,128)(2,1)} async-done(((bf16[1536,2048]{1,0:T(8,128)(2,1)}), bf16[1536,256]{1,0:T(8,128)(2,1)}) %reduce-scatter.23.cloned.1.call-update) | async-done | bytes 786448 | tf_op jit(solution)/shard_map/reduce_scatter | solution.py:353
  (602 shorter events, 616.2 us)
Async XLA Ops:
  11.2 84.3 %all-gather.27.cloned.1.call-start = ((), (), s32[]{:S(2)}) async-start(), calls=%async_computation.17 | async-start | bytes 1179648 | tf_op jit(solution)/shard_map/while/body/eval_jaxpr/all_gather | solution.py:114
  11.9 113.7 %all-gather.31.cloned.1.call-start = ((), (), s32[]{:S(2)}) async-start(), calls=%async_computation.19 | async-start | bytes 2359296 | tf_op jit(solution)/shard_map/while/body/eval_jaxpr/all_gather | solution.py:112
  12.5 146.4 %all-gather.35.cloned.1.call-start = ((), (), s32[]{:S(2)}) async-start(), calls=%async_computation.21 | async-start | bytes 2359296 | tf_op jit(solution)/shard_map/while/body/eval_jaxpr/all_gather | solution.py:117
  13.1 217.1 %all-reduce.15.cloned.1.call-start = ((), (), s32[]{:S(2)}) async-start(), calls=%async_computation.22 | async-start | bytes 4194304 | tf_op jit(solution)/shard_map/while/body/eval_jaxpr/psum | solution.py:174
  163.3 131.2 %all-gather.37.cloned.1.call-start = ((), (), s32[]{:S(2)}) async-start(), calls=%async_computation.23 | async-start | bytes 7077888 | tf_op jit(solution)/shard_map/while/body/eval_jaxpr/all_gather | solution.py:121
  164.0 168.8 %all-gather.41.cloned.1.call-start = ((), (), s32[]{:S(2)}) async-start(), calls=%async_computation.25 | async-start | bytes 2621440 | tf_op jit(solution)/shard_map/while/body/eval_jaxpr/all_gather | solution.py:213
  166.0 230.6 %all-gather.39.cloned.1.call-start = ((), (), s32[]{:S(2)}) async-start(), calls=%async_computation.24 | async-start | bytes 7077888 | tf_op jit(solution)/shard_map/while/body/eval_jaxpr/all_gather | solution.py:209
  166.7 295.2 %all-gather.43.cloned.1.call-start = ((), (), s32[]{:S(2)}) async-start(), calls=%async_computation.26 | async-start | bytes 7077888 | tf_op jit(solution)/shard_map/while/body/eval_jaxpr/all_gather | solution.py:122
  167.3 353.3 %reduce-scatter.25.cloned.1.call-start = ((), (), s32[]{:S(2)}) async-start(), calls=%async_computation.27 | async-start | bytes 2621440 | tf_op jit(solution)/shard_map/while/body/eval_jaxpr/reduce_scatter | solution.py:220
  554.4 83.2 %reduce-scatter.27.cloned.1.call-start = ((), (), s32[]{:S(2)}) async-start(), calls=%async_computation.29 | async-start | bytes 2621440 | tf_op jit(solution)/shard_map/while/body/eval_jaxpr/reduce_scatter | solution.py:275
  645.3 82.7 %all-gather.27.cloned.1.call-start = ((), (), s32[]{:S(2)}) async-start(), calls=%async_computation.17 | async-start | bytes 1179648 | tf_op jit(solution)/shard_map/while/body/eval_jaxpr/all_gather | solution.py:114
  645.9 112.3 %all-gather.31.cloned.1.call-start = ((), (), s32[]{:S(2)}) async-start(), calls=%async_computation.19 | async-start | bytes 2359296 | tf_op jit(solution)/shard_map/while/body/eval_jaxpr/all_gather | solution.py:112
  646.5 145.1 %all-gather.35.cloned.1.call-start = ((), (), s32[]{:S(2)}) async-start(), calls=%async_computation.21 | async-start | bytes 2359296 | tf_op jit(solution)/shard_map/while/body/eval_jaxpr/all_gather | solution.py:117
  647.2 215.6 %all-reduce.15.cloned.1.call-start = ((), (), s32[]{:S(2)}) async-start(), calls=%async_computation.22 | async-start | bytes 4194304 | tf_op jit(solution)/shard_map/while/body/eval_jaxpr/psum | solution.py:174
  795.9 131.2 %all-gather.37.cloned.1.call-start = ((), (), s32[]{:S(2)}) async-start(), calls=%async_computation.23 | async-start | bytes 7077888 | tf_op jit(solution)/shard_map/while/body/eval_jaxpr/all_gather | solution.py:121
  796.7 168.8 %all-gather.41.cloned.1.call-start = ((), (), s32[]{:S(2)}) async-start(), calls=%async_computation.25 | async-start | bytes 2621440 | tf_op jit(solution)/shard_map/while/body/eval_jaxpr/all_gather | solution.py:213
  798.6 230.7 %all-gather.39.cloned.1.call-start = ((), (), s32[]{:S(2)}) async-start(), calls=%async_computation.24 | async-start | bytes 7077888 | tf_op jit(solution)/shard_map/while/body/eval_jaxpr/all_gather | solution.py:209
  799.4 295.2 %all-gather.43.cloned.1.call-start = ((), (), s32[]{:S(2)}) async-start(), calls=%async_computation.26 | async-start | bytes 7077888 | tf_op jit(solution)/shard_map/while/body/eval_jaxpr/all_gather | solution.py:122
  800.0 353.6 %reduce-scatter.25.cloned.1.call-start = ((), (), s32[]{:S(2)}) async-start(), calls=%async_computation.27 | async-start | bytes 2621440 | tf_op jit(solution)/shard_map/while/body/eval_jaxpr/reduce_scatter | solution.py:220
  1284.0 98.8 %reduce-scatter.11.cloned.1.call-start = ((), (), s32[]{:S(2)}) async-start(), calls=%async_computation.10 | async-start | bytes 2359296 | tf_op jit(solution)/shard_map/reduce_scatter | solution.py:326
  1287.9 131.4 %reduce-scatter.17.cloned.1.call-start = ((), (), s32[]{:S(2)}) async-start(), calls=%async_computation.13 | async-start | bytes 2359296 | tf_op jit(solution)/shard_map/reduce_scatter | solution.py:341
  1291.9 198.9 %reduce-scatter.19.cloned.1.call-start = ((), (), s32[]{:S(2)}) async-start(), calls=%async_computation.14 | async-start | bytes 7077888 | tf_op jit(solution)/shard_map/reduce_scatter | solution.py:347
  1299.9 261.3 %reduce-scatter.21.cloned.1.call-start = ((), (), s32[]{:S(2)}) async-start(), calls=%async_computation.15 | async-start | bytes 7077888 | tf_op jit(solution)/shard_map/reduce_scatter | solution.py:350
  1308.0 323.6 %reduce-scatter.23.cloned.1.call-start = ((), (), s32[]{:S(2)}) async-start(), calls=%async_computation.16 | async-start | bytes 7077888 | tf_op jit(solution)/shard_map/reduce_scatter | solution.py:353
  (157 other events, 2123.9 us)
Sparse Core Ops, SparseCore 0:
  11.7 36.3 all-gather.28
  96.9 28.6 all-gather.30
  127.0 31.7 all-gather.34
  163.4 66.7 all-reduce.14
  231.8 62.6 all-gather.36
  296.9 35.8 all-gather.40
  334.4 62.1 all-gather.38
  398.1 63.7 all-gather.42
  484.7 35.8 reduce-scatter.24
  526.2 35.1 all-gather.44
  564.4 35.1 reduce-scatter.28
  602.4 35.1 reduce-scatter.26
  645.7 35.1 all-gather.28
  729.5 28.6 all-gather.30
  759.7 31.7 all-gather.34
  796.1 66.7 all-reduce.14
  864.5 62.6 all-gather.36
  929.6 35.8 all-gather.40
  967.1 62.1 all-gather.38
  1030.8 63.7 all-gather.42
  1117.7 35.8 reduce-scatter.24
  1159.2 35.1 all-gather.44
  1197.2 35.1 reduce-scatter.28
  1235.4 35.1 reduce-scatter.26
  (4 shorter events, 88.1 us)
Sparse Core Ops, SparseCore 1:
  1283.3 28.8 reduce-scatter.12
  1314.8 31.3 reduce-scatter.14
  1348.3 34.4 reduce-scatter.10
  1385.1 34.2 reduce-scatter.16
  1421.6 69.1 reduce-scatter.18
  1493.1 68.1 reduce-scatter.20
  1563.5 68.1 reduce-scatter.22
where the time goes:
time: 1650 us; the launch traced here: 1640 us
  waiting for transfers between devices  1090 us (66%)
  matrix products  252 us (15%)
  other arithmetic  132 us (8%)
  blocking collectives  87.3 us (5%)
  local copies, waits for them, and re-layouts  53.8 us (3%)
  between operations  17.2 us (1%)
    all_gather x2, waiting for transfers between devices, micro_step(): lax.all_gather(w_down, 'dp', axis=1, tiled=True)  128 us
    all_gather x2, waiting for transfers between devices, micro_step(): lax.all_gather(w_up, 'dp', axis=0, tiled=True)  113 us
    psum x2, waiting for transfers between devices, micro_step(): lax.psum(jnp.dot(mixed_bf, wo_full, preferred_element_type=jnp.float32).a...  110 us
    all_gather x2, waiting for transfers between devices, micro_step(): lax.all_gather(w_gate, 'dp', axis=0, tiled=True)  108 us
    dot_general x14, matrix products, contract_rows(): lax.dot_general(left, right, (((0,), (0,)), ((), ())), preferred_element_...  92.8 us
    reduce_scatter x1, waiting for transfers between devices, on_device(): lax.psum_scatter(totals[8].astype(jnp.bfloat16), 'dp', scatter_dimension=...  69.7 us
    reduce_scatter x1, waiting for transfers between devices, on_device(): lax.psum_scatter(totals[9].astype(jnp.bfloat16), 'dp', scatter_dimension=...  68 us
    reduce_scatter x1, waiting for transfers between devices, on_device(): lax.psum_scatter(totals[10].astype(jnp.bfloat16), 'dp', scatter_dimension...  67.9 us
  transfers between devices with their start and end apart: 35, of which 32 were waited for; matrix products, arithmetic and copies ran while one was open for 21% of the time, Pallas kernels for 0%

commit v1 on v0

v1 whole, which is shorter than its diff:
```python
import math

import jax
import jax.numpy as jnp
from jax import lax
from jax.experimental import pallas as pl
from jax.experimental.pallas import tpu as pltpu
from jax.sharding import PartitionSpec as P

HEAD_SIZE = 128
EPS = 1e-06
THETA = 1000000.0
CHUNKS = 3
F32 = jnp.float32
BF16 = jnp.bfloat16

ORDER = (0, 2, 4, 6, 1, 3, 5, 7)
PAIR = [(d, d ^ 2) for d in range(8)]
CORE = [(d, d ^ 1) for d in range(8)]
INNER = [(2, 4), (3, 5), (4, 2), (5, 3)]
OUTWARD = [(2, 0), (3, 1), (4, 6), (5, 7)]
INWARD = [(0, 2), (1, 3), (6, 4), (7, 5)]
XNEXT = [(t, t ^ 1) for t in range(4)]
YNEXT = [(t, t ^ 2) for t in range(4)]


def add_rounded(left, right):
    return (left.astype(F32) + right.astype(F32)).astype(BF16)


def dot_nn(left, right):
    return jnp.dot(left, right, preferred_element_type=F32)


def dot_nt(left, right):
    return lax.dot_general(left, right, (((1,), (1,)), ((), ())), preferred_element_type=F32)


def dot_tn(left, right):
    return lax.dot_general(left, right, (((0,), (0,)), ((), ())), preferred_element_type=F32)


def block_move(table, rows):
    micro, count, width = rows.shape
    blocks = table.shape[0]
    size = width // blocks

    def body(table_ref, in_ref, out_ref):
        out_ref[...] = in_ref[...]

    return pl.pallas_call(
        body,
        out_shape=jax.ShapeDtypeStruct(rows.shape, rows.dtype),
        grid_spec=pltpu.PrefetchScalarGridSpec(
            num_scalar_prefetch=1,
            grid=(blocks,),
            in_specs=[pl.BlockSpec((micro, count, size), lambda i, ref: (0, 0, ref[i]))],
            out_specs=pl.BlockSpec((micro, count, size), lambda i, ref: (0, 0, i)),
        ),
        cost_estimate=pl.CostEstimate(
            flops=0, bytes_accessed=4 * micro * count * width, transcendentals=0
        ),
    )(table, rows)


class Direct:
    def __init__(self, dp, tensor):
        self.dp, self.tensor = dp, tensor
        self.me = lax.axis_index("dp")
        self.own = lax.axis_index("tensor")

    def to_local(self, rows):
        return rows

    def from_local(self, rows):
        return rows

    def row_order(self, value):
        return value

    def gather_gains(self, packed):
        return lax.all_gather(packed, "dp", axis=0)

    def gains_local(self, blocks):
        return blocks.reshape(-1)

    def gains_plain(self, blocks):
        return blocks.reshape(-1)

    def plain_vector(self, vector):
        return vector

    def gather_weights(self, buf):
        return lax.all_gather(buf, "dp", axis=0, tiled=True)

    def scatter_grads(self, parts):
        full = jnp.concatenate([dot_tn(l, r).astype(BF16) for l, r in parts], axis=1)
        return lax.psum_scatter(full, "dp", scatter_dimension=0, tiled=True).astype(F32)

    def gather_rows(self, rows):
        return lax.all_gather(rows, "tensor", axis=1, tiled=True)

    def scatter_rows(self, partial):
        return lax.psum_scatter(partial, "tensor", scatter_dimension=1, tiled=True).astype(F32)


class Links(Direct):
    def __init__(self, dp, tensor):
        super().__init__(dp, tensor)
        z = self.me // 2
        self.inner = (z == 1) | (z == 2)
        self.blocks = self.me ^ jnp.array(ORDER, jnp.int32)
        place = jnp.array([ORDER.index(b) for b in range(8)], jnp.int32)
        hit = (self.me ^ jnp.arange(8, dtype=jnp.int32))[:, None] == jnp.array(ORDER, jnp.int32)
        self.hit = hit
        self.places = jnp.sum(jnp.where(hit, jnp.arange(8, dtype=jnp.int32)[None, :], 0), axis=1)

    def to_local(self, rows):
        return block_move(self.blocks, rows)

    def from_local(self, rows):
        return block_move(self.places, rows)

    def row_order(self, value):
        parts = list(jnp.split(value, 4, axis=-1))
        for bit in (1, 2):
            swap = (self.own & bit) != 0
            parts = [jnp.where(swap, parts[j ^ bit], parts[j]) for j in range(4)]
        return jnp.concatenate(parts, axis=-1)

    def gather_gains(self, packed):
        got = [packed]
        for b in ORDER[1:]:
            got.append(lax.ppermute(packed, "dp", [(d, d ^ b) for d in range(8)]))
        return jnp.stack(got)

    def gains_plain(self, blocks):
        return jnp.sum(jnp.where(self.hit[:, :, None], blocks[None], 0), axis=1).reshape(-1)

    def plain_vector(self, vector):
        return self.gains_plain(vector.reshape(8, -1))

    def gather_weights(self, buf):
        pair = lax.ppermute(buf, "dp", PAIR)
        over_own = lax.ppermute(buf, "dp", INNER)
        over_pair = lax.ppermute(pair, "dp", INNER)
        out_own = lax.ppermute(over_own, "dp", OUTWARD)
        out_pair = lax.ppermute(over_pair, "dp", OUTWARD)
        far_two = jnp.where(self.inner, over_pair, out_own)
        far_three = jnp.where(self.inner, over_own, out_pair)
        mine = jnp.concatenate([buf, pair, far_two, far_three], axis=0)
        other = lax.ppermute(mine, "dp", CORE)
        return jnp.concatenate([mine, other], axis=0)

    def scatter_grads(self, parts):
        summed = []
        for left, right in parts:
            half = left.shape[1] // 2
            away = dot_tn(left[:, half:], right).astype(BF16)
            here = dot_tn(left[:, :half], right)
            summed.append((here + lax.ppermute(away, "dp", CORE).astype(F32)).astype(BF16))
        own, pair, two, three = jnp.split(jnp.concatenate(summed, axis=1), 4, axis=0)
        two = add_rounded(two, lax.ppermute(three, "dp", INWARD)), two
        three = add_rounded(three, lax.ppermute(two[1], "dp", INWARD))
        pair = add_rounded(pair, lax.ppermute(two[0], "dp", INNER))
        own = own.astype(F32) + lax.ppermute(three, "dp", INNER).astype(F32)
        return own + lax.ppermute(pair, "dp", PAIR).astype(F32)

    def gather_rows(self, rows):
        first, second = rows[0], rows[1]
        x_first = lax.ppermute(first, "tensor", XNEXT)
        y_second = lax.ppermute(second, "tensor", YNEXT)
        x_second = lax.ppermute(second, "tensor", XNEXT)
        y_first = lax.ppermute(first, "tensor", YNEXT)
        d_first = lax.ppermute(x_first, "tensor", YNEXT)
        d_second = lax.ppermute(y_second, "tensor", XNEXT)
        return jnp.stack(
            [
                jnp.concatenate([first, x_first, y_first, d_first], axis=0),
                jnp.concatenate([second, x_second, y_second, d_second], axis=0),
            ]
        )

    def scatter_rows(self, partial):
        out = []
        for part, near, far, a, b in (
            (partial[0], XNEXT, YNEXT, 1, 2),
            (partial[1], YNEXT, XNEXT, 2, 1),
        ):
            block = jnp.split(part, 4, axis=0)
            got_diag = lax.ppermute(block[3], "tensor", near)
            got_own = lax.ppermute(block[a], "tensor", near)
            passed = lax.ppermute(add_rounded(block[b], got_diag), "tensor", far)
            out.append(block[0].astype(F32) + got_own.astype(F32) + passed.astype(F32))
        return jnp.stack(out)


def unit_of(rows):
    recip = lax.rsqrt(jnp.mean(rows * rows, axis=-1, keepdims=True) + EPS)
    return rows * recip, recip


def norm_back(upstream, unit, recip, gain):
    scaled = upstream * gain
    return recip * (scaled - unit * jnp.mean(scaled * unit, axis=-1, keepdims=True))


def rotary(offsets):
    freqs = jnp.exp(
        jnp.arange(0, HEAD_SIZE, 2).astype(F32) * (-math.log(THETA) / HEAD_SIZE)
    )
    angles = offsets.astype(F32)[..., None] * freqs
    return jnp.cos(angles)[..., None, :], jnp.sin(angles)[..., None, :]


def rotate(rows, cosine, sine):
    half = rows.shape[-1] // 2
    low, high = rows[..., :half], rows[..., half:]
    return jnp.concatenate([low * cosine - high * sine, high * cosine + low * sine], axis=-1)


def on_device(
    net,
    hidden_in,
    cotangent,
    segment_ids,
    positions,
    pad_mask,
    attn_gain,
    w_query,
    key_weight,
    value_weight,
    query_norm_gain,
    key_gain,
    w_out,
    ffn_gain,
    w_gate,
    w_up,
    w_down,
):
    net = net()
    scale = 1.0 / math.sqrt(HEAD_SIZE)
    micro, own_rows, width = hidden_in.shape
    seq_len = segment_ids.shape[1]
    rows = micro * seq_len
    share = attn_gain.shape[0]
    head_share = query_norm_gain.shape[0]
    q_cols, kv_cols = w_query.shape[1], key_weight.shape[1]
    heads_q, heads_kv = q_cols // HEAD_SIZE, kv_cols // HEAD_SIZE
    groups = heads_q // heads_kv
    qkv_cols = q_cols + 2 * kv_cols
    units = w_gate.shape[1] // CHUNKS

    attn_buf = jnp.concatenate([w_query, key_weight, value_weight, w_out.T], axis=1)
    w_attn = net.gather_weights(attn_buf)
    w_qkv, w_out_t = w_attn[:, :qkv_cols], w_attn[:, qkv_cols:]
    x_own = net.to_local(hidden_in)
    x_all = net.gather_rows(x_own).reshape(rows, width).astype(F32)
    packed = jnp.concatenate(
        [attn_gain, ffn_gain, query_norm_gain, key_gain], axis=0
    )
    gains = net.gather_gains(packed).astype(F32)
    gain_one = net.gains_local(gains[:, :share])
    gain_two = net.gains_local(gains[:, share : 2 * share])
    gain_q = net.gains_plain(gains[:, 2 * share : 2 * share + head_share])
    gain_k = net.gains_plain(gains[:, 2 * share + head_share :])
    ffn_sets = []
    for chunk in range(CHUNKS):
        cut = slice(chunk * units, (chunk + 1) * units)
        ffn_sets.append(
            net.gather_weights(
                jnp.concatenate([w_gate[:, cut], w_up[:, cut], w_down[cut, :].T], axis=1)
            )
        )
    g_own = net.to_local(cotangent)
    g_all = net.gather_rows(g_own).reshape(rows, width)

    segment = net.row_order(segment_ids)
    offsets = net.row_order(positions)
    valid = net.row_order(pad_mask)
    row_ids = net.row_order(jnp.arange(seq_len, dtype=jnp.int32))
    cosine, sine = rotary(offsets)
    valid_col = valid.reshape(rows, 1).astype(F32)
    unit_all, _ = unit_of(x_all)
    a1 = (unit_all * gain_one).astype(BF16)
    qkv = dot_nn(a1, w_qkv)
    q_raw = qkv[:, :q_cols].reshape(micro, seq_len, heads_q, HEAD_SIZE)
    k_raw = qkv[:, q_cols : q_cols + kv_cols].reshape(micro, seq_len, heads_kv, HEAD_SIZE)
    value = (
        qkv[:, q_cols + kv_cols :].astype(BF16).reshape(micro, seq_len, heads_kv, HEAD_SIZE)
    )
    q_unit, q_recip = unit_of(q_raw)
    k_unit, k_recip = unit_of(k_raw)
    query = (
        rotate(q_unit * gain_q, cosine, sine)
        .astype(BF16)
        .reshape(micro, seq_len, heads_kv, groups, HEAD_SIZE)
    )
    key = rotate(k_unit * gain_k, cosine, sine).astype(BF16)
    allowed = (
        (segment[:, :, None] == segment[:, None, :])
        & (row_ids[None, None, :] <= row_ids[None, :, None])
        & ((valid[:, None, :] > 0) | (row_ids[None, None, :] == row_ids[None, :, None]))
    )[:, None, None]
    scores = scale * jnp.einsum("mqkgd,mtkd->mkgqt", query, key, preferred_element_type=F32)
    masked = jnp.where(allowed, scores, -1e30)
    lse = jax.nn.logsumexp(masked, axis=-1, keepdims=True)
    probs = jnp.where(allowed, jnp.exp(masked - lse), 0.0)
    probs_bf = probs.astype(BF16)
    mixed = jnp.einsum("mkgqt,mtkd->mqkgd", probs_bf, value, preferred_element_type=F32)
    mixed_bf = (mixed.reshape(rows, q_cols) * valid_col).astype(BF16)
    attn_part = dot_nt(mixed_bf, w_out_t).astype(BF16).reshape(micro, seq_len, width)
    resid = x_own.astype(F32) + net.scatter_rows(attn_part)
    unit_two, recip_two = unit_of(resid)
    a2_own = (unit_two * gain_two).astype(BF16)
    a2 = net.gather_rows(a2_own).reshape(rows, width)

    mlp = da2 = None
    grads_ffn = []
    for chunk in range(CHUNKS):
        w_chunk = ffn_sets[chunk]
        w_gu, w_down_t = w_chunk[:, : 2 * units], w_chunk[:, 2 * units :]
        gate_up = dot_nn(a2, w_gu)
        gate, upper = gate_up[:, :units], gate_up[:, units:]
        d_inner = dot_nn(g_all, w_down_t)
        sigma = jax.nn.sigmoid(gate)
        swish = gate * sigma
        inner = (swish * upper).astype(BF16)
        d_gate = (d_inner * upper * sigma * (1.0 + gate * (1.0 - sigma))).astype(BF16)
        d_upper = (d_inner * swish).astype(BF16)
        d_gu = jnp.concatenate([d_gate, d_upper], axis=1)
        part_mlp = dot_nt(inner, w_down_t)
        part_da2 = dot_nt(d_gu, w_gu)
        mlp = part_mlp if mlp is None else mlp + part_mlp
        da2 = part_da2 if da2 is None else da2 + part_da2
        grads_ffn.append(net.scatter_grads([(a2, d_gu), (g_all, inner)]))
    d_normed_two = net.scatter_rows(da2.astype(BF16).reshape(micro, seq_len, width))
    d_resid = g_own.astype(F32) + norm_back(d_normed_two, unit_two, recip_two, gain_two)
    acc_ffn_gain = jnp.sum(d_normed_two * unit_two, axis=(0, 1))
    d_resid_all = net.gather_rows(d_resid.astype(BF16)).reshape(rows, width)
    mlp_own = net.scatter_rows(mlp.astype(BF16).reshape(micro, seq_len, width))
    layer_out = net.from_local((resid + mlp_own).astype(BF16))

    d_mixed = dot_nn(d_resid_all, w_out_t).astype(BF16) * valid_col.astype(BF16)
    d_mixed = d_mixed.reshape(micro, seq_len, heads_kv, groups, HEAD_SIZE)
    d_probs = jnp.einsum("mqkgd,mtkd->mkgqt", d_mixed, value, preferred_element_type=F32)
    delta = jnp.sum(probs * d_probs, axis=-1, keepdims=True)
    d_scores = (probs * (d_probs - delta)).astype(BF16)
    d_query = scale * jnp.einsum("mkgqt,mtkd->mqkgd", d_scores, key, preferred_element_type=F32)
    d_key = scale * jnp.einsum("mkgqt,mqkgd->mtkd", d_scores, query, preferred_element_type=F32)
    d_value = jnp.einsum("mkgqt,mqkgd->mtkd", probs_bf, d_mixed, preferred_element_type=F32)
    d_query = rotate(
        d_query.reshape(micro, seq_len, heads_q, HEAD_SIZE), cosine, -sine
    )
    d_key = rotate(d_key, cosine, -sine)
    acc_q_gain = jnp.sum(d_query * q_unit, axis=(0, 1, 2))
    acc_k_gain = jnp.sum(d_key * k_unit, axis=(0, 1, 2))
    d_qkv = jnp.concatenate(
        [
            norm_back(d_query, q_unit, q_recip, gain_q).astype(BF16).reshape(rows, q_cols),
            norm_back(d_key, k_unit, k_recip, gain_k).astype(BF16).reshape(rows, kv_cols),
            d_value.astype(BF16).reshape(rows, kv_cols),
        ],
        axis=1,
    )
    da1 = dot_nt(d_qkv, w_qkv)
    acc_attn_gain = jnp.sum(da1 * unit_all, axis=0)
    d_normed = net.scatter_rows(da1.astype(BF16).reshape(micro, seq_len, width))
    grads_attn = net.scatter_grads([(a1, d_qkv), (d_resid_all, mixed_bf)])
    unit_one, recip_one = unit_of(x_own.astype(F32))
    input_grad = net.from_local(
        (d_resid + norm_back(d_normed, unit_one, recip_one, gain_one)).astype(BF16)
    )

    sums = lax.psum(
        jnp.concatenate(
            [
                net.plain_vector(acc_attn_gain),
                net.plain_vector(acc_ffn_gain),
                acc_q_gain,
                acc_k_gain,
            ]
        ),
        ("dp", "tensor"),
    )

    def own_part(start, size):
        return lax.dynamic_slice_in_dim(sums, start + net.me * size, size, 0)

    return (
        layer_out,
        input_grad,
        own_part(0, share),
        grads_attn[:, :q_cols],
        grads_attn[:, q_cols : q_cols + kv_cols],
        grads_attn[:, q_cols + kv_cols : qkv_cols],
        own_part(2 * width, head_share),
        own_part(2 * width + HEAD_SIZE, head_share),
        grads_attn[:, qkv_cols:].T,
        own_part(width, share),
        jnp.concatenate([g[:, :units] for g in grads_ffn], axis=1),
        jnp.concatenate([g[:, units : 2 * units] for g in grads_ffn], axis=1),
        jnp.concatenate([g[:, 2 * units :] for g in grads_ffn], axis=1).T,
    )


def solution(mesh):
    dp, tensor = mesh.shape["dp"], mesh.shape["tensor"]
    kind = Links if (dp, tensor) == (8, 4) else Direct
    weight, weight_t = P("dp", "tensor"), P("tensor", "dp")
    acts, ids = P(None, ("dp", "tensor"), None), P(None, "dp")
    gain = P("dp")

    def step(*args):
        return on_device(lambda: kind(dp, tensor), *args)

    return jax.shard_map(
        step,
        mesh=mesh,
        in_specs=(
            acts,
            acts,
            ids,
            ids,
            ids,
            gain,
            weight,
            weight,
            weight,
            gain,
            gain,
            weight_t,
            gain,
            weight,
            weight,
            weight_t,
        ),
        out_specs=(
            acts,
            acts,
            gain,
            weight,
            weight,
            weight,
            gain,
            gain,
            weight_t,
            gain,
            weight,
            weight,
            weight_t,
        ),
        check_vma=False,
    )
```

time: 1650 us -> 1050 us (0.64)
  waiting for transfers between devices: 1090 us -> 403 us
  starting transfers between devices: 1.86 us -> 149 us
  matrix products: 252 us -> 166 us
  blocking collectives: 87.3 us -> 41.3 us
  local copies, waits for them, and re-layouts: 53.8 us -> 99.1 us
  Pallas kernels: 0 us -> 23.8 us
  other arithmetic: 132 us -> 154 us
    all_gather x20 -> x0, waiting for transfers between devices: 587 us -> none  [the longest x2 128 us: micro_step(): lax.all_gather(w_down, 'dp', axis=1, tiled=True)]
    ppermute x0 -> x107, waiting for transfers between devices: none -> 403 us  [the longest x4 50.6 us: scatter_grads(): pair = add_rounded(pair, lax.ppermute(two[0], 'dp', INNER))]
    reduce_scatter x13 -> x0, waiting for transfers between devices: 383 us -> none  [the longest x1 69.7 us: on_device(): lax.psum_scatter(totals[8].astype(jnp.bfloat16), 'dp', scatter_dimension=...]
    ppermute x0 -> x107, starting transfers between devices: none -> 149 us  [the longest x4 13.4 us: gather_weights(): over_pair = lax.ppermute(pair, 'dp', INNER)]
    psum x2 -> x0, waiting for transfers between devices: 110 us -> none  [micro_step(): lax.psum(jnp.dot(mixed_bf, wo_full, preferred_element_type=jnp.float32).a...]
    dot_general x54 -> x38, matrix products: 252 us -> 166 us  [the longest x8 56 us: dot_nt(): lax.dot_general(left, right, (((1,), (1,)), ((), ())), preferred_element_...]
    convert_element_type x36 -> x25, other arithmetic: 76 us -> 30.8 us  [the longest x16 20.4 us: add_rounded(): return (left.astype(F32) + right.astype(F32)).astype(BF16)]
    unnamed x13 -> x401, local copies, waits for them, and re-layouts: 1.21 us -> 38.3 us
  transfers between devices with their start and end apart: 35 -> 107, of which waited for: 32 -> 52; matrix products, arithmetic and copies ran while one was open for 21% -> 33% of each run, Pallas kernels for 0% -> 2%
where the time goes in v1:
time: 1050 us; the launch traced here: 1040 us
  waiting for transfers between devices  403 us (38%)
  matrix products  166 us (16%)
  other arithmetic  154 us (15%)
  starting transfers between devices  149 us (14%)
  local copies, waits for them, and re-layouts  99.1 us (9%)
  blocking collectives  41.3 us (4%)
  Pallas kernels  23.8 us (2%)
    dot_general x8, matrix products, dot_nt(): lax.dot_general(left, right, (((1,), (1,)), ((), ())), preferred_element_...  56 us
    dot_general x16, matrix products, dot_tn(): lax.dot_general(left, right, (((0,), (0,)), ((), ())), preferred_element_...  51.8 us
    ppermute x4, waiting for transfers between devices, scatter_grads(): pair = add_rounded(pair, lax.ppermute(two[0], 'dp', INNER))  50.6 us
    ppermute x4, waiting for transfers between devices, gather_weights(): out_pair = lax.ppermute(over_pair, 'dp', OUTWARD)  44.2 us
    ppermute x4, waiting for transfers between devices, scatter_grads(): three = add_rounded(three, lax.ppermute(two[1], 'dp', INWARD))  41.9 us
    ppermute x4, waiting for transfers between devices, gather_weights(): pair = lax.ppermute(buf, 'dp', PAIR)  41.4 us
    psum x1, blocking collectives, on_device(): lax.psum(jnp.concatenate([net.plain_vector(acc_attn_gain), net.plain_vect...  41.3 us
    unnamed x401, local copies, waits for them, and re-layouts  38.3 us
  transfers between devices with their start and end apart: 107, of which 52 were waited for; matrix products, arithmetic and copies ran while one was open for 33% of the time, Pallas kernels for 2%

profile of v1, /device:TPU:8, one launch (start us, length us, event | category | flops | bytes accessed | tf_op | source)
XLA Modules:
  0.0 1040.2 jit_solution(14233512976572893059)
XLA Ops:
  90.5 16.2 %collective-permute-done.43 = bf16[256,1536]{0,1:T(8,128)(2,1)S(1)} collective-permute-done((bf16[256,1536]{0,1:T(8,128)(2,1)}, bf16[256,1536]{0,1:T(8,128)(2,1)S(1)}, u32[]{:S(2)}, u32[]{:S(2)}) %collective-permute-start.43) | collective-permute-done | bytes 786464 | tf_op jit(solution)/shard_map/ppermute | solution.py:144
  110.4 12.1 %collective-permute-done.37 = bf16[256,1536]{0,1:T(8,128)(2,1)S(1)} collective-permute-done((bf16[256,1536]{0,1:T(8,128)(2,1)}, bf16[256,1536]{0,1:T(8,128)(2,1)S(1)}, u32[]{:S(2)}, u32[]{:S(2)}) %collective-permute-start.37) | collective-permute-done | bytes 786464 | tf_op jit(solution)/shard_map/ppermute | solution.py:144
  172.4 10.7 %collective-permute-done.35 = bf16[256,1536]{0,1:T(8,128)(2,1)S(1)} collective-permute-done((bf16[256,1536]{0,1:T(8,128)(2,1)S(1)}, bf16[256,1536]{0,1:T(8,128)(2,1)S(1)}, u32[]{:S(2)}, u32[]{:S(2)}) %collective-permute-start.35) | collective-permute-done | bytes 786464 | tf_op jit(solution)/shard_map/ppermute | solution.py:148
  183.6 14.0 %collective-permute-done.17 = bf16[256,1536]{0,1:T(8,128)(2,1)S(1)} collective-permute-done((bf16[256,1536]{0,1:T(8,128)(2,1)S(1)}, bf16[256,1536]{0,1:T(8,128)(2,1)S(1)}, u32[]{:S(2)}, u32[]{:S(2)}) %collective-permute-start.17) | collective-permute-done | bytes 786464 | tf_op jit(solution)/shard_map/ppermute | solution.py:148
  230.7 9.7 collective-permute-done.38
  255.3 19.5 %collective-permute-done.41 = bf16[256,1536]{0,1:T(8,128)(2,1)S(1)} collective-permute-done((bf16[256,1536]{0,1:T(8,128)(2,1)S(1)}, bf16[256,1536]{0,1:T(8,128)(2,1)S(1)}, u32[]{:S(2)}, u32[]{:S(2)}) %collective-permute-start.41) | collective-permute-done | bytes 786464 | tf_op jit(solution)/shard_map/ppermute | solution.py:148
  293.8 11.2 %subtract_convert_fusion = (bf16[2,512,4,64]{3,2,1,0:T(4,128)(2,1)S(1)}, bf16[2,512,4,64]{3,2,1,0:T(4,128)(2,1)S(1)}) fusion(f32[2,512,4,128]{3,2,1,0:T(4,128)S(1)} %multiply_multiply_fusion, f32[2,512,64]{2,1,0:T(8,128)S(1)} %copy-done.58, f32[2,512,64]{2,1,0:T(8,128)S(1)} %get-tuple-element.231), kind=kLoop, calls=%fused_computation.142 | loop fusion | flops 2097152 | bytes 3670016 | tf_op jit(solution)/shard_map/convert.4
  400.6 9.4 collective-permute-done.27
  483.6 14.1 %add_convert_fusion = bf16[1024,2048]{1,0:T(8,128)(2,1)} fusion(f32[1024,2048]{1,0:T(8,128)} %fusion.12, f32[1024,2048]{1,0:T(8,128)} %fusion.8, bf16[2048,1536]{0,1:T(8,128)(2,1)} %constant_dynamic-update-slice_fusion.15, bf16[1024,512]{0,1:T(8,128)(2,1)} %copy-done.172, bf16[1024,512]{0,1:T(8,128)(2,1)S(1)} %get-tuple-element.133), kind=kOutput, calls=%fused_computation.8 | convolution fusion | flops 4305453056 | bytes 27262976 | tf_op jit(solution)/shard_map/dot_general | solution.py:36
  515.1 10.6 %collective-permute-done.50 = bf16[128,2048]{1,0:T(8,128)(2,1)S(1)} collective-permute-done((bf16[128,2048]{1,0:T(8,128)(2,1)S(1)}, bf16[128,2048]{1,0:T(8,128)(2,1)S(1)}, u32[]{:S(2)}, u32[]{:S(2)}) %collective-permute-start.50) | collective-permute-done | bytes 524320 | tf_op jit(solution)/shard_map/ppermute | solution.py:191
  542.8 10.7 %collective-permute-done.63 = bf16[128,2048]{1,0:T(8,128)(2,1)S(1)} collective-permute-done((bf16[128,2048]{1,0:T(8,128)(2,1)S(1)}, bf16[128,2048]{1,0:T(8,128)(2,1)S(1)}, u32[]{:S(2)}, u32[]{:S(2)}) %collective-permute-start.63) | collective-permute-done | bytes 524320 | tf_op jit(solution)/shard_map/ppermute | solution.py:193
  554.5 10.1 collective-permute-done.53
  565.2 10.7 %collective-permute-done.51 = bf16[128,2048]{1,0:T(8,128)(2,1)S(1)} collective-permute-done((bf16[128,2048]{1,0:T(8,128)(2,1)S(1)}, bf16[128,2048]{1,0:T(8,128)(2,1)S(1)}, u32[]{:S(2)}, u32[]{:S(2)}) %collective-permute-start.51) | collective-permute-done | bytes 524320 | tf_op jit(solution)/shard_map/ppermute | solution.py:193
  678.8 16.7 %multiply_reduce_fusion.3 = (f32[2,512,4]{2,1,0:T(8,128)S(1)}, f32[2,512,4,128]{3,2,1,0:T(4,128)}) fusion(f32[2,512,4,128]{3,2,1,0:T(4,128)S(1)} %copy-done.2, f32[128]{0:T(128)S(1)} %copy-done.148, f32[2,512,4]{2,1,0:T(8,128)S(1)} %copy-done.48, f32[2,512,4,64]{3,2,1,0:T(4,128)S(1)} %get-tuple-element.140, f32[2,512,4,64]{3,2,1,0:T(4,128)S(1)} %get-tuple-element.139), kind=kLoop, calls=%fused_computation.118 | loop fusion | flops 2617344 | bytes 6324736 | tf_op jit(solution)/shard_map/reduce_sum | solution.py:205
  733.2 41.3 %psum.7 = f32[4352]{0:T(1024)S(1)} all-reduce(f32[4352]{0:T(1024)S(1)} %pad_maximum_fusion.37), channel_id=1, replica_groups=mesh['dp'=8,'tensor'=4] {'dp','tensor'}, use_global_device_ids=true, to_apply=%region_23.24 | all-reduce | flops 4352 | bytes 34816 | tf_op jit(solution)/shard_map/psum | solution.py:375
  792.6 13.4 %collective-permute-done.90 = bf16[256,1536]{0,1:T(8,128)(2,1)S(1)} collective-permute-done((bf16[256,1536]{0,1:T(8,128)(2,1)S(1)}, bf16[256,1536]{0,1:T(8,128)(2,1)S(1)}, u32[]{:S(2)}, u32[]{:S(2)}) %collective-permute-start.90) | collective-permute-done | bytes 786464 | tf_op jit(solution)/shard_map/ppermute | solution.py:163
  810.3 10.3 collective-permute-done.97
  872.9 13.4 %collective-permute-done.91 = bf16[256,1536]{0,1:T(8,128)(2,1)} collective-permute-done((bf16[256,1536]{0,1:T(8,128)(2,1)}, bf16[256,1536]{0,1:T(8,128)(2,1)}, u32[]{:S(2)}, u32[]{:S(2)}) %collective-permute-start.91) | collective-permute-done | bytes 786464 | tf_op jit(solution)/shard_map/ppermute | solution.py:165
  890.8 12.3 %collective-permute-done.98 = bf16[256,1536]{0,1:T(8,128)(2,1)} collective-permute-done((bf16[256,1536]{0,1:T(8,128)(2,1)}, bf16[256,1536]{0,1:T(8,128)(2,1)}, u32[]{:S(2)}, u32[]{:S(2)}) %collective-permute-start.98) | collective-permute-done | bytes 786464 | tf_op jit(solution)/shard_map/ppermute | solution.py:165
  908.4 11.5 %collective-permute-done.105 = bf16[256,1536]{0,1:T(8,128)(2,1)S(1)} collective-permute-done((bf16[256,1536]{0,1:T(8,128)(2,1)}, bf16[256,1536]{0,1:T(8,128)(2,1)S(1)}, u32[]{:S(2)}, u32[]{:S(2)}) %collective-permute-start.105) | collective-permute-done | bytes 786464 | tf_op jit(solution)/shard_map/ppermute | solution.py:165
  926.7 13.6 %collective-permute-done.92 = bf16[256,1536]{0,1:T(8,128)(2,1)S(1)} collective-permute-done((bf16[256,1536]{0,1:T(8,128)(2,1)S(1)}, bf16[256,1536]{0,1:T(8,128)(2,1)S(1)}, u32[]{:S(2)}, u32[]{:S(2)}) %collective-permute-start.92) | collective-permute-done | bytes 786464 | tf_op jit(solution)/shard_map/ppermute | solution.py:167
  943.1 41.9 %collective-permute-done.81 = bf16[256,1536]{0,1:T(8,128)(2,1)S(1)} collective-permute-done((bf16[256,1536]{0,1:T(8,128)(2,1)S(1)}, bf16[256,1536]{0,1:T(8,128)(2,1)S(1)}, u32[]{:S(2)}, u32[]{:S(2)}) %collective-permute-start.81) | collective-permute-done | bytes 786464 | tf_op jit(solution)/shard_map/ppermute | solution.py:164
  990.0 10.2 collective-permute-done.83
  1007.6 13.4 %collective-permute-done.84 = bf16[256,1536]{0,1:T(8,128)(2,1)S(1)} collective-permute-done((bf16[256,1536]{0,1:T(8,128)(2,1)S(1)}, bf16[256,1536]{0,1:T(8,128)(2,1)S(1)}, u32[]{:S(2)}, u32[]{:S(2)}) %collective-permute-start.84) | collective-permute-done | bytes 786464 | tf_op jit(solution)/shard_map/ppermute | solution.py:165
  (820 shorter events, 679.2 us)
Async XLA Ops:
  55.1 51.6 %collective-permute-start.43 = (bf16[256,1536]{0,1:T(8,128)(2,1)}, bf16[256,1536]{0,1:T(8,128)(2,1)S(1)}, u32[]{:S(2)}, u32[]{:S(2)}) collective-permute-start(bf16[256,1536]{0,1:T(8,128)(2,1)} %get-tuple-element.200), channel_id=1, source_target_pairs={{0,8},{4,12},{8,0},{12,4},{16,24},{20,28},{24,16},{28,20},{1,9},{5... | collective-permute-start | bytes 2359304 | tf_op jit(solution)/shard_map/ppermute | solution.py:144
  65.1 57.4 %collective-permute-start.37 = (bf16[256,1536]{0,1:T(8,128)(2,1)}, bf16[256,1536]{0,1:T(8,128)(2,1)S(1)}, u32[]{:S(2)}, u32[]{:S(2)}) collective-permute-start(bf16[256,1536]{0,1:T(8,128)(2,1)} %get-tuple-element.211), channel_id=1, source_target_pairs={{0,8},{4,12},{8,0},{12,4},{16,24},{20,28},{24,16},{28,20},{1,9},{5... | collective-permute-start | bytes 2359304 | tf_op jit(solution)/shard_map/ppermute | solution.py:144
  73.1 55.2 %collective-permute-start.33 = (bf16[256,1536]{0,1:T(8,128)(2,1)}, bf16[256,1536]{0,1:T(8,128)(2,1)S(1)}, u32[]{:S(2)}, u32[]{:S(2)}) collective-permute-start(bf16[256,1536]{0,1:T(8,128)(2,1)} %get-tuple-element.213), channel_id=1, source_target_pairs={{8,16},{12,20},{16,8},{20,12},{9,17},{13,21},{17,9},{21,13},{10,18... | collective-permute-start | bytes 2359304 | tf_op jit(solution)/shard_map/ppermute | solution.py:145
  79.5 53.7 %collective-permute-start.15 = (bf16[256,1536]{0,1:T(8,128)(2,1)}, bf16[256,1536]{0,1:T(8,128)(2,1)S(1)}, u32[]{:S(2)}, u32[]{:S(2)}) collective-permute-start(bf16[256,1536]{0,1:T(8,128)(2,1)} %get-tuple-element.215), channel_id=1, source_target_pairs={{8,16},{12,20},{16,8},{20,12},{9,17},{13,21},{17,9},{21,13},{10,18... | collective-permute-start | bytes 2359304 | tf_op jit(solution)/shard_map/ppermute | solution.py:145
  146.8 57.9 %collective-permute-start.56 = (bf16[128,2048]{1,0:T(8,128)(2,1)S(1)}, bf16[128,2048]{1,0:T(8,128)(2,1)S(1)}, u32[]{:S(2)}, u32[]{:S(2)}) collective-permute-start(bf16[128,2048]{1,0:T(8,128)(2,1)S(1)} %copy-done.100), channel_id=1, source_target_pairs={{0,2},{1,3},{2,0},{3,1},{4,6},{5,7},{6,4},{7,5},{8,10},{9,11},{10,... | collective-permute-start | bytes 1572872 | tf_op jit(solution)/shard_map/ppermute | solution.py:174
  210.2 66.6 %collective-permute-start.18 = (bf16[1024,1536]{0,1:T(8,128)(2,1)S(1)}, bf16[1024,1536]{0,1:T(8,128)(2,1)S(1)}, u32[]{:S(2)}, u32[]{:S(2)}) collective-permute-start(bf16[1024,1536]{0,1:T(8,128)(2,1)S(1)} %pad_maximum_fusion.4), channel_id=1, source_target_pairs={{0,4},{4,0},{8,12},{12,8},{16,20},{20,16},{24,28},{28,24},{1,5},{5... | collective-permute-start | bytes 9437192 | tf_op jit(solution)/shard_map/ppermute | solution.py:152
  227.1 130.0 %collective-permute-start.58 = (bf16[128,2048]{1,0:T(8,128)(2,1)}, bf16[128,2048]{1,0:T(8,128)(2,1)}, u32[]{:S(2)}, u32[]{:S(2)}) collective-permute-start(bf16[128,2048]{1,0:T(8,128)(2,1)} %get-tuple-element.195), channel_id=1, source_target_pairs={{0,1},{1,0},{2,3},{3,2},{4,5},{5,4},{6,7},{7,6},{8,9},{9,8},{10,11... | collective-permute-start | bytes 1572872 | tf_op jit(solution)/shard_map/ppermute | solution.py:173
  228.6 130.1 %collective-permute-start.60 = (bf16[128,2048]{1,0:T(8,128)(2,1)}, bf16[128,2048]{1,0:T(8,128)(2,1)}, u32[]{:S(2)}, u32[]{:S(2)}) collective-permute-start(bf16[128,2048]{1,0:T(8,128)(2,1)} %collective-permute-done.59), channel_id=1, source_target_pairs={{0,1},{1,0},{2,3},{3,2},{4,5},{5,4},{6,7},{7,6},{8,9},{9,8},{10,11... | collective-permute-start | bytes 1572872 | tf_op jit(solution)/shard_map/ppermute | solution.py:176
  467.2 60.1 %collective-permute-start.87 = (bf16[1024,512]{0,1:T(8,128)(2,1)}, bf16[1024,512]{0,1:T(8,128)(2,1)}, u32[]{:S(2)}, u32[]{:S(2)}) collective-permute-start(bf16[1024,512]{0,1:T(8,128)(2,1)} %fusion.102), channel_id=1, source_target_pairs={{0,4},{4,0},{8,12},{12,8},{16,20},{20,16},{24,28},{28,24},{1,5},{5... | collective-permute-start | bytes 3145736 | tf_op jit(solution)/shard_map/ppermute | solution.py:161
  513.5 89.6 %collective-permute-start.86 = (bf16[1024,1024]{0,1:T(8,128)(2,1)}, bf16[1024,1024]{0,1:T(8,128)(2,1)}, u32[]{:S(2)}, u32[]{:S(2)}) collective-permute-start(bf16[1024,1024]{0,1:T(8,128)(2,1)} %convolution_convert_fusion.3), channel_id=1, source_target_pairs={{0,4},{4,0},{8,12},{12,8},{16,20},{20,16},{24,28},{28,24},{1,5},{5... | collective-permute-start | bytes 6291464 | tf_op jit(solution)/shard_map/ppermute | solution.py:161
  535.2 74.0 %collective-permute-start.93 = (bf16[1024,1024]{0,1:T(8,128)(2,1)}, bf16[1024,1024]{0,1:T(8,128)(2,1)}, u32[]{:S(2)}, u32[]{:S(2)}) collective-permute-start(bf16[1024,1024]{0,1:T(8,128)(2,1)} %convolution_convert_fusion.2), channel_id=1, source_target_pairs={{0,4},{4,0},{8,12},{12,8},{16,20},{20,16},{24,28},{28,24},{1,5},{5... | collective-permute-start | bytes 6291464 | tf_op jit(solution)/shard_map/ppermute | solution.py:161
  554.5 60.7 %collective-permute-start.100 = (bf16[1024,1024]{0,1:T(8,128)(2,1)}, bf16[1024,1024]{0,1:T(8,128)(2,1)}, u32[]{:S(2)}, u32[]{:S(2)}) collective-permute-start(bf16[1024,1024]{0,1:T(8,128)(2,1)} %convolution_convert_fusion.1), channel_id=1, source_target_pairs={{0,4},{4,0},{8,12},{12,8},{16,20},{20,16},{24,28},{28,24},{1,5},{5... | collective-permute-start | bytes 6291464 | tf_op jit(solution)/shard_map/ppermute | solution.py:161
  615.2 160.6 %collective-permute-start.88 = (bf16[256,1536]{0,1:T(8,128)(2,1)}, bf16[256,1536]{0,1:T(8,128)(2,1)}, u32[]{:S(2)}, u32[]{:S(2)}) collective-permute-start(bf16[256,1536]{0,1:T(8,128)(2,1)} %fusion.135), channel_id=1, source_target_pairs={{0,8},{4,12},{24,16},{28,20},{1,9},{5,13},{25,17},{29,21},{2,10},{... | collective-permute-start | bytes 2359304 | tf_op jit(solution)/shard_map/ppermute | solution.py:164
  627.5 153.2 %collective-permute-start.95 = (bf16[256,1536]{0,1:T(8,128)(2,1)}, bf16[256,1536]{0,1:T(8,128)(2,1)}, u32[]{:S(2)}, u32[]{:S(2)}) collective-permute-start(bf16[256,1536]{0,1:T(8,128)(2,1)} %fusion.132), channel_id=1, source_target_pairs={{0,8},{4,12},{24,16},{28,20},{1,9},{5,13},{25,17},{29,21},{2,10},{... | collective-permute-start | bytes 2359304 | tf_op jit(solution)/shard_map/ppermute | solution.py:164
  632.6 150.8 %collective-permute-start.102 = (bf16[256,1536]{0,1:T(8,128)(2,1)}, bf16[256,1536]{0,1:T(8,128)(2,1)}, u32[]{:S(2)}, u32[]{:S(2)}) collective-permute-start(bf16[256,1536]{0,1:T(8,128)(2,1)} %fusion.129), channel_id=1, source_target_pairs={{0,8},{4,12},{24,16},{28,20},{1,9},{5,13},{25,17},{29,21},{2,10},{... | collective-permute-start | bytes 2359304 | tf_op jit(solution)/shard_map/ppermute | solution.py:164
  729.7 94.8 %collective-permute-start.80 = (bf16[1024,512]{0,1:T(8,128)(2,1)}, bf16[1024,512]{0,1:T(8,128)(2,1)}, u32[]{:S(2)}, u32[]{:S(2)}) collective-permute-start(bf16[1024,512]{0,1:T(8,128)(2,1)} %fusion.105), channel_id=1, source_target_pairs={{0,4},{4,0},{8,12},{12,8},{16,20},{20,16},{24,28},{28,24},{1,5},{5... | collective-permute-start | bytes 3145736 | tf_op jit(solution)/shard_map/ppermute | solution.py:161
  729.7 190.5 %collective-permute-start.79 = (bf16[1024,1024]{0,1:T(8,128)(2,1)}, bf16[1024,1024]{0,1:T(8,128)(2,1)}, u32[]{:S(2)}, u32[]{:S(2)}) collective-permute-start(bf16[1024,1024]{0,1:T(8,128)(2,1)} %fusion.47), channel_id=1, source_target_pairs={{0,4},{4,0},{8,12},{12,8},{16,20},{20,16},{24,28},{28,24},{1,5},{5... | collective-permute-start | bytes 6291464 | tf_op jit(solution)/shard_map/ppermute | solution.py:161
  780.7 48.7 %collective-permute-start.73 = (bf16[128,2048]{1,0:T(8,128)(2,1)S(1)}, bf16[128,2048]{1,0:T(8,128)(2,1)S(1)}, u32[]{:S(2)}, u32[]{:S(2)}) collective-permute-start(bf16[128,2048]{1,0:T(8,128)(2,1)S(1)} %copy-done.128), channel_id=1, source_target_pairs={{0,1},{1,0},{2,3},{3,2},{4,5},{5,4},{6,7},{7,6},{8,9},{9,8},{10,11... | collective-permute-start | bytes 1572872 | tf_op jit(solution)/shard_map/ppermute | solution.py:192
  830.0 96.6 %collective-permute-start.89 = (bf16[256,1536]{0,1:T(8,128)(2,1)}, bf16[256,1536]{0,1:T(8,128)(2,1)}, u32[]{:S(2)}, u32[]{:S(2)}) collective-permute-start(bf16[256,1536]{0,1:T(8,128)(2,1)} %get-tuple-element.97), channel_id=1, source_target_pairs={{8,16},{12,20},{16,8},{20,12},{9,17},{13,21},{17,9},{21,13},{10,18... | collective-permute-start | bytes 2359304 | tf_op jit(solution)/shard_map/ppermute | solution.py:166
  835.4 152.1 %collective-permute-start.96 = (bf16[256,1536]{0,1:T(8,128)(2,1)}, bf16[256,1536]{0,1:T(8,128)(2,1)}, u32[]{:S(2)}, u32[]{:S(2)}) collective-permute-start(bf16[256,1536]{0,1:T(8,128)(2,1)} %get-tuple-element.99), channel_id=1, source_target_pairs={{8,16},{12,20},{16,8},{20,12},{9,17},{13,21},{17,9},{21,13},{10,18... | collective-permute-start | bytes 2359304 | tf_op jit(solution)/shard_map/ppermute | solution.py:166
  853.1 50.0 %collective-permute-start.98 = (bf16[256,1536]{0,1:T(8,128)(2,1)}, bf16[256,1536]{0,1:T(8,128)(2,1)}, u32[]{:S(2)}, u32[]{:S(2)}) collective-permute-start(bf16[256,1536]{0,1:T(8,128)(2,1)} %add_convert_fusion.15), channel_id=1, source_target_pairs={{8,16},{12,20},{16,8},{20,12},{9,17},{13,21},{17,9},{21,13},{10,18... | collective-permute-start | bytes 2359304 | tf_op jit(solution)/shard_map/ppermute | solution.py:165
  903.1 100.3 %collective-permute-start.103 = (bf16[256,1536]{0,1:T(8,128)(2,1)S(1)}, bf16[256,1536]{0,1:T(8,128)(2,1)S(1)}, u32[]{:S(2)}, u32[]{:S(2)}) collective-permute-start(bf16[256,1536]{0,1:T(8,128)(2,1)S(1)} %copy-done.120), channel_id=1, source_target_pairs={{8,16},{12,20},{16,8},{20,12},{9,17},{13,21},{17,9},{21,13},{10,18... | collective-permute-start | bytes 2359304 | tf_op jit(solution)/shard_map/ppermute | solution.py:166
  920.2 67.3 %collective-permute-start.99 = (bf16[256,1536]{0,1:T(8,128)(2,1)S(1)}, bf16[256,1536]{0,1:T(8,128)(2,1)S(1)}, u32[]{:S(2)}, u32[]{:S(2)}) collective-permute-start(bf16[256,1536]{0,1:T(8,128)(2,1)S(1)} %add_convert_fusion.14), channel_id=1, source_target_pairs={{0,8},{4,12},{8,0},{12,4},{16,24},{20,28},{24,16},{28,20},{1,9},{5... | collective-permute-start | bytes 2359304 | tf_op jit(solution)/shard_map/ppermute | solution.py:167
  926.5 76.9 %collective-permute-start.106 = (bf16[256,1536]{0,1:T(8,128)(2,1)S(1)}, bf16[256,1536]{0,1:T(8,128)(2,1)S(1)}, u32[]{:S(2)}, u32[]{:S(2)}) collective-permute-start(bf16[256,1536]{0,1:T(8,128)(2,1)S(1)} %add_convert_fusion.11), channel_id=1, source_target_pairs={{0,8},{4,12},{8,0},{12,4},{16,24},{20,28},{24,16},{28,20},{1,9},{5... | collective-permute-start | bytes 2359304 | tf_op jit(solution)/shard_map/ppermute | solution.py:167
  (269 other events, 5170.4 us)

commit v2 on v1

--- a/solution.py
+++ b/solution.py
@@ -16,6 +16,7 @@
 
 ORDER = (0, 2, 4, 6, 1, 3, 5, 7)
 PAIR = [(d, d ^ 2) for d in range(8)]
+ACROSS = [(d, d ^ 4) for d in range(8)]
 CORE = [(d, d ^ 1) for d in range(8)]
 INNER = [(2, 4), (3, 5), (4, 2), (5, 3)]
 OUTWARD = [(2, 0), (3, 1), (4, 6), (5, 7)]
@@ -63,11 +64,97 @@
     )(table, rows)
 
 
+class Job:
+    def __init__(self, gen, open_at):
+        self.gen, self.open_at = gen, open_at
+        self.rounds, self.flight, self.value, self.done = 0, (), None, False
+
+    def step(self, results, anchor=()):
+        try:
+            sends = self.gen.send(results)
+        except StopIteration as stop:
+            self.value, self.done, self.flight = stop.value, True, ()
+            return
+        arrays = [array for array, _ in sends]
+        if anchor:
+            arrays = lax.optimization_barrier((*arrays, *anchor))[: len(arrays)]
+        self.flight = tuple(
+            lax.ppermute(array, "dp", perm) for array, (_, perm) in zip(arrays, sends)
+        )
+        self.rounds += 1
+
+    @property
+    def open(self):
+        return self.done or self.rounds >= self.open_at
+
+
+class Rounds:
+    def __init__(self):
+        self.live, self.queue = [], []
+
+    def add(self, gen, open_at):
+        job = Job(gen, open_at)
+        self.queue.append(job)
+        return job
+
+    def pump(self, *values):
+        flight = [array for job in self.live for array in job.flight]
+        if flight:
+            out = lax.optimization_barrier((*values, *flight))
+            values, flight = out[: len(values)], list(out[len(values) :])
+            for job in self.live:
+                count = len(job.flight)
+                results, flight = flight[:count], flight[count:]
+                job.step(results)
+            self.live = [job for job in self.live if not job.done]
+        while self.queue and all(job.open for job in self.live):
+            job = self.queue.pop(0)
+            job.step(None, values[:1])
+            if not job.done:
+                self.live.append(job)
+        return values
+
+    def drain(self):
+        while self.live or self.queue:
+            self.pump()
+
+
+class Steps:
+    def __init__(self, gen):
+        self.gen, self.pending, self.value = gen, (), None
+        self.feed(None)
+
+    def feed(self, results):
+        try:
+            self.pending = self.gen.send(results)
+        except StopIteration as stop:
+            self.value, self.pending = stop.value, ()
+
+
 class Direct:
     def __init__(self, dp, tensor):
         self.dp, self.tensor = dp, tensor
         self.me = lax.axis_index("dp")
         self.own = lax.axis_index("tensor")
+        self.rounds = Rounds()
+
+    def mix(self, steps, *values):
+        out = self.rounds.pump(*values, *steps.pending)
+        if steps.pending:
+            steps.feed(out[len(values) :])
+        return out[: len(values)]
+
+    def run(self, gen):
+        steps = Steps(gen)
+        while steps.pending:
+            self.mix(steps)
+        return steps.value
+
+    def free(self, gen):
+        steps = gen if isinstance(gen, Steps) else Steps(gen)
+        while steps.pending:
+            steps.feed(steps.pending)
+        return steps.value
 
     def to_local(self, rows):
         return rows
@@ -90,18 +177,25 @@
     def plain_vector(self, vector):
         return vector
 
+    def sum_all(self, vector):
+        return lax.psum(vector, ("dp", "tensor"))
+
     def gather_weights(self, buf):
         return lax.all_gather(buf, "dp", axis=0, tiled=True)
+        yield
 
     def scatter_grads(self, parts):
         full = jnp.concatenate([dot_tn(l, r).astype(BF16) for l, r in parts], axis=1)
         return lax.psum_scatter(full, "dp", scatter_dimension=0, tiled=True).astype(F32)
+        yield
 
     def gather_rows(self, rows):
         return lax.all_gather(rows, "tensor", axis=1, tiled=True)
+        yield
 
     def scatter_rows(self, partial):
         return lax.psum_scatter(partial, "tensor", scatter_dimension=1, tiled=True).astype(F32)
+        yield
 
 
 class Links(Direct):
@@ -110,7 +204,6 @@
         z = self.me // 2
         self.inner = (z == 1) | (z == 2)
         self.blocks = self.me ^ jnp.array(ORDER, jnp.int32)
-        place = jnp.array([ORDER.index(b) for b in range(8)], jnp.int32)
         hit = (self.me ^ jnp.arange(8, dtype=jnp.int32))[:, None] == jnp.array(ORDER, jnp.int32)
         self.hit = hit
         self.places = jnp.sum(jnp.where(hit, jnp.arange(8, dtype=jnp.int32)[None, :], 0), axis=1)
@@ -129,10 +222,10 @@
         return jnp.concatenate(parts, axis=-1)
 
     def gather_gains(self, packed):
-        got = [packed]
-        for b in ORDER[1:]:
-            got.append(lax.ppermute(packed, "dp", [(d, d ^ b) for d in range(8)]))
-        return jnp.stack(got)
+        got = packed[None]
+        for perm in (PAIR, ACROSS, CORE):
+            got = jnp.concatenate([got, lax.ppermute(got, "dp", perm)], axis=0)
+        return got
 
     def gains_plain(self, blocks):
         return jnp.sum(jnp.where(self.hit[:, :, None], blocks[None], 0), axis=1).reshape(-1)
@@ -140,31 +233,43 @@
     def plain_vector(self, vector):
         return self.gains_plain(vector.reshape(8, -1))
 
+    def sum_all(self, vector):
+        for axis, perm in (
+            ("tensor", XNEXT),
+            ("tensor", YNEXT),
+            ("dp", CORE),
+            ("dp", PAIR),
+            ("dp", ACROSS),
+        ):
+            vector = vector + lax.ppermute(vector, axis, perm)
+        return vector
+
     def gather_weights(self, buf):
-        pair = lax.ppermute(buf, "dp", PAIR)
-        over_own = lax.ppermute(buf, "dp", INNER)
-        over_pair = lax.ppermute(pair, "dp", INNER)
-        out_own = lax.ppermute(over_own, "dp", OUTWARD)
-        out_pair = lax.ppermute(over_pair, "dp", OUTWARD)
-        far_two = jnp.where(self.inner, over_pair, out_own)
-        far_three = jnp.where(self.inner, over_own, out_pair)
-        mine = jnp.concatenate([buf, pair, far_two, far_three], axis=0)
-        other = lax.ppermute(mine, "dp", CORE)
-        return jnp.concatenate([mine, other], axis=0)
+        pair, over_own, other = yield [(buf, PAIR), (buf, INNER), (buf, CORE)]
+        over_pair, out_own, other_pair = yield [(pair, INNER), (over_own, OUTWARD), (pair, CORE)]
+        two = jnp.where(self.inner, over_pair, out_own)
+        out_pair, other_two = yield [(over_pair, OUTWARD), (two, CORE)]
+        three = jnp.where(self.inner, over_own, out_pair)
+        other_three = lax.ppermute(three, "dp", CORE)
+        return jnp.concatenate(
+            [buf, pair, two, three, other, other_pair, other_two, other_three], axis=0
+        )
 
     def scatter_grads(self, parts):
-        summed = []
+        away, half = [], parts[0][0].shape[1] // 2
         for left, right in parts:
-            half = left.shape[1] // 2
-            away = dot_tn(left[:, half:], right).astype(BF16)
-            here = dot_tn(left[:, :half], right)
-            summed.append((here + lax.ppermute(away, "dp", CORE).astype(F32)).astype(BF16))
+            away.append(dot_tn(left[:, half:], right).astype(BF16))
+        summed = [
+            (dot_tn(left[:, :half], right) + lax.ppermute(array, "dp", CORE).astype(F32)).astype(BF16)
+            for (left, right), array in zip(parts, away)
+        ]
         own, pair, two, three = jnp.split(jnp.concatenate(summed, axis=1), 4, axis=0)
-        two = add_rounded(two, lax.ppermute(three, "dp", INWARD)), two
-        three = add_rounded(three, lax.ppermute(two[1], "dp", INWARD))
-        pair = add_rounded(pair, lax.ppermute(two[0], "dp", INNER))
-        own = own.astype(F32) + lax.ppermute(three, "dp", INNER).astype(F32)
-        return own + lax.ppermute(pair, "dp", PAIR).astype(F32)
+        (got,) = yield [(three, INWARD)]
+        two_sum = add_rounded(two, got)
+        got, got_inner = yield [(two, INWARD), (two_sum, INNER)]
+        three, pair = add_rounded(three, got), add_rounded(pair, got_inner)
+        got_inner, got_pair = yield [(three, INNER), (pair, PAIR)]
+        return own.astype(F32) + got_inner.astype(F32) + got_pair.astype(F32)
 
     def gather_rows(self, rows):
         first, second = rows[0], rows[1]
@@ -172,8 +277,10 @@
         y_second = lax.ppermute(second, "tensor", YNEXT)
         x_second = lax.ppermute(second, "tensor", XNEXT)
         y_first = lax.ppermute(first, "tensor", YNEXT)
+        x_first, y_second = yield (x_first, y_second)
         d_first = lax.ppermute(x_first, "tensor", YNEXT)
         d_second = lax.ppermute(y_second, "tensor", XNEXT)
+        x_second, y_first, d_first, d_second = yield (x_second, y_first, d_first, d_second)
         return jnp.stack(
             [
                 jnp.concatenate([first, x_first, y_first, d_first], axis=0),
@@ -182,17 +289,26 @@
         )
 
     def scatter_rows(self, partial):
-        out = []
-        for part, near, far, a, b in (
-            (partial[0], XNEXT, YNEXT, 1, 2),
-            (partial[1], YNEXT, XNEXT, 2, 1),
-        ):
-            block = jnp.split(part, 4, axis=0)
-            got_diag = lax.ppermute(block[3], "tensor", near)
-            got_own = lax.ppermute(block[a], "tensor", near)
-            passed = lax.ppermute(add_rounded(block[b], got_diag), "tensor", far)
-            out.append(block[0].astype(F32) + got_own.astype(F32) + passed.astype(F32))
-        return jnp.stack(out)
+        first, second = (jnp.split(partial[i], 4, axis=0) for i in range(2))
+        diag_first = lax.ppermute(first[3], "tensor", XNEXT)
+        diag_second = lax.ppermute(second[3], "tensor", YNEXT)
+        near_first = lax.ppermute(first[1], "tensor", XNEXT)
+        near_second = lax.ppermute(second[2], "tensor", YNEXT)
+        diag_first, diag_second = yield (diag_first, diag_second)
+        far_first = lax.ppermute(add_rounded(first[2], diag_first), "tensor", YNEXT)
+        far_second = lax.ppermute(add_rounded(second[1], diag_second), "tensor", XNEXT)
+        near_first, near_second, far_first, far_second = yield (
+            near_first,
+            near_second,
+            far_first,
+            far_second,
+        )
+        return jnp.stack(
+            [
+                first[0].astype(F32) + near_first.astype(F32) + far_first.astype(F32),
+                second[0].astype(F32) + near_second.astype(F32) + far_second.astype(F32),
+            ]
+        )
 
 
 def unit_of(rows):
@@ -248,14 +364,24 @@
     q_cols, kv_cols = w_query.shape[1], key_weight.shape[1]
     heads_q, heads_kv = q_cols // HEAD_SIZE, kv_cols // HEAD_SIZE
     groups = heads_q // heads_kv
-    qkv_cols = q_cols + 2 * kv_cols
     units = w_gate.shape[1] // CHUNKS
 
-    attn_buf = jnp.concatenate([w_query, key_weight, value_weight, w_out.T], axis=1)
-    w_attn = net.gather_weights(attn_buf)
-    w_qkv, w_out_t = w_attn[:, :qkv_cols], w_attn[:, qkv_cols:]
+    rounds = net.rounds
+    job_qkv = rounds.add(
+        net.gather_weights(jnp.concatenate([w_query, key_weight, value_weight], axis=1)), 2
+    )
+    job_out = rounds.add(net.gather_weights(w_out.T), 3)
+    ffn_jobs = []
+    for chunk in range(CHUNKS):
+        cut = slice(chunk * units, (chunk + 1) * units)
+        buf = jnp.concatenate([w_gate[:, cut], w_up[:, cut], w_down[cut, :].T], axis=1)
+        ffn_jobs.append(rounds.add(net.gather_weights(buf), 4))
+    for _ in range(3):
+        rounds.pump()
     x_own = net.to_local(hidden_in)
-    x_all = net.gather_rows(x_own).reshape(rows, width).astype(F32)
+    x_bf = net.free(net.gather_rows(x_own)).reshape(rows, width)
+    g_own, x_bf = lax.optimization_barrier((net.to_local(cotangent), x_bf))
+    g_steps = Steps(net.gather_rows(g_own))
     packed = jnp.concatenate(
         [attn_gain, ffn_gain, query_norm_gain, key_gain], axis=0
     )
@@ -264,16 +390,6 @@
     gain_two = net.gains_local(gains[:, share : 2 * share])
     gain_q = net.gains_plain(gains[:, 2 * share : 2 * share + head_share])
     gain_k = net.gains_plain(gains[:, 2 * share + head_share :])
-    ffn_sets = []
-    for chunk in range(CHUNKS):
-        cut = slice(chunk * units, (chunk + 1) * units)
-        ffn_sets.append(
-            net.gather_weights(
-                jnp.concatenate([w_gate[:, cut], w_up[:, cut], w_down[cut, :].T], axis=1)
-            )
-        )
-    g_own = net.to_local(cotangent)
-    g_all = net.gather_rows(g_own).reshape(rows, width)
 
     segment = net.row_order(segment_ids)
     offsets = net.row_order(positions)
@@ -281,9 +397,10 @@
     row_ids = net.row_order(jnp.arange(seq_len, dtype=jnp.int32))
     cosine, sine = rotary(offsets)
     valid_col = valid.reshape(rows, 1).astype(F32)
-    unit_all, _ = unit_of(x_all)
-    a1 = (unit_all * gain_one).astype(BF16)
-    qkv = dot_nn(a1, w_qkv)
+    unit_all, _ = unit_of(x_bf.astype(F32))
+    (a1,) = net.mix(g_steps, (unit_all * gain_one).astype(BF16))
+    w_qkv = job_qkv.value
+    (qkv,) = rounds.pump(dot_nn(a1, w_qkv))
     q_raw = qkv[:, :q_cols].reshape(micro, seq_len, heads_q, HEAD_SIZE)
     k_raw = qkv[:, q_cols : q_cols + kv_cols].reshape(micro, seq_len, heads_kv, HEAD_SIZE)
     value = (
@@ -297,6 +414,7 @@
         .reshape(micro, seq_len, heads_kv, groups, HEAD_SIZE)
     )
     key = rotate(k_unit * gain_k, cosine, sine).astype(BF16)
+    query, key = rounds.pump(query, key)
     allowed = (
         (segment[:, :, None] == segment[:, None, :])
         & (row_ids[None, None, :] <= row_ids[None, :, None])
@@ -308,47 +426,58 @@
     probs = jnp.where(allowed, jnp.exp(masked - lse), 0.0)
     probs_bf = probs.astype(BF16)
     mixed = jnp.einsum("mkgqt,mtkd->mqkgd", probs_bf, value, preferred_element_type=F32)
-    mixed_bf = (mixed.reshape(rows, q_cols) * valid_col).astype(BF16)
+    (mixed_bf,) = rounds.pump((mixed.reshape(rows, q_cols) * valid_col).astype(BF16))
+    w_out_t = job_out.value
     attn_part = dot_nt(mixed_bf, w_out_t).astype(BF16).reshape(micro, seq_len, width)
-    resid = x_own.astype(F32) + net.scatter_rows(attn_part)
+    resid = x_own.astype(F32) + net.run(net.scatter_rows(attn_part))
     unit_two, recip_two = unit_of(resid)
     a2_own = (unit_two * gain_two).astype(BF16)
-    a2 = net.gather_rows(a2_own).reshape(rows, width)
-
-    mlp = da2 = None
-    grads_ffn = []
+    a2 = net.run(net.gather_rows(a2_own)).reshape(rows, width)
+    g_all = net.free(g_steps).reshape(rows, width)
+
+    da2, inners = None, []
+    grad_jobs = []
     for chunk in range(CHUNKS):
-        w_chunk = ffn_sets[chunk]
+        w_chunk = ffn_jobs[chunk].value
         w_gu, w_down_t = w_chunk[:, : 2 * units], w_chunk[:, 2 * units :]
         gate_up = dot_nn(a2, w_gu)
+        d_inner = dot_nn(g_all, w_down_t)
+        (gate_up,) = rounds.pump(gate_up)
         gate, upper = gate_up[:, :units], gate_up[:, units:]
-        d_inner = dot_nn(g_all, w_down_t)
         sigma = jax.nn.sigmoid(gate)
         swish = gate * sigma
         inner = (swish * upper).astype(BF16)
         d_gate = (d_inner * upper * sigma * (1.0 + gate * (1.0 - sigma))).astype(BF16)
         d_upper = (d_inner * swish).astype(BF16)
         d_gu = jnp.concatenate([d_gate, d_upper], axis=1)
-        part_mlp = dot_nt(inner, w_down_t)
+        inner, d_gu = rounds.pump(inner, d_gu)
+        inners.append(inner)
         part_da2 = dot_nt(d_gu, w_gu)
-        mlp = part_mlp if mlp is None else mlp + part_mlp
         da2 = part_da2 if da2 is None else da2 + part_da2
-        grads_ffn.append(net.scatter_grads([(a2, d_gu), (g_all, inner)]))
-    d_normed_two = net.scatter_rows(da2.astype(BF16).reshape(micro, seq_len, width))
+        grad_jobs.append(rounds.add(net.scatter_grads([(a2, d_gu), (g_all, inner)]), 4))
+    da2, *inners = lax.optimization_barrier((da2.astype(BF16), *inners))
+    d_normed_two = net.run(net.scatter_rows(da2.reshape(micro, seq_len, width)))
+    mlp = sum(
+        dot_nt(inner, job.value[:, 2 * units :]) for inner, job in zip(inners, ffn_jobs)
+    )
     d_resid = g_own.astype(F32) + norm_back(d_normed_two, unit_two, recip_two, gain_two)
     acc_ffn_gain = jnp.sum(d_normed_two * unit_two, axis=(0, 1))
-    d_resid_all = net.gather_rows(d_resid.astype(BF16)).reshape(rows, width)
-    mlp_own = net.scatter_rows(mlp.astype(BF16).reshape(micro, seq_len, width))
-    layer_out = net.from_local((resid + mlp_own).astype(BF16))
+    d_resid_all = net.run(net.gather_rows(d_resid.astype(BF16))).reshape(rows, width)
+    d_resid_all, mlp = lax.optimization_barrier((d_resid_all, mlp.astype(BF16)))
+    mlp_steps = Steps(net.scatter_rows(mlp.reshape(micro, seq_len, width)))
+    job_grad_out = rounds.add(net.scatter_grads([(d_resid_all, mixed_bf)]), 4)
 
     d_mixed = dot_nn(d_resid_all, w_out_t).astype(BF16) * valid_col.astype(BF16)
+    (d_mixed,) = net.mix(mlp_steps, d_mixed)
     d_mixed = d_mixed.reshape(micro, seq_len, heads_kv, groups, HEAD_SIZE)
     d_probs = jnp.einsum("mqkgd,mtkd->mkgqt", d_mixed, value, preferred_element_type=F32)
     delta = jnp.sum(probs * d_probs, axis=-1, keepdims=True)
-    d_scores = (probs * (d_probs - delta)).astype(BF16)
+    (d_scores,) = net.mix(mlp_steps, (probs * (d_probs - delta)).astype(BF16))
+    layer_out = net.from_local((resid + mlp_steps.value).astype(BF16))
     d_query = scale * jnp.einsum("mkgqt,mtkd->mqkgd", d_scores, key, preferred_element_type=F32)
     d_key = scale * jnp.einsum("mkgqt,mqkgd->mtkd", d_scores, query, preferred_element_type=F32)
     d_value = jnp.einsum("mkgqt,mqkgd->mtkd", probs_bf, d_mixed, preferred_element_type=F32)
+    d_query, d_key, d_value = rounds.pump(d_query, d_key, d_value)
     d_query = rotate(
         d_query.reshape(micro, seq_len, heads_q, HEAD_SIZE), cosine, -sine
     )
@@ -363,16 +492,17 @@
         ],
         axis=1,
     )
-    da1 = dot_nt(d_qkv, w_qkv)
+    (d_qkv,) = rounds.pump(d_qkv)
+    job_grad_qkv = rounds.add(net.scatter_grads([(a1, d_qkv)]), 4)
+    (da1,) = rounds.pump(dot_nt(d_qkv, w_qkv))
     acc_attn_gain = jnp.sum(da1 * unit_all, axis=0)
-    d_normed = net.scatter_rows(da1.astype(BF16).reshape(micro, seq_len, width))
-    grads_attn = net.scatter_grads([(a1, d_qkv), (d_resid_all, mixed_bf)])
+    d_normed = net.run(net.scatter_rows(da1.astype(BF16).reshape(micro, seq_len, width)))
     unit_one, recip_one = unit_of(x_own.astype(F32))
     input_grad = net.from_local(
         (d_resid + norm_back(d_normed, unit_one, recip_one, gain_one)).astype(BF16)
     )
 
-    sums = lax.psum(
+    sums = net.sum_all(
         jnp.concatenate(
             [
                 net.plain_vector(acc_attn_gain),
@@ -380,9 +510,11 @@
                 acc_q_gain,
                 acc_k_gain,
             ]
-        ),
-        ("dp", "tensor"),
-    )
+        )
+    )
+    rounds.drain()
+    grad_qkv = job_grad_qkv.value
+    grads_ffn = [job.value for job in grad_jobs]
 
     def own_part(start, size):
         return lax.dynamic_slice_in_dim(sums, start + net.me * size, size, 0)
@@ -391,12 +523,12 @@
         layer_out,
         input_grad,
         own_part(0, share),
-        grads_attn[:, :q_cols],
-        grads_attn[:, q_cols : q_cols + kv_cols],
-        grads_attn[:, q_cols + kv_cols : qkv_cols],
+        grad_qkv[:, :q_cols],
+        grad_qkv[:, q_cols : q_cols + kv_cols],
+        grad_qkv[:, q_cols + kv_cols :],
         own_part(2 * width, head_share),
         own_part(2 * width + HEAD_SIZE, head_share),
-        grads_attn[:, qkv_cols:].T,
+        job_grad_out.value.T,
         own_part(width, share),
         jnp.concatenate([g[:, :units] for g in grads_ffn], axis=1),
         jnp.concatenate([g[:, units : 2 * units] for g in grads_ffn], axis=1),

time: 1050 us -> 821 us (0.78)
  waiting for transfers between devices: 403 us -> 197 us
  blocking collectives: 41.3 us -> 0 us
  local copies, waits for them, and re-layouts: 99.1 us -> 137 us
  other arithmetic: 154 us -> 118 us
  starting transfers between devices: 149 us -> 170 us
    ppermute x83 -> x110, waiting for transfers between devices: 367 us -> 132 us  [the longest x65 85 us: step(): lax.ppermute(array, 'dp', perm)]
    psum x1 -> x0, blocking collectives: 41.3 us -> none  [on_device(): lax.psum(jnp.concatenate([net.plain_vector(acc_attn_gain), net.plain_vect...]
    unnamed x401 -> x373, local copies, waits for them, and re-layouts: 38.3 us -> 74.1 us
    concatenate x8 -> x9, other arithmetic: 26 us -> 3.47 us  [the longest x3 2.26 us: rotate(): jnp.concatenate([low * cosine - high * sine, high * cosine + low * sine],...]
    ppermute x83 -> x110, starting transfers between devices: 124 us -> 145 us  [the longest x65 111 us: step(): lax.ppermute(array, 'dp', perm)]
    ppermute x4, waiting for transfers between devices: 2.39 us -> 23.6 us  [gather_rows(): d_second = lax.ppermute(y_second, 'tensor', XNEXT)]
    sub x0 -> x1, matrix products: none -> 14.7 us  [on_device(): d_scores, = net.mix(mlp_steps, (probs * (d_probs - delta)).astype(BF16))]
    reduce_sum x3 -> x2, other arithmetic: 18.7 us -> 4.8 us  [norm_back(): jnp.mean(scaled * unit, axis=-1, keepdims=True)]
  transfers between devices with their start and end apart: 107 -> 134, of which waited for: 52 -> 49; matrix products, arithmetic and copies ran while one was open for 33% -> 45% of each run, Pallas kernels for 2% -> 3%
where the time goes in v2:
time: 821 us; the launch traced here: 809 us
  waiting for transfers between devices  197 us (24%)
  starting transfers between devices  170 us (21%)
  matrix products  160 us (19%)
  local copies, waits for them, and re-layouts  137 us (17%)
  other arithmetic  118 us (14%)
  Pallas kernels  23.4 us (3%)
    ppermute x65, starting transfers between devices, step(): lax.ppermute(array, 'dp', perm)  111 us
    ppermute x65, waiting for transfers between devices, step(): lax.ppermute(array, 'dp', perm)  85 us
    unnamed x373, local copies, waits for them, and re-layouts  74.1 us
    dot_general x8, matrix products, dot_nt(): lax.dot_general(left, right, (((1,), (1,)), ((), ())), preferred_element_...  50.8 us
    dot_general x16, matrix products, dot_tn(): lax.dot_general(left, right, (((0,), (0,)), ((), ())), preferred_element_...  42.8 us
    dot_general x8, matrix products, dot_nn(): return jnp.dot(left, right, preferred_element_type=F32)  37.2 us
    ppermute x4, waiting for transfers between devices, gather_rows(): d_second = lax.ppermute(y_second, 'tensor', XNEXT)  23.6 us
    pallas_call x4, Pallas kernels, block_move(): pl.pallas_call(body, out_shape=jax.ShapeDtypeStruct(rows.shape, rows.dtyp...  23.4 us
  transfers between devices with their start and end apart: 134, of which 49 were waited for; matrix products, arithmetic and copies ran while one was open for 45% of the time, Pallas kernels for 3%

profile of v2, /device:TPU:8, one launch (start us, length us, event | category | flops | bytes accessed | tf_op | source)
XLA Modules:
  0.0 809.0 jit_solution(6097849867933311948)
XLA Ops:
  18.7 5.9 shard_map.273
  39.3 5.9 shard_map.274
  242.8 8.0 collective-permute-done.45
  266.6 8.0 collective-permute-done.49
  289.1 11.6 %collective-permute-done.56 = bf16[128,2048]{1,0:T(8,128)(2,1)S(1)} collective-permute-done((bf16[128,2048]{1,0:T(8,128)(2,1)S(1)}, bf16[128,2048]{1,0:T(8,128)(2,1)S(1)}, u32[]{:S(2)}, u32[]{:S(2)}) %collective-permute-start.56) | collective-permute-done | bytes 524320 | tf_op jit(solution)/shard_map/ppermute | solution.py:282
  334.2 6.6 fusion.20
  348.4 11.1 %collective-permute-done.68 = bf16[256,1536]{0,1:T(8,128)(2,1)S(1)} collective-permute-done((bf16[256,1536]{0,1:T(8,128)(2,1)}, bf16[256,1536]{0,1:T(8,128)(2,1)S(1)}, u32[]{:S(2)}, u32[]{:S(2)}) %collective-permute-start.68) | collective-permute-done | bytes 786464 | tf_op jit(solution)/shard_map/ppermute | solution.py:82
  370.6 7.0 fusion.18
  384.0 6.4 fusion.12
  390.4 14.2 %collective-permute-done.73 = bf16[256,1536]{0,1:T(8,128)(2,1)S(1)} collective-permute-done((bf16[256,1536]{0,1:T(8,128)(2,1)S(1)}, bf16[256,1536]{0,1:T(8,128)(2,1)S(1)}, u32[]{:S(2)}, u32[]{:S(2)}) %collective-permute-start.73) | collective-permute-done | bytes 786464 | tf_op jit(solution)/shard_map/ppermute | solution.py:82
  415.3 7.2 fusion.14
  438.6 9.0 %collective-permute-done.78 = bf16[256,1536]{0,1:T(8,128)(2,1)S(1)} collective-permute-done((bf16[256,1536]{0,1:T(8,128)(2,1)S(1)}, bf16[256,1536]{0,1:T(8,128)(2,1)S(1)}, u32[]{:S(2)}, u32[]{:S(2)}) %collective-permute-start.78) | collective-permute-done | bytes 786464 | tf_op jit(solution)/shard_map/ppermute | solution.py:82
  451.8 9.6 %add_convert_fusion.1 = bf16[1024,2048]{1,0:T(8,128)(2,1)S(1)} fusion(f32[1024,2048]{1,0:T(8,128)} %fusion.18, f32[1024,2048]{1,0:T(8,128)} %fusion.14, bf16[1024,1024]{1,0:T(8,128)(2,1)S(1)} %pad_maximum_fusion.6, bf16[2048,1536]{0,1:T(8,128)(2,1)} %constant_dynamic-update-slice_fusion.37), kind=kOutput, calls=%fused_computation.14 | convolution fusion | flops 4301258752 | bytes 27262976 | tf_op jit(solution)/shard_map/dot_general | solution.py:37
  471.1 7.3 fusion.58
  488.3 8.8 %add_convert_fusion = bf16[1024,2048]{1,0:T(8,128)(2,1)} fusion(f32[1024,2048]{1,0:T(8,128)S(1)} %fusion.62, f32[1024,2048]{1,0:T(8,128)} %fusion.58, bf16[1024,512]{1,0:T(8,128)(2,1)S(1)} %copy-done.81, bf16[2048,1536]{0,1:T(8,128)(2,1)} %constant_dynamic-update-slice_fusion.37), kind=kOutput, calls=%fused_computation.13 | convolution fusion | flops 2153775104 | bytes 24117248 | tf_op jit(solution)/shard_map/dot_general | solution.py:37
  499.2 8.5 %collective-permute-done.85 = bf16[256,1536]{0,1:T(8,128)(2,1)S(1)} collective-permute-done((bf16[256,1536]{0,1:T(8,128)(2,1)S(1)}, bf16[256,1536]{0,1:T(8,128)(2,1)S(1)}, u32[]{:S(2)}, u32[]{:S(2)}) %collective-permute-start.85) | collective-permute-done | bytes 786464 | tf_op jit(solution)/shard_map/ppermute | solution.py:82
  519.8 6.1 collective-permute-done.87
  568.8 6.5 collective-permute-done.97
  593.8 8.1 collective-permute-done.102
  612.8 7.3 convolution_bitcast_fusion.1
  620.1 14.7 %fusion.7 = bf16[2,2,2,512,512]{3,4,2,1,0:T(8,128)(2,1)} fusion(f32[2,2,2,512]{3,2,1,0:T(2,128)S(1)} %copy-done.142, f32[2,2,512,512,2]{3,2,4,1,0:T(8,128)} %copy-done.6, pred[2,512,512]{1,2,0:T(8,128)(4,1)} %copy-done.38, bf16[2,512,2,2,128]{1,4,3,2,0:T(8,128)(2,1)} %copy.299, bf16[2,512,2,128,1]{3,2,1,0,4:T(2,128)(2,1)} %bitcast.292), kind=kOutput, calls=%fused_computation.11 | convolution fusion | flops 1098912256 | bytes 14696448 | tf_op jit(solution)/shard_map/sub | solution.py:475
  746.3 9.2 %collective-permute-done.130 = f32[4352]{0:T(1024)S(1)} collective-permute-done((f32[4352]{0:T(1024)S(1)}, f32[4352]{0:T(1024)S(1)}, u32[]{:S(2)}, u32[]{:S(2)}) %collective-permute-start.130) | collective-permute-done | bytes 17440 | tf_op jit(solution)/shard_map/ppermute | solution.py:244
  793.6 5.9 shard_map.276
  799.4 5.9 shard_map.275
  (852 shorter events, 605.9 us)
Async XLA Ops:
  5.8 41.8 %collective-permute-start.13 = (bf16[256,1024]{1,0:T(8,128)(2,1)}, bf16[256,1024]{1,0:T(8,128)(2,1)}, u32[]{:S(2)}, u32[]{:S(2)}) collective-permute-start(bf16[256,1024]{1,0:T(8,128)(2,1)} %get-tuple-element.526), channel_id=1, source_target_pairs={{0,4},{4,0},{8,12},{12,8},{16,20},{20,16},{24,28},{28,24},{1,5},{5... | collective-permute-start | bytes 1572872 | tf_op jit(solution)/shard_map/ppermute | solution.py:82
  5.8 43.4 %collective-permute-start.12 = (bf16[256,1024]{1,0:T(8,128)(2,1)}, bf16[256,1024]{1,0:T(8,128)(2,1)}, u32[]{:S(2)}, u32[]{:S(2)}) collective-permute-start(bf16[256,1024]{1,0:T(8,128)(2,1)} %get-tuple-element.526), channel_id=1, source_target_pairs={{8,16},{12,20},{16,8},{20,12},{9,17},{13,21},{17,9},{21,13},{10,18... | collective-permute-start | bytes 1572872 | tf_op jit(solution)/shard_map/ppermute | solution.py:82
  9.3 41.6 %collective-permute-start.11 = (bf16[256,1024]{1,0:T(8,128)(2,1)}, bf16[256,1024]{1,0:T(8,128)(2,1)}, u32[]{:S(2)}, u32[]{:S(2)}) collective-permute-start(bf16[256,1024]{1,0:T(8,128)(2,1)} %get-tuple-element.526), channel_id=1, source_target_pairs={{0,8},{4,12},{8,0},{12,4},{16,24},{20,28},{24,16},{28,20},{1,9},{5... | collective-permute-start | bytes 1572872 | tf_op jit(solution)/shard_map/ppermute | solution.py:82
  12.2 38.8 %collective-permute-start.19 = (bf16[256,512]{0,1:T(8,128)(2,1)}, bf16[256,512]{0,1:T(8,128)(2,1)}, u32[]{:S(2)}, u32[]{:S(2)}) collective-permute-start(bf16[256,512]{0,1:T(8,128)(2,1)} %bitcast.293), channel_id=1, source_target_pairs={{0,4},{4,0},{8,12},{12,8},{16,20},{20,16},{24,28},{28,24},{1,5},{5... | collective-permute-start | bytes 786440 | tf_op jit(solution)/shard_map/ppermute | solution.py:82
  77.0 31.9 %collective-permute-start.24 = (bf16[256,512]{0,1:T(8,128)(2,1)}, bf16[256,512]{0,1:T(8,128)(2,1)S(1)}, u32[]{:S(2)}, u32[]{:S(2)}) collective-permute-start(bf16[256,512]{0,1:T(8,128)(2,1)} %copy-done.115), channel_id=1, source_target_pairs={{0,4},{4,0},{8,12},{12,8},{16,20},{20,16},{24,28},{28,24},{1,5},{5... | collective-permute-start | bytes 786440 | tf_op jit(solution)/shard_map/ppermute | solution.py:82
  77.0 34.4 %collective-permute-start.22 = (bf16[256,512]{0,1:T(8,128)(2,1)}, bf16[256,512]{0,1:T(8,128)(2,1)S(1)}, u32[]{:S(2)}, u32[]{:S(2)}) collective-permute-start(bf16[256,512]{0,1:T(8,128)(2,1)} %copy-done.115), channel_id=1, source_target_pairs={{8,16},{12,20},{16,8},{20,12},{9,17},{13,21},{17,9},{21,13},{10,18... | collective-permute-start | bytes 786440 | tf_op jit(solution)/shard_map/ppermute | solution.py:82
  138.5 68.6 %collective-permute-start.66 = (bf16[128,2048]{1,0:T(8,128)(2,1)}, bf16[128,2048]{1,0:T(8,128)(2,1)}, u32[]{:S(2)}, u32[]{:S(2)}) collective-permute-start(bf16[128,2048]{1,0:T(8,128)(2,1)} %get-tuple-element.504), channel_id=1, source_target_pairs={{0,1},{1,0},{2,3},{3,2},{4,5},{5,4},{6,7},{7,6},{8,9},{9,8},{10,11... | collective-permute-start | bytes 1572872 | tf_op jit(solution)/shard_map/ppermute | solution.py:278
  144.4 35.6 %collective-permute-start.33 = (bf16[256,1536]{0,1:T(8,128)(2,1)}, bf16[256,1536]{0,1:T(8,128)(2,1)}, u32[]{:S(2)}, u32[]{:S(2)}) collective-permute-start(bf16[256,1536]{0,1:T(8,128)(2,1)} %collective-permute-done.28), channel_id=1, source_target_pairs={{0,4},{4,0},{8,12},{12,8},{16,20},{20,16},{24,28},{28,24},{1,5},{5... | collective-permute-start | bytes 2359304 | tf_op jit(solution)/shard_map/ppermute | solution.py:82
  144.5 35.5 %collective-permute-start.31 = (bf16[256,1536]{0,1:T(8,128)(2,1)}, bf16[256,1536]{0,1:T(8,128)(2,1)}, u32[]{:S(2)}, u32[]{:S(2)}) collective-permute-start(bf16[256,1536]{0,1:T(8,128)(2,1)} %collective-permute-done.28), channel_id=1, source_target_pairs={{8,16},{12,20},{16,8},{20,12},{9,17},{13,21},{17,9},{21,13},{10,18... | collective-permute-start | bytes 2359304 | tf_op jit(solution)/shard_map/ppermute | solution.py:82
  177.7 29.4 %collective-permute-start.67 = (bf16[128,2048]{1,0:T(8,128)(2,1)}, bf16[128,2048]{1,0:T(8,128)(2,1)}, u32[]{:S(2)}, u32[]{:S(2)}) collective-permute-start(bf16[128,2048]{1,0:T(8,128)(2,1)} %copy-done.108), channel_id=1, source_target_pairs={{0,1},{1,0},{2,3},{3,2},{4,5},{5,4},{6,7},{7,6},{8,9},{9,8},{10,11... | collective-permute-start | bytes 1572872 | tf_op jit(solution)/shard_map/ppermute | solution.py:282
  300.8 40.1 %collective-permute-start.63 = (bf16[256,1536]{0,1:T(8,128)(2,1)}, bf16[256,1536]{0,1:T(8,128)(2,1)}, u32[]{:S(2)}, u32[]{:S(2)}) collective-permute-start(bf16[256,1536]{0,1:T(8,128)(2,1)} %collective-permute-done.57), channel_id=1, source_target_pairs={{0,4},{4,0},{8,12},{12,8},{16,20},{20,16},{24,28},{28,24},{1,5},{5... | collective-permute-start | bytes 2359304 | tf_op jit(solution)/shard_map/ppermute | solution.py:82
  301.4 39.5 %collective-permute-start.61 = (bf16[256,1536]{0,1:T(8,128)(2,1)}, bf16[256,1536]{0,1:T(8,128)(2,1)}, u32[]{:S(2)}, u32[]{:S(2)}) collective-permute-start(bf16[256,1536]{0,1:T(8,128)(2,1)} %collective-permute-done.57), channel_id=1, source_target_pairs={{8,16},{12,20},{16,8},{20,12},{9,17},{13,21},{17,9},{21,13},{10,18... | collective-permute-start | bytes 2359304 | tf_op jit(solution)/shard_map/ppermute | solution.py:82
  303.7 37.1 %collective-permute-start.62 = (bf16[256,1536]{0,1:T(8,128)(2,1)}, bf16[256,1536]{0,1:T(8,128)(2,1)}, u32[]{:S(2)}, u32[]{:S(2)}) collective-permute-start(bf16[256,1536]{0,1:T(8,128)(2,1)} %collective-permute-done.58), channel_id=1, source_target_pairs={{8,0},{12,4},{16,24},{20,28},{9,1},{13,5},{17,25},{21,29},{10,2},{... | collective-permute-start | bytes 2359304 | tf_op jit(solution)/shard_map/ppermute | solution.py:82
  411.0 26.3 %collective-permute-start.84 = (bf16[1024,512]{0,1:T(8,128)(2,1)S(1)}, bf16[1024,512]{0,1:T(8,128)(2,1)S(1)}, u32[]{:S(2)}, u32[]{:S(2)}) collective-permute-start(bf16[1024,512]{0,1:T(8,128)(2,1)S(1)} %fusion.89), channel_id=1, source_target_pairs={{0,4},{4,0},{8,12},{12,8},{16,20},{20,16},{24,28},{28,24},{1,5},{5... | collective-permute-start | bytes 3145736 | tf_op jit(solution)/shard_map/ppermute | solution.py:263
  414.8 67.5 %collective-permute-start.83 = (bf16[1024,1024]{0,1:T(8,128)(2,1)}, bf16[1024,1024]{0,1:T(8,128)(2,1)}, u32[]{:S(2)}, u32[]{:S(2)}) collective-permute-start(bf16[1024,1024]{0,1:T(8,128)(2,1)} %convolution_convert_fusion.2), channel_id=1, source_target_pairs={{0,4},{4,0},{8,12},{12,8},{16,20},{20,16},{24,28},{28,24},{1,5},{5... | collective-permute-start | bytes 6291464 | tf_op jit(solution)/shard_map/ppermute | solution.py:263
  451.8 62.7 %collective-permute-start.99 = (bf16[1024,512]{0,1:T(8,128)(2,1)}, bf16[1024,512]{0,1:T(8,128)(2,1)}, u32[]{:S(2)}, u32[]{:S(2)}) collective-permute-start(bf16[1024,512]{0,1:T(8,128)(2,1)} %fusion.92), channel_id=1, source_target_pairs={{0,4},{4,0},{8,12},{12,8},{16,20},{20,16},{24,28},{28,24},{1,5},{5... | collective-permute-start | bytes 3145736 | tf_op jit(solution)/shard_map/ppermute | solution.py:263
  464.1 33.5 %collective-permute-start.82 = (bf16[128,2048]{1,0:T(8,128)(2,1)}, bf16[128,2048]{1,0:T(8,128)(2,1)}, u32[]{:S(2)}, u32[]{:S(2)}) collective-permute-start(bf16[128,2048]{1,0:T(8,128)(2,1)} %get-tuple-element.449), channel_id=1, source_target_pairs={{0,2},{1,3},{2,0},{3,1},{4,6},{5,7},{6,4},{7,5},{8,10},{9,11},{10,... | collective-permute-start | bytes 1572872 | tf_op jit(solution)/shard_map/ppermute | solution.py:294
  465.3 33.9 %collective-permute-start.81 = (bf16[128,2048]{1,0:T(8,128)(2,1)}, bf16[128,2048]{1,0:T(8,128)(2,1)}, u32[]{:S(2)}, u32[]{:S(2)}) collective-permute-start(bf16[128,2048]{1,0:T(8,128)(2,1)} %get-tuple-element.450), channel_id=1, source_target_pairs={{0,1},{1,0},{2,3},{3,2},{4,5},{5,4},{6,7},{7,6},{8,9},{9,8},{10,11... | collective-permute-start | bytes 1572872 | tf_op jit(solution)/shard_map/ppermute | solution.py:293
  466.0 47.5 %collective-permute-start.80 = (bf16[128,2048]{1,0:T(8,128)(2,1)}, bf16[128,2048]{1,0:T(8,128)(2,1)}, u32[]{:S(2)}, u32[]{:S(2)}) collective-permute-start(bf16[128,2048]{1,0:T(8,128)(2,1)} %get-tuple-element.451), channel_id=1, source_target_pairs={{0,2},{1,3},{2,0},{3,1},{4,6},{5,7},{6,4},{7,5},{8,10},{9,11},{10,... | collective-permute-start | bytes 1572872 | tf_op jit(solution)/shard_map/ppermute | solution.py:296
  582.5 62.6 %collective-permute-start.111 = (bf16[1024,512]{1,0:T(8,128)(2,1)}, bf16[1024,512]{1,0:T(8,128)(2,1)}, u32[]{:S(2)}, u32[]{:S(2)}) collective-permute-start(bf16[1024,512]{1,0:T(8,128)(2,1)} %fusion.95), channel_id=1, source_target_pairs={{0,4},{4,0},{8,12},{12,8},{16,20},{20,16},{24,28},{28,24},{1,5},{5... | collective-permute-start | bytes 3145736 | tf_op jit(solution)/shard_map/ppermute | solution.py:263
  601.9 42.1 %collective-permute-start.106 = (bf16[128,2048]{1,0:T(8,128)(2,1)}, bf16[128,2048]{1,0:T(8,128)(2,1)}, u32[]{:S(2)}, u32[]{:S(2)}) collective-permute-start(bf16[128,2048]{1,0:T(8,128)(2,1)} %get-tuple-element.441), channel_id=1, source_target_pairs={{0,2},{1,3},{2,0},{3,1},{4,6},{5,7},{6,4},{7,5},{8,10},{9,11},{10,... | collective-permute-start | bytes 1572872 | tf_op jit(solution)/shard_map/ppermute | solution.py:296
  603.1 47.1 %collective-permute-start.105 = (bf16[128,2048]{1,0:T(8,128)(2,1)}, bf16[128,2048]{1,0:T(8,128)(2,1)}, u32[]{:S(2)}, u32[]{:S(2)}) collective-permute-start(bf16[128,2048]{1,0:T(8,128)(2,1)} %get-tuple-element.442), channel_id=1, source_target_pairs={{0,1},{1,0},{2,3},{3,2},{4,5},{5,4},{6,7},{7,6},{8,9},{9,8},{10,11... | collective-permute-start | bytes 1572872 | tf_op jit(solution)/shard_map/ppermute | solution.py:295
  650.2 54.5 %collective-permute-start.113 = (bf16[256,512]{1,0:T(8,128)(2,1)}, bf16[256,512]{1,0:T(8,128)(2,1)}, u32[]{:S(2)}, u32[]{:S(2)}) collective-permute-start(bf16[256,512]{1,0:T(8,128)(2,1)} %get-tuple-element.496), channel_id=1, source_target_pairs={{0,8},{4,12},{24,16},{28,20},{1,9},{5,13},{25,17},{29,21},{2,10},{... | collective-permute-start | bytes 786440 | tf_op jit(solution)/shard_map/ppermute | solution.py:82
  670.6 34.1 %collective-permute-start.114 = (bf16[256,512]{1,0:T(8,128)(2,1)}, bf16[256,512]{1,0:T(8,128)(2,1)}, u32[]{:S(2)}, u32[]{:S(2)}) collective-permute-start(bf16[256,512]{1,0:T(8,128)(2,1)} %add_convert_fusion.33), channel_id=1, source_target_pairs={{8,16},{12,20},{16,8},{20,12},{9,17},{13,21},{17,9},{21,13},{10,18... | collective-permute-start | bytes 786440 | tf_op jit(solution)/shard_map/ppermute | solution.py:82
  (274 other events, 3881.8 us)

commit v3 on v2

--- a/solution.py
+++ b/solution.py
@@ -1,3 +1,4 @@
+import functools
 import math
 
 import jax
@@ -47,21 +48,295 @@
     size = width // blocks
 
     def body(table_ref, in_ref, out_ref):
-        out_ref[...] = in_ref[...]
+        for i in range(blocks):
+            start = pl.multiple_of(table_ref[i] * size, size)
+            out_ref[:, :, i * size : (i + 1) * size] = in_ref[:, :, pl.ds(start, size)]
 
     return pl.pallas_call(
         body,
         out_shape=jax.ShapeDtypeStruct(rows.shape, rows.dtype),
         grid_spec=pltpu.PrefetchScalarGridSpec(
             num_scalar_prefetch=1,
-            grid=(blocks,),
-            in_specs=[pl.BlockSpec((micro, count, size), lambda i, ref: (0, 0, ref[i]))],
-            out_specs=pl.BlockSpec((micro, count, size), lambda i, ref: (0, 0, i)),
+            grid=(micro,),
+            in_specs=[pl.BlockSpec((1, count, width), lambda i, ref: (i, 0, 0))],
+            out_specs=pl.BlockSpec((1, count, width), lambda i, ref: (i, 0, 0)),
         ),
         cost_estimate=pl.CostEstimate(
             flops=0, bytes_accessed=4 * micro * count * width, transcendentals=0
         ),
     )(table, rows)
+
+
+def turn(rows, cosine, sine):
+    return rows * cosine + pltpu.roll(rows, HEAD_SIZE // 2, 1) * sine
+
+
+def allowed_bias(col_ref, row_ref):
+    segment, row_id, valid = row_ref[0, 0:1, :], row_ref[0, 1:2, :], row_ref[0, 2:3, :]
+    segment_col, row_id_col = col_ref[:, 0:1], col_ref[:, 1:2]
+    allowed = (
+        (segment_col == segment)
+        & (row_id <= row_id_col)
+        & ((valid > 0) | (row_id == row_id_col))
+    )
+    return jnp.where(allowed, 0.0, -1e30)
+
+
+def head(index):
+    return slice(index * HEAD_SIZE, (index + 1) * HEAD_SIZE)
+
+
+def softmax_rows(query, key, bias):
+    scores = dot_nt(query, key) * (1.0 / math.sqrt(HEAD_SIZE)) + bias
+    shifted = jnp.exp(scores - jnp.max(scores, axis=-1, keepdims=True))
+    return shifted * (1.0 / jnp.sum(shifted, axis=-1, keepdims=True))
+
+
+def attention_forward(
+    heads_q, heads_kv, qkv_ref, cos_ref, sin_ref, col_ref, row_ref, gain_q_ref, gain_k_ref, out_ref
+):
+    cosine, sine = cos_ref[...], sin_ref[...]
+    bias = allowed_bias(col_ref, row_ref)
+    valid = col_ref[:, 2:3].astype(F32)
+    groups = heads_q // heads_kv
+    for kv in range(heads_kv):
+        k_unit, _ = unit_of(qkv_ref[:, head(heads_q + kv)])
+        key = turn(k_unit * gain_k_ref[...], cosine, sine).astype(BF16)
+        value = qkv_ref[:, head(heads_q + heads_kv + kv)].astype(BF16)
+        for h in range(kv * groups, (kv + 1) * groups):
+            q_unit, _ = unit_of(qkv_ref[:, head(h)])
+            query = turn(q_unit * gain_q_ref[...], cosine, sine).astype(BF16)
+            probs = softmax_rows(query, key, bias).astype(BF16)
+            out_ref[:, head(h)] = (dot_nn(probs, value) * valid).astype(BF16)
+
+
+def attention_backward(
+    heads_q,
+    heads_kv,
+    qkv_ref,
+    grad_ref,
+    cos_ref,
+    sin_ref,
+    col_ref,
+    row_ref,
+    gain_q_ref,
+    gain_k_ref,
+    out_ref,
+    sums_ref,
+):
+    cosine, sine = cos_ref[...], sin_ref[...]
+    bias = allowed_bias(col_ref, row_ref)
+    valid = col_ref[:, 2:3].astype(BF16)
+    groups = heads_q // heads_kv
+    scale = 1.0 / math.sqrt(HEAD_SIZE)
+    gain_q, gain_k = gain_q_ref[...], gain_k_ref[...]
+    sum_q = sum_k = jnp.zeros((1, HEAD_SIZE), F32)
+    for kv in range(heads_kv):
+        k_unit, k_recip = unit_of(qkv_ref[:, head(heads_q + kv)])
+        key = turn(k_unit * gain_k, cosine, sine).astype(BF16)
+        value = qkv_ref[:, head(heads_q + heads_kv + kv)].astype(BF16)
+        d_key = d_value = None
+        for h in range(kv * groups, (kv + 1) * groups):
+            q_unit, q_recip = unit_of(qkv_ref[:, head(h)])
+            query = turn(q_unit * gain_q, cosine, sine).astype(BF16)
+            probs = softmax_rows(query, key, bias)
+            d_mixed = grad_ref[:, head(h)] * valid
+            d_probs = dot_nt(d_mixed, value)
+            delta = jnp.sum(probs * d_probs, axis=-1, keepdims=True)
+            d_scores = (probs * (d_probs - delta)).astype(BF16)
+            d_query = turn(scale * dot_nn(d_scores, key), cosine, -sine)
+            sum_q = sum_q + jnp.sum(d_query * q_unit, axis=0, keepdims=True)
+            out_ref[:, head(h)] = norm_back(d_query, q_unit, q_recip, gain_q).astype(BF16)
+            part_key, part_value = dot_tn(d_scores, query), dot_tn(probs.astype(BF16), d_mixed)
+            d_key = part_key if d_key is None else d_key + part_key
+            d_value = part_value if d_value is None else d_value + part_value
+        d_key = turn(scale * d_key, cosine, -sine)
+        sum_k = sum_k + jnp.sum(d_key * k_unit, axis=0, keepdims=True)
+        out_ref[:, head(heads_q + kv)] = norm_back(d_key, k_unit, k_recip, gain_k).astype(BF16)
+        out_ref[:, head(heads_q + heads_kv + kv)] = d_value.astype(BF16)
+    sums_ref[0, 0:1, :] = sum_q
+    sums_ref[0, 1:2, :] = sum_k
+
+
+def attention_call(body, micro, heads_q, heads_kv, wide, tables, out_shape, out_specs, passes):
+    seq_len = wide[0].shape[0] // micro
+
+    def rows_of(array):
+        return pl.BlockSpec((seq_len, array.shape[1]), lambda i: (i, 0))
+
+    def whole(array):
+        return pl.BlockSpec(array.shape, lambda i: (0, 0))
+
+    cosine, sine, col, row, gain_q, gain_k = tables
+    return pl.pallas_call(
+        functools.partial(body, heads_q, heads_kv),
+        out_shape=out_shape,
+        grid=(micro,),
+        in_specs=[rows_of(array) for array in (*wide, cosine, sine, col)]
+        + [
+            pl.BlockSpec((1,) + row.shape[1:], lambda i: (i, 0, 0)),
+            whole(gain_q),
+            whole(gain_k),
+        ],
+        out_specs=out_specs,
+        cost_estimate=pl.CostEstimate(
+            flops=2 * passes * micro * heads_q * seq_len * seq_len * HEAD_SIZE,
+            bytes_accessed=sum(array.size * array.dtype.itemsize for array in wide) * 2,
+            transcendentals=micro * heads_q * seq_len * seq_len,
+        ),
+    )(*wide, *tables)
+
+
+class ZLane:
+    def __init__(self, me, own, out, send_sems, recv_sems):
+        self.me, self.own, self.out = me, own, out
+        self.send_sems, self.recv_sems = send_sems, recv_sems
+
+    def copy(self, index, source, slot, device):
+        return pltpu.make_async_remote_copy(
+            src_ref=source,
+            dst_ref=self.out.at[slot],
+            send_sem=self.send_sems.at[index],
+            recv_sem=self.recv_sems.at[slot],
+            device_id={"dp": device},
+            device_id_type=pl.DeviceIdType.MESH,
+        )
+
+    def parts(self, slot):
+        return self.own if slot == 0 else self.out.at[slot]
+
+    def along(self, slot):
+        index, to_slot, bits = {0: (1, 3, 6), 1: (2, 2, 6), 3: (3, 2, 2), 2: (4, 3, 2)}[slot]
+        return self.copy(index, self.parts(slot), to_slot, self.me ^ bits)
+
+    def across(self, slot):
+        return self.copy(5 + slot, self.parts(slot), 4 + slot, self.me ^ 1)
+
+    def pair(self):
+        return self.copy(0, self.own, 1, self.me ^ 2)
+
+    def arrived(self, slot):
+        self.copy(0, self.own, slot, self.me ^ 2).wait_recv()
+
+    def begin(self, inner):
+        self.pair().start()
+
+        @pl.when(inner)
+        def _():
+            self.along(0).start()
+
+        self.across(0).start()
+
+    def middle(self, inner):
+        self.arrived(1)
+
+        @pl.when(inner)
+        def _():
+            self.along(1).start()
+            self.arrived(3)
+            self.along(3).start()
+            self.across(3).start()
+
+        self.across(1).start()
+
+    def last(self, inner):
+        self.arrived(2)
+
+        @pl.when(inner)
+        def _():
+            self.along(2).start()
+
+        self.across(2).start()
+
+        @pl.when(jnp.logical_not(inner))
+        def _():
+            self.arrived(3)
+            self.across(3).start()
+
+    def end(self, inner):
+        self.pair().wait_send()
+        for slot in range(4):
+            self.across(slot).wait_send()
+            self.arrived(4 + slot)
+
+        @pl.when(inner)
+        def _():
+            for slot in range(4):
+                self.along(slot).wait_send()
+
+
+def first_gathers(
+    x_ref, qkv_ref, out_ref, gain_ref, x_all, qkv_all, out_all, gain_all, local_sems, *sems
+):
+    me, own = lax.axis_index("dp"), lax.axis_index("tensor")
+    z = me // 2
+    inner = (z == 1) | (z == 2)
+    barrier = pltpu.get_barrier_semaphore()
+    peers = [{"dp": me ^ bits} for bits in (1, 2, 6)]
+    peers += [{"tensor": own ^ bit} for bit in (1, 2)]
+    for device in peers:
+        pl.semaphore_signal(barrier, device_id=device, device_id_type=pl.DeviceIdType.MESH)
+    pl.semaphore_wait(barrier, len(peers))
+
+    x_send, x_recv, qkv_send, qkv_recv, out_send, out_recv, gain_send, gain_recv = sems
+    local = [
+        pltpu.make_async_copy(source, target, local_sems.at[i])
+        for i, (source, target) in enumerate(
+            (
+                (x_ref.at[0], x_all.at[0, 0]),
+                (x_ref.at[1], x_all.at[1, 0]),
+                (qkv_ref, qkv_all.at[0]),
+                (out_ref, out_all.at[0]),
+                (gain_ref, gain_all.at[0]),
+            )
+        )
+    ]
+
+    def plane(index, source, part, slot, bit):
+        return pltpu.make_async_remote_copy(
+            src_ref=source,
+            dst_ref=x_all.at[part, slot],
+            send_sem=x_send.at[index],
+            recv_sem=x_recv.at[index],
+            device_id={"tensor": own ^ bit},
+            device_id_type=pl.DeviceIdType.MESH,
+        )
+
+    qkv_lane = ZLane(me, qkv_ref, qkv_all, qkv_send, qkv_recv)
+    out_lane = ZLane(me, out_ref, out_all, out_send, out_recv)
+    gain_lane = ZLane(me, gain_ref, gain_all, gain_send, gain_recv)
+    x_first = plane(0, x_ref.at[0], 0, 1, 1)
+    y_second = plane(1, x_ref.at[1], 1, 2, 2)
+    x_second = plane(2, x_ref.at[1], 1, 1, 1)
+    y_first = plane(3, x_ref.at[0], 0, 2, 2)
+    d_first = plane(4, x_all.at[0, 1], 0, 3, 2)
+    d_second = plane(5, x_all.at[1, 2], 1, 3, 1)
+    gain_lane.begin(inner)
+    qkv_lane.begin(inner)
+    for copy in (x_first, y_second, x_second, y_first):
+        copy.start()
+    for copy in local:
+        copy.start()
+    gain_lane.middle(inner)
+    gain_lane.last(inner)
+    x_first.wait_recv()
+    d_first.start()
+    y_second.wait_recv()
+    d_second.start()
+    qkv_lane.middle(inner)
+    out_lane.begin(inner)
+    qkv_lane.last(inner)
+    out_lane.middle(inner)
+    out_lane.last(inner)
+    for copy in (x_second, y_first, d_first, d_second):
+        copy.wait_recv()
+    for copy in (x_first, y_second, x_second, y_first, d_first, d_second):
+        copy.wait_send()
+    for copy in local:
+        copy.wait()
+    gain_lane.end(inner)
+    qkv_lane.end(inner)
+    out_lane.end(inner)
 
 
 class Job:
@@ -153,7 +428,7 @@
     def free(self, gen):
         steps = gen if isinstance(gen, Steps) else Steps(gen)
         while steps.pending:
-            steps.feed(steps.pending)
+            steps.feed(lax.optimization_barrier(steps.pending))
         return steps.value
 
     def to_local(self, rows):
@@ -165,9 +440,6 @@
     def row_order(self, value):
         return value
 
-    def gather_gains(self, packed):
-        return lax.all_gather(packed, "dp", axis=0)
-
     def gains_local(self, blocks):
         return blocks.reshape(-1)
 
@@ -181,8 +453,12 @@
         return lax.psum(vector, ("dp", "tensor"))
 
     def gather_weights(self, buf):
-        return lax.all_gather(buf, "dp", axis=0, tiled=True)
+        return list(lax.all_gather(buf, "dp", axis=0))
         yield
+
+    def first_gathers(self, rows, *weights):
+        gathered = self.free(self.gather_rows(rows))
+        return gathered, *(lax.all_gather(array, "dp", axis=0) for array in weights)
 
     def scatter_grads(self, parts):
         full = jnp.concatenate([dot_tn(l, r).astype(BF16) for l, r in parts], axis=1)
@@ -220,12 +496,6 @@
             swap = (self.own & bit) != 0
             parts = [jnp.where(swap, parts[j ^ bit], parts[j]) for j in range(4)]
         return jnp.concatenate(parts, axis=-1)
-
-    def gather_gains(self, packed):
-        got = packed[None]
-        for perm in (PAIR, ACROSS, CORE):
-            got = jnp.concatenate([got, lax.ppermute(got, "dp", perm)], axis=0)
-        return got
 
     def gains_plain(self, blocks):
         return jnp.sum(jnp.where(self.hit[:, :, None], blocks[None], 0), axis=1).reshape(-1)
@@ -251,9 +521,25 @@
         out_pair, other_two = yield [(over_pair, OUTWARD), (two, CORE)]
         three = jnp.where(self.inner, over_own, out_pair)
         other_three = lax.ppermute(three, "dp", CORE)
-        return jnp.concatenate(
-            [buf, pair, two, three, other, other_pair, other_two, other_three], axis=0
-        )
+        return [buf, pair, two, three, other, other_pair, other_two, other_three]
+
+    def first_gathers(self, rows, *weights):
+        micro, count, width = rows.shape
+        hbm = pl.BlockSpec(memory_space=pl.ANY)
+        lanes = len(weights)
+        return pl.pallas_call(
+            first_gathers,
+            out_shape=(
+                jax.ShapeDtypeStruct((micro, 4, count, width), rows.dtype),
+                *(jax.ShapeDtypeStruct((8,) + w.shape, w.dtype) for w in weights),
+            ),
+            in_specs=[hbm] * (1 + lanes),
+            out_specs=[hbm] * (1 + lanes),
+            scratch_shapes=[
+                pltpu.SemaphoreType.DMA((copies,)) for copies in (5, 6, 6, *(9, 8) * lanes)
+            ],
+            compiler_params=pltpu.CompilerParams(collective_id=0, has_side_effects=True),
+        )(rows, *weights)
 
     def scatter_grads(self, parts):
         away, half = [], parts[0][0].shape[1] // 2
@@ -272,41 +558,30 @@
         return own.astype(F32) + got_inner.astype(F32) + got_pair.astype(F32)
 
     def gather_rows(self, rows):
-        first, second = rows[0], rows[1]
-        x_first = lax.ppermute(first, "tensor", XNEXT)
-        y_second = lax.ppermute(second, "tensor", YNEXT)
-        x_second = lax.ppermute(second, "tensor", XNEXT)
-        y_first = lax.ppermute(first, "tensor", YNEXT)
-        x_first, y_second = yield (x_first, y_second)
-        d_first = lax.ppermute(x_first, "tensor", YNEXT)
-        d_second = lax.ppermute(y_second, "tensor", XNEXT)
-        x_second, y_first, d_first, d_second = yield (x_second, y_first, d_first, d_second)
+        near_x, near_y = yield (
+            lax.ppermute(rows, "tensor", XNEXT),
+            lax.ppermute(rows, "tensor", YNEXT),
+        )
+        diag_first, diag_second = yield (
+            lax.ppermute(near_x[0], "tensor", YNEXT),
+            lax.ppermute(near_y[1], "tensor", XNEXT),
+        )
+        return jnp.concatenate([rows, near_x, near_y, jnp.stack([diag_first, diag_second])], axis=1)
+
+    def scatter_rows(self, partial):
+        first, second = (jnp.split(partial[i], 4, axis=0) for i in range(2))
+        near_first, near_second = yield (
+            lax.ppermute(jnp.stack([first[1], first[3]]), "tensor", XNEXT),
+            lax.ppermute(jnp.stack([second[2], second[3]]), "tensor", YNEXT),
+        )
+        far_first, far_second = yield (
+            lax.ppermute(add_rounded(first[2], near_first[1]), "tensor", YNEXT),
+            lax.ppermute(add_rounded(second[1], near_second[1]), "tensor", XNEXT),
+        )
         return jnp.stack(
             [
-                jnp.concatenate([first, x_first, y_first, d_first], axis=0),
-                jnp.concatenate([second, x_second, y_second, d_second], axis=0),
-            ]
-        )
-
-    def scatter_rows(self, partial):
-        first, second = (jnp.split(partial[i], 4, axis=0) for i in range(2))
-        diag_first = lax.ppermute(first[3], "tensor", XNEXT)
-        diag_second = lax.ppermute(second[3], "tensor", YNEXT)
-        near_first = lax.ppermute(first[1], "tensor", XNEXT)
-        near_second = lax.ppermute(second[2], "tensor", YNEXT)
-        diag_first, diag_second = yield (diag_first, diag_second)
-        far_first = lax.ppermute(add_rounded(first[2], diag_first), "tensor", YNEXT)
-        far_second = lax.ppermute(add_rounded(second[1], diag_second), "tensor", XNEXT)
-        near_first, near_second, far_first, far_second = yield (
-            near_first,
-            near_second,
-            far_first,
-            far_second,
-        )
-        return jnp.stack(
-            [
-                first[0].astype(F32) + near_first.astype(F32) + far_first.astype(F32),
-                second[0].astype(F32) + near_second.astype(F32) + far_second.astype(F32),
+                first[0].astype(F32) + near_first[0].astype(F32) + far_first.astype(F32),
+                second[0].astype(F32) + near_second[0].astype(F32) + far_second.astype(F32),
             ]
         )
 
@@ -326,13 +601,8 @@
         jnp.arange(0, HEAD_SIZE, 2).astype(F32) * (-math.log(THETA) / HEAD_SIZE)
     )
     angles = offsets.astype(F32)[..., None] * freqs
-    return jnp.cos(angles)[..., None, :], jnp.sin(angles)[..., None, :]
-
-
-def rotate(rows, cosine, sine):
-    half = rows.shape[-1] // 2
-    low, high = rows[..., :half], rows[..., half:]
-    return jnp.concatenate([low * cosine - high * sine, high * cosine + low * sine], axis=-1)
+    cosine, sine = jnp.cos(angles), jnp.sin(angles)
+    return jnp.concatenate([cosine, cosine], -1), jnp.concatenate([-sine, sine], -1)
 
 
 def on_device(
@@ -355,7 +625,6 @@
     w_down,
 ):
     net = net()
-    scale = 1.0 / math.sqrt(HEAD_SIZE)
     micro, own_rows, width = hidden_in.shape
     seq_len = segment_ids.shape[1]
     rows = micro * seq_len
@@ -363,71 +632,65 @@
     head_share = query_norm_gain.shape[0]
     q_cols, kv_cols = w_query.shape[1], key_weight.shape[1]
     heads_q, heads_kv = q_cols // HEAD_SIZE, kv_cols // HEAD_SIZE
-    groups = heads_q // heads_kv
     units = w_gate.shape[1] // CHUNKS
 
     rounds = net.rounds
-    job_qkv = rounds.add(
-        net.gather_weights(jnp.concatenate([w_query, key_weight, value_weight], axis=1)), 2
-    )
-    job_out = rounds.add(net.gather_weights(w_out.T), 3)
+    x_own = net.to_local(hidden_in)
+    packed = jnp.concatenate([attn_gain, ffn_gain, query_norm_gain, key_gain], axis=0)
+    pad = -packed.shape[0] % 2048
+    packed = jnp.pad(packed, (0, pad)).reshape(-1, 128)
+    x_all, w_qkv, w_out_t, gains = net.first_gathers(
+        x_own, jnp.concatenate([w_query, key_weight, value_weight], axis=1), w_out.T, packed
+    )
+    w_qkv = w_qkv.reshape(width, -1)
+    w_out_t = w_out_t.reshape(width, -1)
+    gains = gains.reshape(gains.shape[0], -1).astype(F32)
+    x_bf = x_all.reshape(rows, width)
+    later = (segment_ids, positions, pad_mask, cotangent, w_gate, w_up, w_down)
+    x_bf, *later = lax.optimization_barrier((x_bf, *later))
+    segment_ids, positions, pad_mask, cotangent, *ffn_weights = later
     ffn_jobs = []
-    for chunk in range(CHUNKS):
+
+    def gather_chunk(chunk, w_gate, w_up, w_down):
         cut = slice(chunk * units, (chunk + 1) * units)
         buf = jnp.concatenate([w_gate[:, cut], w_up[:, cut], w_down[cut, :].T], axis=1)
         ffn_jobs.append(rounds.add(net.gather_weights(buf), 4))
-    for _ in range(3):
-        rounds.pump()
-    x_own = net.to_local(hidden_in)
-    x_bf = net.free(net.gather_rows(x_own)).reshape(rows, width)
+
+    gather_chunk(0, *ffn_weights)
+    (x_bf,) = rounds.pump(x_bf)
     g_own, x_bf = lax.optimization_barrier((net.to_local(cotangent), x_bf))
     g_steps = Steps(net.gather_rows(g_own))
-    packed = jnp.concatenate(
-        [attn_gain, ffn_gain, query_norm_gain, key_gain], axis=0
-    )
-    gains = net.gather_gains(packed).astype(F32)
     gain_one = net.gains_local(gains[:, :share])
     gain_two = net.gains_local(gains[:, share : 2 * share])
     gain_q = net.gains_plain(gains[:, 2 * share : 2 * share + head_share])
-    gain_k = net.gains_plain(gains[:, 2 * share + head_share :])
+    gain_k = net.gains_plain(gains[:, 2 * share + head_share : 2 * (share + head_share)])
 
     segment = net.row_order(segment_ids)
     offsets = net.row_order(positions)
     valid = net.row_order(pad_mask)
     row_ids = net.row_order(jnp.arange(seq_len, dtype=jnp.int32))
-    cosine, sine = rotary(offsets)
-    valid_col = valid.reshape(rows, 1).astype(F32)
+    cosine, sine = rotary(offsets.reshape(rows))
+    ids = jnp.stack([segment, jnp.broadcast_to(row_ids, segment.shape), valid], axis=1)
+    ids_col = jnp.stack([ids[:, i].reshape(rows) for i in range(3)], axis=1)
+    tables = (cosine, sine, ids_col, ids, gain_q.reshape(1, -1), gain_k.reshape(1, -1))
     unit_all, _ = unit_of(x_bf.astype(F32))
-    (a1,) = net.mix(g_steps, (unit_all * gain_one).astype(BF16))
-    w_qkv = job_qkv.value
-    (qkv,) = rounds.pump(dot_nn(a1, w_qkv))
-    q_raw = qkv[:, :q_cols].reshape(micro, seq_len, heads_q, HEAD_SIZE)
-    k_raw = qkv[:, q_cols : q_cols + kv_cols].reshape(micro, seq_len, heads_kv, HEAD_SIZE)
-    value = (
-        qkv[:, q_cols + kv_cols :].astype(BF16).reshape(micro, seq_len, heads_kv, HEAD_SIZE)
-    )
-    q_unit, q_recip = unit_of(q_raw)
-    k_unit, k_recip = unit_of(k_raw)
-    query = (
-        rotate(q_unit * gain_q, cosine, sine)
-        .astype(BF16)
-        .reshape(micro, seq_len, heads_kv, groups, HEAD_SIZE)
-    )
-    key = rotate(k_unit * gain_k, cosine, sine).astype(BF16)
-    query, key = rounds.pump(query, key)
-    allowed = (
-        (segment[:, :, None] == segment[:, None, :])
-        & (row_ids[None, None, :] <= row_ids[None, :, None])
-        & ((valid[:, None, :] > 0) | (row_ids[None, None, :] == row_ids[None, :, None]))
-    )[:, None, None]
-    scores = scale * jnp.einsum("mqkgd,mtkd->mkgqt", query, key, preferred_element_type=F32)
-    masked = jnp.where(allowed, scores, -1e30)
-    lse = jax.nn.logsumexp(masked, axis=-1, keepdims=True)
-    probs = jnp.where(allowed, jnp.exp(masked - lse), 0.0)
-    probs_bf = probs.astype(BF16)
-    mixed = jnp.einsum("mkgqt,mtkd->mqkgd", probs_bf, value, preferred_element_type=F32)
-    (mixed_bf,) = rounds.pump((mixed.reshape(rows, q_cols) * valid_col).astype(BF16))
-    w_out_t = job_out.value
+    a1 = (unit_all * gain_one).astype(BF16)
+    (qkv,) = net.mix(g_steps, dot_nn(a1, w_qkv))
+    mixed_bf = attention_call(
+        attention_forward,
+        micro,
+        heads_q,
+        heads_kv,
+        (qkv,),
+        tables,
+        jax.ShapeDtypeStruct((rows, q_cols), BF16),
+        pl.BlockSpec((seq_len, q_cols), lambda i: (i, 0)),
+        2,
+    )
+    (mixed_bf,) = net.mix(g_steps, mixed_bf)
+    mixed_bf, *ffn_weights = lax.optimization_barrier((mixed_bf, *ffn_weights))
+    for chunk in range(1, CHUNKS):
+        gather_chunk(chunk, *ffn_weights)
     attn_part = dot_nt(mixed_bf, w_out_t).astype(BF16).reshape(micro, seq_len, width)
     resid = x_own.astype(F32) + net.run(net.scatter_rows(attn_part))
     unit_two, recip_two = unit_of(resid)
@@ -435,10 +698,11 @@
     a2 = net.run(net.gather_rows(a2_own)).reshape(rows, width)
     g_all = net.free(g_steps).reshape(rows, width)
 
-    da2, inners = None, []
+    da2, inners, w_chunks = None, [], []
     grad_jobs = []
     for chunk in range(CHUNKS):
-        w_chunk = ffn_jobs[chunk].value
+        w_chunk = jnp.concatenate(ffn_jobs[chunk].value, axis=0)
+        w_chunks.append(w_chunk)
         w_gu, w_down_t = w_chunk[:, : 2 * units], w_chunk[:, 2 * units :]
         gate_up = dot_nn(a2, w_gu)
         d_inner = dot_nn(g_all, w_down_t)
@@ -454,45 +718,40 @@
         inners.append(inner)
         part_da2 = dot_nt(d_gu, w_gu)
         da2 = part_da2 if da2 is None else da2 + part_da2
-        grad_jobs.append(rounds.add(net.scatter_grads([(a2, d_gu), (g_all, inner)]), 4))
+        grad_jobs.append(rounds.add(net.scatter_grads([(a2, d_gu), (g_all, inner)]), 3 if chunk == CHUNKS - 1 else 4))
     da2, *inners = lax.optimization_barrier((da2.astype(BF16), *inners))
     d_normed_two = net.run(net.scatter_rows(da2.reshape(micro, seq_len, width)))
     mlp = sum(
-        dot_nt(inner, job.value[:, 2 * units :]) for inner, job in zip(inners, ffn_jobs)
+        dot_nt(inner, w_chunk[:, 2 * units :]) for inner, w_chunk in zip(inners, w_chunks)
     )
     d_resid = g_own.astype(F32) + norm_back(d_normed_two, unit_two, recip_two, gain_two)
     acc_ffn_gain = jnp.sum(d_normed_two * unit_two, axis=(0, 1))
     d_resid_all = net.run(net.gather_rows(d_resid.astype(BF16))).reshape(rows, width)
     d_resid_all, mlp = lax.optimization_barrier((d_resid_all, mlp.astype(BF16)))
     mlp_steps = Steps(net.scatter_rows(mlp.reshape(micro, seq_len, width)))
-    job_grad_out = rounds.add(net.scatter_grads([(d_resid_all, mixed_bf)]), 4)
-
-    d_mixed = dot_nn(d_resid_all, w_out_t).astype(BF16) * valid_col.astype(BF16)
-    (d_mixed,) = net.mix(mlp_steps, d_mixed)
-    d_mixed = d_mixed.reshape(micro, seq_len, heads_kv, groups, HEAD_SIZE)
-    d_probs = jnp.einsum("mqkgd,mtkd->mkgqt", d_mixed, value, preferred_element_type=F32)
-    delta = jnp.sum(probs * d_probs, axis=-1, keepdims=True)
-    (d_scores,) = net.mix(mlp_steps, (probs * (d_probs - delta)).astype(BF16))
-    layer_out = net.from_local((resid + mlp_steps.value).astype(BF16))
-    d_query = scale * jnp.einsum("mkgqt,mtkd->mqkgd", d_scores, key, preferred_element_type=F32)
-    d_key = scale * jnp.einsum("mkgqt,mqkgd->mtkd", d_scores, query, preferred_element_type=F32)
-    d_value = jnp.einsum("mkgqt,mqkgd->mtkd", probs_bf, d_mixed, preferred_element_type=F32)
-    d_query, d_key, d_value = rounds.pump(d_query, d_key, d_value)
-    d_query = rotate(
-        d_query.reshape(micro, seq_len, heads_q, HEAD_SIZE), cosine, -sine
-    )
-    d_key = rotate(d_key, cosine, -sine)
-    acc_q_gain = jnp.sum(d_query * q_unit, axis=(0, 1, 2))
-    acc_k_gain = jnp.sum(d_key * k_unit, axis=(0, 1, 2))
-    d_qkv = jnp.concatenate(
-        [
-            norm_back(d_query, q_unit, q_recip, gain_q).astype(BF16).reshape(rows, q_cols),
-            norm_back(d_key, k_unit, k_recip, gain_k).astype(BF16).reshape(rows, kv_cols),
-            d_value.astype(BF16).reshape(rows, kv_cols),
-        ],
-        axis=1,
-    )
-    (d_qkv,) = rounds.pump(d_qkv)
+    job_grad_out = rounds.add(net.scatter_grads([(d_resid_all, mixed_bf)]), 3)
+
+    (d_mixed,) = net.mix(mlp_steps, dot_nn(d_resid_all, w_out_t).astype(BF16))
+    d_qkv, head_sums = attention_call(
+        attention_backward,
+        micro,
+        heads_q,
+        heads_kv,
+        (qkv, d_mixed),
+        tables,
+        (
+            jax.ShapeDtypeStruct(qkv.shape, BF16),
+            jax.ShapeDtypeStruct((micro, 2, HEAD_SIZE), F32),
+        ),
+        (
+            pl.BlockSpec((seq_len, qkv.shape[1]), lambda i: (i, 0)),
+            pl.BlockSpec((1, 2, HEAD_SIZE), lambda i: (i, 0, 0)),
+        ),
+        5,
+    )
+    acc_q_gain, acc_k_gain = jnp.sum(head_sums, axis=0)
+    (d_qkv,) = net.mix(mlp_steps, d_qkv)
+    layer_out = net.from_local((resid + net.free(mlp_steps)).astype(BF16))
     job_grad_qkv = rounds.add(net.scatter_grads([(a1, d_qkv)]), 4)
     (da1,) = rounds.pump(dot_nt(d_qkv, w_qkv))
     acc_attn_gain = jnp.sum(da1 * unit_all, axis=0)

time: 821 us -> 710 us (0.86)
  Pallas kernels: 23.4 us -> 111 us
  local copies, waits for them, and re-layouts: 137 us -> 60 us
  starting transfers between devices: 170 us -> 119 us
  other arithmetic: 118 us -> 84.7 us
  waiting for transfers between devices: 197 us -> 172 us
  matrix products: 160 us -> 151 us
    pallas_call x0 -> x3, Pallas kernels: none -> 99.8 us  [the longest x1 59.1 us: first_gathers(): pl.pallas_call(first_gathers, out_shape=(jax.ShapeDtypeStruct((micro, 4,...]
    ppermute x51 -> x28, waiting for transfers between devices: 101 us -> 56.3 us  [the longest x4 16.2 us: scatter_rows(): lax.ppermute(add_rounded(second[1], near_second[1]), 'tensor', XNEXT)]
    unnamed x373 -> x237, local copies, waits for them, and re-layouts: 74.1 us -> 35.8 us
    ppermute x65 -> x49, waiting for transfers between devices: 85 us -> 114 us  [step(): lax.ppermute(array, 'dp', perm)]
    ppermute x65 -> x49, starting transfers between devices: 111 us -> 86.2 us  [step(): lax.ppermute(array, 'dp', perm)]
    ppermute x51 -> x28, starting transfers between devices: 51.2 us -> 28 us  [the longest x4 5.32 us: scatter_rows(): lax.ppermute(jnp.stack([second[2], second[3]]), 'tensor', YNEXT)]
    dot_general x5 -> x0, matrix products: 14.8 us -> none  [the longest x1 7.33 us: on_device(): jnp.einsum('mkgqt,mqkgd->mtkd', probs_bf, d_mixed, preferred_element_type...]
    sub x1 -> x0, matrix products: 14.7 us -> none  [on_device(): d_scores, = net.mix(mlp_steps, (probs * (d_probs - delta)).astype(BF16))]
  transfers between devices with their start and end apart: 134 -> 93, of which waited for: 49 -> 36; matrix products, arithmetic and copies ran while one was open for 45% -> 37% of each run, Pallas kernels for 3% -> 7%
where the time goes in v3:
time: 710 us; the launch traced here: 702 us
  waiting for transfers between devices  172 us (24%)
  matrix products  151 us (21%)
  starting transfers between devices  119 us (17%)
  Pallas kernels  111 us (16%)
  other arithmetic  84.7 us (12%)
  local copies, waits for them, and re-layouts  60 us (8%)
    ppermute x49, waiting for transfers between devices, step(): lax.ppermute(array, 'dp', perm)  114 us
    ppermute x49, starting transfers between devices, step(): lax.ppermute(array, 'dp', perm)  86.2 us
    pallas_call x1, Pallas kernels, first_gathers(): pl.pallas_call(first_gathers, out_shape=(jax.ShapeDtypeStruct((micro, 4,...  59.1 us
    dot_general x8, matrix products, dot_nt(): lax.dot_general(left, right, (((1,), (1,)), ((), ())), preferred_element_...  52.4 us
    dot_general x16, matrix products, dot_tn(): lax.dot_general(left, right, (((0,), (0,)), ((), ())), preferred_element_...  50 us
    dot_general x8, matrix products, dot_nn(): return jnp.dot(left, right, preferred_element_type=F32)  48.8 us
    pallas_call x2, Pallas kernels, attention_call(): pl.pallas_call(functools.partial(body, heads_q, heads_kv), out_shape=out_...  40.8 us
    unnamed x237, local copies, waits for them, and re-layouts  35.8 us
  transfers between devices with their start and end apart: 93, of which 36 were waited for; matrix products, arithmetic and copies ran while one was open for 37% of the time, Pallas kernels for 7%

profile of v3, /device:TPU:8, one launch (start us, length us, event | category | flops | bytes accessed | tf_op | source)
XLA Modules:
  0.0 701.6 jit_solution(13488692722637380466)
XLA Ops:
  8.1 59.1 %shard_map.274 = (bf16[2,4,128,2048]{3,2,1,0:T(8,128)(2,1)}, bf16[8,256,1024]{2,1,0:T(8,128)(2,1)}, bf16[8,256,512]{2,1,0:T(8,128)(2,1)}, bf16[8,16,128]{2,1,0:T(8,128)(2,1)}) custom-call(bf16[2,128,2048]{2,1,0:T(8,128)(2,1)} %shard_map.273.x_ref, bf16[256,1024]{1,0:T(8,128)(2,1)} %pad_maximum_fusion.20.qkv_ref, bf16[256,512]{1,0:T(8,128)(2,1)} %bitcast.228, ...), custom_call_target="tpu_custom_call" | custom-call | tf_op jit(solution)/shard_map/pallas_call | solution.py:530
  115.1 20.6 %shard_map.276 = bf16[1024,512]{1,0:T(8,128)(2,1)} custom-call(f32[1024,1024]{1,0:T(8,128)} %fusion.157.qkv_ref, f32[1024,128]{1,0:T(8,128)} %pad_maximum_fusion.21.cos_ref, f32[1024,128]{1,0:T(8,128)} %pad_maximum_fusion.22.sin_ref, s32[1024,3]{1,0:T(8,128)} %copy.86.col_ref, s32[2,3,512]{2,1,0:T(4,128)} %pad_add_fusion.1.row_ref, ...), custom_call_target="tpu_custom_call" | custom-call | flops 1073741824 | bytes 8388608 | tf_op jit(solution)/shard_map/pallas_call | solution.py:171
  156.8 15.2 %collective-permute-done.10 = bf16[2,128,2048]{2,1,0:T(8,128)(2,1)} collective-permute-done((bf16[2,128,2048]{2,1,0:T(8,128)(2,1)}, bf16[2,128,2048]{2,1,0:T(8,128)(2,1)}, u32[]{:S(2)}, u32[]{:S(2)}) %collective-permute-start.10) | collective-permute-done | bytes 1048608 | tf_op jit(solution)/shard_map/ppermute | solution.py:574
  183.3 10.3 %collective-permute-done.15 = bf16[128,2048]{1,0:T(8,128)(2,1)S(1)} collective-permute-done((bf16[128,2048]{1,0:T(8,128)(2,1)S(1)}, bf16[128,2048]{1,0:T(8,128)(2,1)S(1)}, u32[]{:S(2)}, u32[]{:S(2)}) %collective-permute-start.15) | collective-permute-done | bytes 524320 | tf_op jit(solution)/shard_map/ppermute | solution.py:579
  210.8 9.7 %collective-permute-done.22 = bf16[256,1536]{0,1:T(8,128)(2,1)S(1)} collective-permute-done((bf16[256,1536]{0,1:T(8,128)(2,1)S(1)}, bf16[256,1536]{0,1:T(8,128)(2,1)S(1)}, u32[]{:S(2)}, u32[]{:S(2)}) %collective-permute-start.22) | collective-permute-done | bytes 786464 | tf_op jit(solution)/shard_map/ppermute | solution.py:357
  235.9 7.9 %collective-permute-done.25 = bf16[128,2048]{1,0:T(8,128)(2,1)S(1)} collective-permute-done((bf16[128,2048]{1,0:T(8,128)(2,1)S(1)}, bf16[128,2048]{1,0:T(8,128)(2,1)S(1)}, u32[]{:S(2)}, u32[]{:S(2)}) %collective-permute-start.25) | collective-permute-done | bytes 524320 | tf_op jit(solution)/shard_map/ppermute | solution.py:567
  254.4 9.8 %fusion.15 = f32[1024,1024]{1,0:T(8,128)} fusion(bf16[1024,2048]{1,0:T(8,128)(2,1)S(1)} %bitcast.216, bf16[2048,1536]{0,1:T(8,128)(2,1)} %constant_dynamic-update-slice_fusion), kind=kOutput, calls=%fused_computation.36 | convolution fusion | flops 4294967296 | bytes 12582912 | tf_op jit(solution)/shard_map/dot_general | solution.py:34
  277.4 8.3 %fusion.11 = f32[1024,1024]{1,0:T(8,128)} fusion(bf16[1024,2048]{1,0:T(8,128)(2,1)S(1)} %bitcast.217, bf16[2048,1536]{0,1:T(8,128)(2,1)} %constant_dynamic-update-slice_fusion.8), kind=kOutput, calls=%fused_computation.32 | convolution fusion | flops 4294967296 | bytes 12582912 | tf_op jit(solution)/shard_map/dot_general | solution.py:34
  298.6 6.9 fusion.13
  322.4 6.1 fusion.7
  328.5 14.6 %collective-permute-done.40 = bf16[256,1536]{0,1:T(8,128)(2,1)S(1)} collective-permute-done((bf16[256,1536]{0,1:T(8,128)(2,1)S(1)}, bf16[256,1536]{0,1:T(8,128)(2,1)S(1)}, u32[]{:S(2)}, u32[]{:S(2)}) %collective-permute-start.40) | collective-permute-done | bytes 786464 | tf_op jit(solution)/shard_map/ppermute | solution.py:357
  354.9 6.7 fusion.9
  377.9 8.4 %collective-permute-done.45 = bf16[256,1536]{0,1:T(8,128)(2,1)S(1)} collective-permute-done((bf16[256,1536]{0,1:T(8,128)(2,1)S(1)}, bf16[256,1536]{0,1:T(8,128)(2,1)S(1)}, u32[]{:S(2)}, u32[]{:S(2)}) %collective-permute-start.45) | collective-permute-done | bytes 786464 | tf_op jit(solution)/shard_map/ppermute | solution.py:357
  390.8 9.9 %add_convert_fusion.1 = bf16[1024,2048]{1,0:T(8,128)(2,1)S(1)} fusion(f32[1024,2048]{1,0:T(8,128)} %fusion.13, f32[1024,2048]{1,0:T(8,128)} %fusion.9, bf16[1024,1024]{1,0:T(8,128)(2,1)S(1)} %pad_maximum_fusion.2, bf16[2048,1536]{0,1:T(8,128)(2,1)} %copy-done.49), kind=kOutput, calls=%fused_computation.8 | convolution fusion | flops 4301258752 | bytes 27262976 | tf_op jit(solution)/shard_map/dot_general | solution.py:38
  410.1 7.3 %fusion.48 = f32[1024,2048]{1,0:T(8,128)} fusion(bf16[1024,512]{1,0:T(8,128)(2,1)S(1)} %copy-done.98, bf16[2048,1536]{0,1:T(8,128)(2,1)} %constant_dynamic-update-slice_fusion.8), kind=kOutput, calls=%fused_computation.105 | convolution fusion | flops 2147483648 | bytes 11534336 | tf_op jit(solution)/shard_map/dot_general | solution.py:38
  417.3 8.9 %add_convert_fusion = bf16[1024,2048]{1,0:T(8,128)(2,1)} fusion(f32[1024,2048]{1,0:T(8,128)S(1)} %fusion.52, f32[1024,2048]{1,0:T(8,128)} %fusion.48, bf16[1024,512]{1,0:T(8,128)(2,1)S(1)} %get-tuple-element.238, bf16[2048,1536]{0,1:T(8,128)(2,1)} %copy-done.49), kind=kOutput, calls=%fused_computation.7 | convolution fusion | flops 2153775104 | bytes 24117248 | tf_op jit(solution)/shard_map/dot_general | solution.py:38
  436.7 15.4 %collective-permute-done.50 = bf16[256,1536]{0,1:T(8,128)(2,1)S(1)} collective-permute-done((bf16[256,1536]{0,1:T(8,128)(2,1)S(1)}, bf16[256,1536]{0,1:T(8,128)(2,1)S(1)}, u32[]{:S(2)}, u32[]{:S(2)}) %collective-permute-start.50) | collective-permute-done | bytes 786464 | tf_op jit(solution)/shard_map/ppermute | solution.py:357
  493.8 8.0 %collective-permute-done.58 = bf16[256,1536]{0,1:T(8,128)(2,1)S(1)} collective-permute-done((bf16[256,1536]{0,1:T(8,128)(2,1)}, bf16[256,1536]{0,1:T(8,128)(2,1)S(1)}, u32[]{:S(2)}, u32[]{:S(2)}) %collective-permute-start.58) | collective-permute-done | bytes 786464 | tf_op jit(solution)/shard_map/ppermute | solution.py:357
  511.6 6.2 collective-permute-done.59
  518.1 7.7 %collective-permute-done.63 = bf16[256,1536]{0,1:T(8,128)(2,1)S(1)} collective-permute-done((bf16[256,1536]{0,1:T(8,128)(2,1)S(1)}, bf16[256,1536]{0,1:T(8,128)(2,1)S(1)}, u32[]{:S(2)}, u32[]{:S(2)}) %collective-permute-start.63) | collective-permute-done | bytes 786464 | tf_op jit(solution)/shard_map/ppermute | solution.py:357
  541.6 7.3 %collective-permute-done.67 = bf16[256,1536]{0,1:T(8,128)(2,1)S(1)} collective-permute-done((bf16[256,1536]{0,1:T(8,128)(2,1)S(1)}, bf16[256,1536]{0,1:T(8,128)(2,1)S(1)}, u32[]{:S(2)}, u32[]{:S(2)}) %collective-permute-start.67) | collective-permute-done | bytes 786464 | tf_op jit(solution)/shard_map/ppermute | solution.py:357
  565.4 20.2 %shard_map.277 = (bf16[1024,1024]{1,0:T(8,128)(2,1)}, f32[2,2,128]{2,1,0:T(2,128)}) custom-call(f32[1024,1024]{1,0:T(8,128)} %fusion.157.qkv_ref, bf16[1024,512]{1,0:T(8,128)(2,1)} %convolution_convert_fusion.4.grad_ref, f32[1024,128]{1,0:T(8,128)} %pad_maximum_fusion.21.cos_ref, f32[1024,128]{1,0:T(8,128)} %pad_maximum_fusion.22.sin_ref, ...), custom_call_target="tpu_custom_call" | custom-call | flops 2684354560 | bytes 10485760 | tf_op jit(solution)/shard_map/pallas_call | solution.py:171
  587.8 6.1 fusion.39
  639.3 12.5 %collective-permute-done.79 = bf16[256,512]{1,0:T(8,128)(2,1)S(1)} collective-permute-done((bf16[256,512]{1,0:T(8,128)(2,1)S(1)}, bf16[256,512]{1,0:T(8,128)(2,1)S(1)}, u32[]{:S(2)}, u32[]{:S(2)}) %collective-permute-start.79) | collective-permute-done | bytes 262176 | tf_op jit(solution)/shard_map/ppermute | solution.py:357
  (583 shorter events, 405.6 us)
Async XLA Ops:
  70.1 31.2 %collective-permute-start.1 = (bf16[2,128,2048]{2,1,0:T(8,128)(2,1)}, bf16[2,128,2048]{2,1,0:T(8,128)(2,1)S(1)}, u32[]{:S(2)}, u32[]{:S(2)}) collective-permute-start(bf16[2,128,2048]{2,1,0:T(8,128)(2,1)} %shard_map.275), channel_id=1, source_target_pairs={{0,2},{1,3},{2,0},{3,1},{4,6},{5,7},{6,4},{7,5},{8,10},{9,11},{10,... | collective-permute-start | bytes 3145736 | tf_op jit(solution)/shard_map/ppermute | solution.py:563
  71.6 29.7 %collective-permute-start = (bf16[2,128,2048]{2,1,0:T(8,128)(2,1)}, bf16[2,128,2048]{2,1,0:T(8,128)(2,1)}, u32[]{:S(2)}, u32[]{:S(2)}) collective-permute-start(bf16[2,128,2048]{2,1,0:T(8,128)(2,1)} %shard_map.275), channel_id=1, source_target_pairs={{0,1},{1,0},{2,3},{3,2},{4,5},{5,4},{6,7},{7,6},{8,9},{9,8},{10,11... | collective-permute-start | bytes 3145736 | tf_op jit(solution)/shard_map/ppermute | solution.py:562
  101.3 36.6 %collective-permute-start.9 = (bf16[256,1536]{0,1:T(8,128)(2,1)}, bf16[256,1536]{0,1:T(8,128)(2,1)}, u32[]{:S(2)}, u32[]{:S(2)}) collective-permute-start(bf16[256,1536]{0,1:T(8,128)(2,1)} %collective-permute-done.2), channel_id=1, source_target_pairs={{0,4},{4,0},{8,12},{12,8},{16,20},{20,16},{24,28},{28,24},{1,5},{5... | collective-permute-start | bytes 2359304 | tf_op jit(solution)/shard_map/ppermute | solution.py:357
  101.4 36.5 %collective-permute-start.7 = (bf16[256,1536]{0,1:T(8,128)(2,1)}, bf16[256,1536]{0,1:T(8,128)(2,1)}, u32[]{:S(2)}, u32[]{:S(2)}) collective-permute-start(bf16[256,1536]{0,1:T(8,128)(2,1)} %collective-permute-done.2), channel_id=1, source_target_pairs={{8,16},{12,20},{16,8},{20,12},{9,17},{13,21},{17,9},{21,13},{10,18... | collective-permute-start | bytes 2359304 | tf_op jit(solution)/shard_map/ppermute | solution.py:357
  106.5 31.4 %collective-permute-start.8 = (bf16[256,1536]{0,1:T(8,128)(2,1)}, bf16[256,1536]{0,1:T(8,128)(2,1)}, u32[]{:S(2)}, u32[]{:S(2)}) collective-permute-start(bf16[256,1536]{0,1:T(8,128)(2,1)} %collective-permute-done.3), channel_id=1, source_target_pairs={{8,0},{12,4},{16,24},{20,28},{9,1},{13,5},{17,25},{21,29},{10,2},{... | collective-permute-start | bytes 2359304 | tf_op jit(solution)/shard_map/ppermute | solution.py:357
  109.7 28.1 %collective-permute-start.6 = (bf16[128,2048]{1,0:T(8,128)(2,1)}, bf16[128,2048]{1,0:T(8,128)(2,1)}, u32[]{:S(2)}, u32[]{:S(2)}) collective-permute-start(bf16[128,2048]{1,0:T(8,128)(2,1)} %slice_bitcast_fusion.20), channel_id=1, source_target_pairs={{0,1},{1,0},{2,3},{3,2},{4,5},{5,4},{6,7},{7,6},{8,9},{9,8},{10,11... | collective-permute-start | bytes 1572872 | tf_op jit(solution)/shard_map/ppermute | solution.py:567
  110.2 27.6 %collective-permute-start.5 = (bf16[128,2048]{1,0:T(8,128)(2,1)}, bf16[128,2048]{1,0:T(8,128)(2,1)}, u32[]{:S(2)}, u32[]{:S(2)}) collective-permute-start(bf16[128,2048]{1,0:T(8,128)(2,1)} %slice_bitcast_fusion.21), channel_id=1, source_target_pairs={{0,2},{1,3},{2,0},{3,1},{4,6},{5,7},{6,4},{7,5},{8,10},{9,11},{10,... | collective-permute-start | bytes 1572872 | tf_op jit(solution)/shard_map/ppermute | solution.py:566
  193.9 26.6 %collective-permute-start.23 = (bf16[256,1536]{0,1:T(8,128)(2,1)S(1)}, bf16[256,1536]{0,1:T(8,128)(2,1)S(1)}, u32[]{:S(2)}, u32[]{:S(2)}) collective-permute-start(bf16[256,1536]{0,1:T(8,128)(2,1)S(1)} %collective-permute-done.16), channel_id=1, source_target_pairs={{0,4},{4,0},{8,12},{12,8},{16,20},{20,16},{24,28},{28,24},{1,5},{5... | collective-permute-start | bytes 2359304 | tf_op jit(solution)/shard_map/ppermute | solution.py:357
  193.9 26.5 %collective-permute-start.21 = (bf16[256,1536]{0,1:T(8,128)(2,1)S(1)}, bf16[256,1536]{0,1:T(8,128)(2,1)S(1)}, u32[]{:S(2)}, u32[]{:S(2)}) collective-permute-start(bf16[256,1536]{0,1:T(8,128)(2,1)S(1)} %collective-permute-done.16), channel_id=1, source_target_pairs={{8,16},{12,20},{16,8},{20,12},{9,17},{13,21},{17,9},{21,13},{10,18... | collective-permute-start | bytes 2359304 | tf_op jit(solution)/shard_map/ppermute | solution.py:357
  199.9 25.4 %collective-permute-start.20 = (bf16[2,128,2048]{2,1,0:T(8,128)(2,1)S(1)}, bf16[2,128,2048]{2,1,0:T(8,128)(2,1)S(1)}, u32[]{:S(2)}, u32[]{:S(2)}) collective-permute-start(bf16[2,128,2048]{2,1,0:T(8,128)(2,1)S(1)} %multiply_convert_fusion.9), channel_id=1, source_target_pairs={{0,2},{1,3},{2,0},{3,1},{4,6},{5,7},{6,4},{7,5},{8,10},{9,11},{10,... | collective-permute-start | bytes 3145736 | tf_op jit(solution)/shard_map/ppermute | solution.py:563
  201.5 25.0 %collective-permute-start.19 = (bf16[2,128,2048]{2,1,0:T(8,128)(2,1)S(1)}, bf16[2,128,2048]{2,1,0:T(8,128)(2,1)S(1)}, u32[]{:S(2)}, u32[]{:S(2)}) collective-permute-start(bf16[2,128,2048]{2,1,0:T(8,128)(2,1)S(1)} %multiply_convert_fusion.9), channel_id=1, source_target_pairs={{0,1},{1,0},{2,3},{3,2},{4,5},{5,4},{6,7},{7,6},{8,9},{9,8},{10,11... | collective-permute-start | bytes 3145736 | tf_op jit(solution)/shard_map/ppermute | solution.py:562
  250.3 26.2 %collective-permute-start.35 = (bf16[256,1536]{0,1:T(8,128)(2,1)S(1)}, bf16[256,1536]{0,1:T(8,128)(2,1)S(1)}, u32[]{:S(2)}, u32[]{:S(2)}) collective-permute-start(bf16[256,1536]{0,1:T(8,128)(2,1)S(1)} %get-tuple-element.331), channel_id=1, source_target_pairs={{0,4},{4,0},{8,12},{12,8},{16,20},{20,16},{24,28},{28,24},{1,5},{5... | collective-permute-start | bytes 2359304 | tf_op jit(solution)/shard_map/ppermute | solution.py:523
  354.4 71.9 %collective-permute-start.48 = (bf16[1024,1024]{0,1:T(8,128)(2,1)}, bf16[1024,1024]{0,1:T(8,128)(2,1)}, u32[]{:S(2)}, u32[]{:S(2)}) collective-permute-start(bf16[1024,1024]{0,1:T(8,128)(2,1)} %convolution_convert_fusion.2), channel_id=1, source_target_pairs={{0,4},{4,0},{8,12},{12,8},{16,20},{20,16},{24,28},{28,24},{1,5},{5... | collective-permute-start | bytes 6291464 | tf_op jit(solution)/shard_map/ppermute | solution.py:549
  390.8 70.9 %collective-permute-start.62 = (bf16[1024,512]{0,1:T(8,128)(2,1)}, bf16[1024,512]{0,1:T(8,128)(2,1)}, u32[]{:S(2)}, u32[]{:S(2)}) collective-permute-start(bf16[1024,512]{0,1:T(8,128)(2,1)} %fusion.82), channel_id=1, source_target_pairs={{0,4},{4,0},{8,12},{12,8},{16,20},{20,16},{24,28},{28,24},{1,5},{5... | collective-permute-start | bytes 3145736 | tf_op jit(solution)/shard_map/ppermute | solution.py:549
  403.7 33.0 %collective-permute-start.46 = (bf16[2,128,2048]{2,1,0:T(8,128)(2,1)}, bf16[2,128,2048]{2,1,0:T(8,128)(2,1)}, u32[]{:S(2)}, u32[]{:S(2)}) collective-permute-start(bf16[2,128,2048]{2,1,0:T(8,128)(2,1)} %pad_maximum_fusion.8), channel_id=1, source_target_pairs={{0,1},{1,0},{2,3},{3,2},{4,5},{5,4},{6,7},{7,6},{8,9},{9,8},{10,11... | collective-permute-start | bytes 3145736 | tf_op jit(solution)/shard_map/ppermute | solution.py:574
  405.5 31.1 %collective-permute-start.47 = (bf16[2,128,2048]{2,1,0:T(8,128)(2,1)}, bf16[2,128,2048]{2,1,0:T(8,128)(2,1)}, u32[]{:S(2)}, u32[]{:S(2)}) collective-permute-start(bf16[2,128,2048]{2,1,0:T(8,128)(2,1)} %pad_maximum_fusion.9), channel_id=1, source_target_pairs={{0,2},{1,3},{2,0},{3,1},{4,6},{5,7},{6,4},{7,5},{8,10},{9,11},{10,... | collective-permute-start | bytes 3145736 | tf_op jit(solution)/shard_map/ppermute | solution.py:575
  461.7 26.7 %collective-permute-start.61 = (bf16[1024,1024]{0,1:T(8,128)(2,1)}, bf16[1024,1024]{0,1:T(8,128)(2,1)}, u32[]{:S(2)}, u32[]{:S(2)}) collective-permute-start(bf16[1024,1024]{0,1:T(8,128)(2,1)} %convolution_convert_fusion.1), channel_id=1, source_target_pairs={{0,4},{4,0},{8,12},{12,8},{16,20},{20,16},{24,28},{28,24},{1,5},{5... | collective-permute-start | bytes 6291464 | tf_op jit(solution)/shard_map/ppermute | solution.py:549
  554.9 32.9 %collective-permute-start.71 = (bf16[256,1536]{0,1:T(8,128)(2,1)}, bf16[256,1536]{0,1:T(8,128)(2,1)}, u32[]{:S(2)}, u32[]{:S(2)}) collective-permute-start(bf16[256,1536]{0,1:T(8,128)(2,1)} %add_convert_fusion.10), channel_id=1, source_target_pairs={{0,8},{4,12},{8,0},{12,4},{16,24},{20,28},{24,16},{28,20},{1,9},{5... | collective-permute-start | bytes 2359304 | tf_op jit(solution)/shard_map/ppermute | solution.py:357
  556.0 31.7 %collective-permute-start.70 = (bf16[256,1536]{0,1:T(8,128)(2,1)}, bf16[256,1536]{0,1:T(8,128)(2,1)}, u32[]{:S(2)}, u32[]{:S(2)}) collective-permute-start(bf16[256,1536]{0,1:T(8,128)(2,1)} %add_convert_fusion.11), channel_id=1, source_target_pairs={{8,16},{12,20},{16,8},{20,12},{9,17},{13,21},{17,9},{21,13},{10,18... | collective-permute-start | bytes 2359304 | tf_op jit(solution)/shard_map/ppermute | solution.py:357
  560.6 27.1 %collective-permute-start.69 = (bf16[128,2048]{1,0:T(8,128)(2,1)}, bf16[128,2048]{1,0:T(8,128)(2,1)}, u32[]{:S(2)}, u32[]{:S(2)}) collective-permute-start(bf16[128,2048]{1,0:T(8,128)(2,1)} %get-tuple-element.358), channel_id=1, source_target_pairs={{0,1},{1,0},{2,3},{3,2},{4,5},{5,4},{6,7},{7,6},{8,9},{9,8},{10,11... | collective-permute-start | bytes 1572872 | tf_op jit(solution)/shard_map/ppermute | solution.py:579
  560.7 27.0 %collective-permute-start.68 = (bf16[128,2048]{1,0:T(8,128)(2,1)}, bf16[128,2048]{1,0:T(8,128)(2,1)}, u32[]{:S(2)}, u32[]{:S(2)}) collective-permute-start(bf16[128,2048]{1,0:T(8,128)(2,1)} %get-tuple-element.359), channel_id=1, source_target_pairs={{0,2},{1,3},{2,0},{3,1},{4,6},{5,7},{6,4},{7,5},{8,10},{9,11},{10,... | collective-permute-start | bytes 1572872 | tf_op jit(solution)/shard_map/ppermute | solution.py:578
  586.3 25.0 %collective-permute-start.74 = (bf16[256,512]{1,0:T(8,128)(2,1)}, bf16[256,512]{1,0:T(8,128)(2,1)S(1)}, u32[]{:S(2)}, u32[]{:S(2)}) collective-permute-start(bf16[256,512]{1,0:T(8,128)(2,1)} %get-tuple-element.403), channel_id=1, source_target_pairs={{0,8},{4,12},{24,16},{28,20},{1,9},{5,13},{25,17},{29,21},{2,10},{... | collective-permute-start | bytes 786440 | tf_op jit(solution)/shard_map/ppermute | solution.py:357
  621.0 32.7 %collective-permute-start.76 = (bf16[2,128,2048]{2,1,0:T(8,128)(2,1)S(1)}, bf16[2,128,2048]{2,1,0:T(8,128)(2,1)S(1)}, u32[]{:S(2)}, u32[]{:S(2)}) collective-permute-start(bf16[2,128,2048]{2,1,0:T(8,128)(2,1)S(1)} %pad_maximum_fusion.12), channel_id=1, source_target_pairs={{0,1},{1,0},{2,3},{3,2},{4,5},{5,4},{6,7},{7,6},{8,9},{9,8},{10,11... | collective-permute-start | bytes 3145736 | tf_op jit(solution)/shard_map/ppermute | solution.py:574
  623.2 30.6 %collective-permute-start.77 = (bf16[2,128,2048]{2,1,0:T(8,128)(2,1)S(1)}, bf16[2,128,2048]{2,1,0:T(8,128)(2,1)S(1)}, u32[]{:S(2)}, u32[]{:S(2)}) collective-permute-start(bf16[2,128,2048]{2,1,0:T(8,128)(2,1)S(1)} %pad_maximum_fusion.13), channel_id=1, source_target_pairs={{0,2},{1,3},{2,0},{3,1},{4,6},{5,7},{6,4},{7,5},{8,10},{9,11},{10,... | collective-permute-start | bytes 3145736 | tf_op jit(solution)/shard_map/ppermute | solution.py:575
  (175 other events, 2722.2 us)

commit v4 on v3

--- a/solution.py
+++ b/solution.py
@@ -11,7 +11,7 @@
 HEAD_SIZE = 128
 EPS = 1e-06
 THETA = 1000000.0
-CHUNKS = 3
+CHUNKS = 2
 F32 = jnp.float32
 BF16 = jnp.bfloat16
 
@@ -339,6 +339,262 @@
     out_lane.end(inner)
 
 
+class Copies:
+    def __init__(self, send_sems, recv_sems):
+        self.send_sems, self.recv_sems, self.count = send_sems, recv_sems, 0
+
+    def make(self, source, target, device):
+        index = self.count
+        self.count += 1
+        return pltpu.make_async_remote_copy(
+            src_ref=source,
+            dst_ref=target,
+            send_sem=self.send_sems.at[index],
+            recv_sem=self.recv_sems.at[index],
+            device_id=device,
+            device_id_type=pl.DeviceIdType.MESH,
+        )
+
+
+def greet(peers):
+    barrier = pltpu.get_barrier_semaphore()
+    for device in peers:
+        pl.semaphore_signal(barrier, device_id=device, device_id_type=pl.DeviceIdType.MESH)
+    pl.semaphore_wait(barrier, len(peers))
+
+
+class PlaneSum:
+    def __init__(self, copies, own, part_ref, near, far_send, far):
+        x, y = {"tensor": own ^ 1}, {"tensor": own ^ 2}
+        self.part, self.near, self.far_send, self.far_got = part_ref, near, far_send, far
+        self.diag, self.direct, self.far = [], [], []
+        for i, (device, other, block) in enumerate(((x, y, 1), (y, x, 2))):
+            self.diag.append(copies.make(self.rows(i, 3), near.at[i, 1], device))
+            self.direct.append(copies.make(self.rows(i, block), near.at[i, 0], device))
+            self.far.append(copies.make(far_send.at[i], far.at[i], other))
+
+    def rows(self, i, block):
+        count = self.far_got.shape[1]
+        return self.part.at[i, block * count : (block + 1) * count]
+
+    def begin(self):
+        for copy in (*self.diag, *self.direct):
+            copy.start()
+
+    def middle(self):
+        for i in range(2):
+            self.diag[i].wait_recv()
+            self.far_send[i] = add_rounded(self.rows(i, 2 - i)[...], self.near[i, 1])
+            self.far[i].start()
+
+    def arrive(self, i):
+        self.direct[i].wait_recv()
+        self.far[i].wait_recv()
+        return (
+            self.rows(i, 0)[...].astype(F32)
+            + self.near[i, 0].astype(F32)
+            + self.far_got[i].astype(F32)
+        )
+
+    def end(self):
+        for copy in (*self.diag, *self.direct, *self.far):
+            copy.wait_send()
+
+
+class LineSum:
+    def __init__(self, copies, me, inner, in_ref, sent, got):
+        self.inner, self.part, self.sent, self.got = inner, in_ref, sent, got
+        pair, over = {"dp": me ^ 2}, {"dp": me ^ 6}
+        self.inward = [
+            copies.make(self.block(3), got.at[0], pair),
+            copies.make(self.block(2), got.at[1], pair),
+        ]
+        self.over = [
+            copies.make(sent.at[0], got.at[2], over),
+            copies.make(sent.at[1], got.at[3], over),
+        ]
+        self.pair = copies.make(sent.at[2], got.at[4], pair)
+
+    def block(self, index):
+        count = self.got.shape[1]
+        return self.part.at[index * count : (index + 1) * count]
+
+    def begin(self):
+        @pl.when(jnp.logical_not(self.inner))
+        def _():
+            for copy in self.inward:
+                copy.start()
+            self.sent[2] = self.block(1)[...]
+            self.pair.start()
+
+    def middle(self):
+        @pl.when(self.inner)
+        def _():
+            self.inward[0].wait_recv()
+            self.sent[0] = add_rounded(self.block(2)[...], self.got[0])
+            self.over[0].start()
+
+    def last(self):
+        @pl.when(self.inner)
+        def _():
+            self.inward[1].wait_recv()
+            self.sent[1] = add_rounded(self.block(3)[...], self.got[1])
+            self.over[1].start()
+            self.over[0].wait_recv()
+            self.sent[2] = add_rounded(self.block(1)[...], self.got[2])
+            self.pair.start()
+
+    def end(self, out_ref):
+        self.pair.wait_recv()
+        out_ref[...] = self.block(0)[...].astype(F32) + self.got[4].astype(F32)
+
+        @pl.when(self.inner)
+        def _():
+            self.over[1].wait_recv()
+            out_ref[...] += self.got[3].astype(F32)
+            for copy in self.over:
+                copy.wait_send()
+
+        @pl.when(jnp.logical_not(self.inner))
+        def _():
+            for copy in self.inward:
+                copy.wait_send()
+
+        self.pair.wait_send()
+
+
+class PlaneShare:
+    def __init__(self, copies, own, mine, out, local_sem):
+        x, y = {"tensor": own ^ 1}, {"tensor": own ^ 2}
+        self.local = pltpu.make_async_copy(mine, out.at[:, 0], local_sem)
+        self.near = [
+            copies.make(mine.at[0], out.at[0, 1], x),
+            copies.make(mine.at[1], out.at[1, 2], y),
+            copies.make(mine.at[1], out.at[1, 1], x),
+            copies.make(mine.at[0], out.at[0, 2], y),
+        ]
+        self.diag = [
+            copies.make(out.at[0, 1], out.at[0, 3], y),
+            copies.make(out.at[1, 2], out.at[1, 3], x),
+        ]
+
+    def begin(self):
+        for copy in self.near:
+            copy.start()
+        self.local.start()
+
+    def middle(self):
+        for i in range(2):
+            self.near[i].wait_recv()
+            self.diag[i].start()
+
+    def end(self):
+        for copy in (*self.near[2:], *self.diag):
+            copy.wait_recv()
+        for copy in (*self.near, *self.diag):
+            copy.wait_send()
+        self.local.wait()
+
+
+def places():
+    me, own = lax.axis_index("dp"), lax.axis_index("tensor")
+    z = me // 2
+    greet(
+        (
+            *({"tensor": own ^ 1}, {"tensor": own ^ 2}),
+            *({"dp": me ^ 1}, {"dp": me ^ 2}, {"dp": me ^ 6}),
+        )
+    )
+    return me, own, (z == 1) | (z == 2)
+
+
+def middle_forward(
+    part_ref,
+    x_ref,
+    gain_ref,
+    buf_ref,
+    resid_ref,
+    rows_ref,
+    bufs_ref,
+    near,
+    far_send,
+    far,
+    mine,
+    local_sems,
+    send_sems,
+    recv_sems,
+    line_send,
+    line_recv,
+):
+    me, own, inner = places()
+    copies = Copies(send_sems, recv_sems)
+    line = ZLane(me, buf_ref, bufs_ref, line_send, line_recv)
+    plane = PlaneSum(copies, own, part_ref, near, far_send, far)
+    share = PlaneShare(copies, own, mine, rows_ref, local_sems.at[0])
+    kept = pltpu.make_async_copy(buf_ref, bufs_ref.at[0], local_sems.at[1])
+    plane.begin()
+    line.begin(inner)
+    kept.start()
+    plane.middle()
+    for i in range(2):
+        resid = x_ref[i].astype(F32) + plane.arrive(i)
+        resid_ref[i] = resid
+        mine[i] = (unit_of(resid)[0] * gain_ref[...]).astype(BF16)
+    share.begin()
+    line.middle(inner)
+    share.middle()
+    line.last(inner)
+    share.end()
+    plane.end()
+    kept.wait()
+    line.end(inner)
+
+
+def middle_backward(
+    part_ref,
+    g_ref,
+    resid_ref,
+    gain_ref,
+    line_ref,
+    out_ref,
+    rows_ref,
+    sum_ref,
+    line_out,
+    near,
+    far_send,
+    far,
+    mine,
+    line_sent,
+    line_got,
+    local_sems,
+    send_sems,
+    recv_sems,
+):
+    me, own, inner = places()
+    copies = Copies(send_sems, recv_sems)
+    line = LineSum(copies, me, inner, line_ref, line_sent, line_got)
+    plane = PlaneSum(copies, own, part_ref, near, far_send, far)
+    share = PlaneShare(copies, own, mine, rows_ref, local_sems.at[0])
+    plane.begin()
+    line.begin()
+    plane.middle()
+    line.middle()
+    sum_ref[...] = jnp.zeros_like(sum_ref)
+    for i in range(2):
+        unit, recip = unit_of(resid_ref[i])
+        upstream = plane.arrive(i)
+        sum_ref[...] += jnp.sum(upstream * unit, axis=0, keepdims=True)
+        total = g_ref[i].astype(F32) + norm_back(upstream, unit, recip, gain_ref[...])
+        out_ref[i] = total
+        mine[i] = total.astype(BF16)
+    share.begin()
+    line.last()
+    share.middle()
+    line.end(line_out)
+    share.end()
+    plane.end()
+
+
 class Job:
     def __init__(self, gen, open_at):
         self.gen, self.open_at = gen, open_at
@@ -459,6 +715,23 @@
     def first_gathers(self, rows, *weights):
         gathered = self.free(self.gather_rows(rows))
         return gathered, *(lax.all_gather(array, "dp", axis=0) for array in weights)
+
+    def middle_forward(self, part, x_own, gain, buf):
+        resid = x_own.astype(F32) + self.free(self.scatter_rows(part))
+        rows = self.free(self.gather_rows((unit_of(resid)[0] * gain).astype(BF16)))
+        return resid, rows, lax.all_gather(buf, "dp", axis=0)
+
+    def middle_backward(self, part, g_own, resid, gain, line):
+        unit, recip = unit_of(resid)
+        upstream = self.free(self.scatter_rows(part))
+        total = g_own.astype(F32) + norm_back(upstream, unit, recip, gain)
+        rows = self.free(self.gather_rows(total.astype(BF16)))
+        return total, rows, jnp.sum(upstream * unit, axis=(0, 1)), line
+
+    def scatter_here(self, parts):
+        job = Job(self.scatter_grads(parts), 0)
+        job.step(None)
+        return job.value
 
     def scatter_grads(self, parts):
         full = jnp.concatenate([dot_tn(l, r).astype(BF16) for l, r in parts], axis=1)
@@ -540,6 +813,67 @@
             ],
             compiler_params=pltpu.CompilerParams(collective_id=0, has_side_effects=True),
         )(rows, *weights)
+
+    def middle_call(self, body, operands, outputs, places, line, line_sems, scratch, identity):
+        micro, count, width = self.rows
+        vmem, hbm = pl.BlockSpec(memory_space=pltpu.VMEM), pl.BlockSpec(memory_space=pl.ANY)
+        return pl.pallas_call(
+            body,
+            out_shape=outputs,
+            in_specs=[vmem] * (len(operands) - 1) + [line],
+            out_specs=[hbm if place else vmem for place in places],
+            scratch_shapes=[
+                pltpu.VMEM((micro, 2, count, width), BF16),
+                *[pltpu.VMEM(self.rows, BF16)] * 3,
+                *scratch,
+                *[pltpu.SemaphoreType.DMA((copies,)) for copies in line_sems],
+            ],
+            compiler_params=pltpu.CompilerParams(collective_id=identity, has_side_effects=True),
+        )(*operands)
+
+    def middle_forward(self, part, x_own, gain, buf):
+        self.rows = micro, count, width = x_own.shape
+        return self.middle_call(
+            middle_forward,
+            (part, x_own, gain.reshape(1, -1), buf),
+            (
+                jax.ShapeDtypeStruct(self.rows, F32),
+                jax.ShapeDtypeStruct((micro, 4, count, width), BF16),
+                jax.ShapeDtypeStruct((8,) + buf.shape, BF16),
+            ),
+            (False, True, True),
+            pl.BlockSpec(memory_space=pl.ANY),
+            (2, 12, 12, 9, 8),
+            (),
+            2,
+        )
+
+    def middle_backward(self, part, g_own, resid, gain, line):
+        self.rows = micro, count, width = g_own.shape
+        block = (line.shape[0] // 4, line.shape[1])
+        total, rows, sums, grads = self.middle_call(
+            middle_backward,
+            (part, g_own, resid, gain.reshape(1, -1), line),
+            (
+                jax.ShapeDtypeStruct(self.rows, F32),
+                jax.ShapeDtypeStruct((micro, 4, count, width), BF16),
+                jax.ShapeDtypeStruct((1, width), F32),
+                jax.ShapeDtypeStruct(block, F32),
+            ),
+            (False, True, False, False),
+            pl.BlockSpec(memory_space=pltpu.VMEM),
+            (1, 17, 17),
+            (pltpu.VMEM((3,) + block, BF16), pltpu.VMEM((5,) + block, BF16)),
+            3,
+        )
+        return total, rows, sums.reshape(-1), grads
+
+    def scatter_here(self, parts):
+        summed, half = [], parts[0][0].shape[1] // 2
+        for left, right in parts:
+            away = lax.ppermute(dot_tn(left[:, half:], right).astype(BF16), "dp", CORE)
+            summed.append((dot_tn(left[:, :half], right) + away.astype(F32)).astype(BF16))
+        return jnp.concatenate(summed, axis=1)
 
     def scatter_grads(self, parts):
         away, half = [], parts[0][0].shape[1] // 2
@@ -649,14 +983,12 @@
     later = (segment_ids, positions, pad_mask, cotangent, w_gate, w_up, w_down)
     x_bf, *later = lax.optimization_barrier((x_bf, *later))
     segment_ids, positions, pad_mask, cotangent, *ffn_weights = later
-    ffn_jobs = []
-
-    def gather_chunk(chunk, w_gate, w_up, w_down):
+    w_gate, w_up, w_down = ffn_weights
+    ffn_bufs = []
+    for chunk in range(CHUNKS):
         cut = slice(chunk * units, (chunk + 1) * units)
-        buf = jnp.concatenate([w_gate[:, cut], w_up[:, cut], w_down[cut, :].T], axis=1)
-        ffn_jobs.append(rounds.add(net.gather_weights(buf), 4))
-
-    gather_chunk(0, *ffn_weights)
+        ffn_bufs.append(jnp.concatenate([w_gate[:, cut], w_up[:, cut], w_down[cut, :].T], axis=1))
+    job_first = rounds.add(net.gather_weights(ffn_bufs[0]), 4)
     (x_bf,) = rounds.pump(x_bf)
     g_own, x_bf = lax.optimization_barrier((net.to_local(cotangent), x_bf))
     g_steps = Steps(net.gather_rows(g_own))
@@ -688,21 +1020,15 @@
         2,
     )
     (mixed_bf,) = net.mix(g_steps, mixed_bf)
-    mixed_bf, *ffn_weights = lax.optimization_barrier((mixed_bf, *ffn_weights))
-    for chunk in range(1, CHUNKS):
-        gather_chunk(chunk, *ffn_weights)
     attn_part = dot_nt(mixed_bf, w_out_t).astype(BF16).reshape(micro, seq_len, width)
-    resid = x_own.astype(F32) + net.run(net.scatter_rows(attn_part))
-    unit_two, recip_two = unit_of(resid)
-    a2_own = (unit_two * gain_two).astype(BF16)
-    a2 = net.run(net.gather_rows(a2_own)).reshape(rows, width)
+    resid, a2, w_second = net.middle_forward(attn_part, x_own, gain_two, ffn_bufs[1])
+    (a2,) = rounds.pump(a2.reshape(rows, width))
+    w_chunks = [jnp.concatenate(job_first.value, axis=0), w_second.reshape(width, -1)]
     g_all = net.free(g_steps).reshape(rows, width)
 
-    da2, inners, w_chunks = None, [], []
-    grad_jobs = []
+    da2, inners = None, []
     for chunk in range(CHUNKS):
-        w_chunk = jnp.concatenate(ffn_jobs[chunk].value, axis=0)
-        w_chunks.append(w_chunk)
+        w_chunk = w_chunks[chunk]
         w_gu, w_down_t = w_chunk[:, : 2 * units], w_chunk[:, 2 * units :]
         gate_up = dot_nn(a2, w_gu)
         d_inner = dot_nn(g_all, w_down_t)
@@ -718,15 +1044,18 @@
         inners.append(inner)
         part_da2 = dot_nt(d_gu, w_gu)
         da2 = part_da2 if da2 is None else da2 + part_da2
-        grad_jobs.append(rounds.add(net.scatter_grads([(a2, d_gu), (g_all, inner)]), 3 if chunk == CHUNKS - 1 else 4))
-    da2, *inners = lax.optimization_barrier((da2.astype(BF16), *inners))
-    d_normed_two = net.run(net.scatter_rows(da2.reshape(micro, seq_len, width)))
+        parts = [(a2, d_gu), (g_all, inner)]
+        if chunk == 0:
+            job_grad = rounds.add(net.scatter_grads(parts), 4)
+    line = net.scatter_here(parts)
     mlp = sum(
         dot_nt(inner, w_chunk[:, 2 * units :]) for inner, w_chunk in zip(inners, w_chunks)
     )
-    d_resid = g_own.astype(F32) + norm_back(d_normed_two, unit_two, recip_two, gain_two)
-    acc_ffn_gain = jnp.sum(d_normed_two * unit_two, axis=(0, 1))
-    d_resid_all = net.run(net.gather_rows(d_resid.astype(BF16))).reshape(rows, width)
+    da2, mlp = rounds.pump(da2.astype(BF16), mlp.astype(BF16))
+    d_resid, d_resid_all, acc_ffn_gain, grad_second = net.middle_backward(
+        da2.reshape(micro, seq_len, width), g_own, resid, gain_two, line
+    )
+    (d_resid_all,) = rounds.pump(d_resid_all.reshape(rows, width))
     d_resid_all, mlp = lax.optimization_barrier((d_resid_all, mlp.astype(BF16)))
     mlp_steps = Steps(net.scatter_rows(mlp.reshape(micro, seq_len, width)))
     job_grad_out = rounds.add(net.scatter_grads([(d_resid_all, mixed_bf)]), 3)
@@ -773,7 +1102,7 @@
     )
     rounds.drain()
     grad_qkv = job_grad_qkv.value
-    grads_ffn = [job.value for job in grad_jobs]
+    grads_ffn = [job_grad.value, grad_second]
 
     def own_part(start, size):
         return lax.dynamic_slice_in_dim(sums, start + net.me * size, size, 0)

time: 710 us -> 689 us (0.970)
  Pallas kernels: 111 us -> 299 us
  waiting for transfers between devices: 172 us -> 61.8 us
  starting transfers between devices: 119 us -> 60.5 us
  other arithmetic: 84.7 us -> 67.4 us
  matrix products: 151 us -> 140 us
  local copies, waits for them, and re-layouts: 60 us -> 50.1 us
    pallas_call x0 -> x2, Pallas kernels: none -> 188 us  [middle_call(): pl.pallas_call(body, out_shape=outputs, in_specs=[vmem] * (len(operands)...]
    ppermute x49 -> x23, waiting for transfers between devices: 114 us -> 45 us  [step(): lax.ppermute(array, 'dp', perm)]
    ppermute x49 -> x23, starting transfers between devices: 86.2 us -> 41.5 us  [step(): lax.ppermute(array, 'dp', perm)]
    ppermute x4 -> x2, waiting for transfers between devices: 16.2 us -> 2.5 us  [scatter_rows(): lax.ppermute(add_rounded(second[1], near_second[1]), 'tensor', XNEXT)]
    unnamed x237 -> x164, local copies, waits for them, and re-layouts: 35.8 us -> 26.8 us
    ppermute x3 -> x1, waiting for transfers between devices: 8.26 us -> 0.01 us  [gather_rows(): lax.ppermute(near_y[1], 'tensor', XNEXT)]
    ppermute x4 -> x2, waiting for transfers between devices: 15.2 us -> 7.21 us  [scatter_rows(): lax.ppermute(jnp.stack([first[1], first[3]]), 'tensor', XNEXT)]
    dot_general x8 -> x6, matrix products: 48.8 us -> 42.1 us  [dot_nn(): return jnp.dot(left, right, preferred_element_type=F32)]
  transfers between devices with their start and end apart: 93 -> 47, of which waited for: 36 -> 12; matrix products, arithmetic and copies ran while one was open for 37% -> 26% of each run, Pallas kernels for 7% -> 34%
where the time goes in v4:
time: 689 us; the launch traced here: 681 us
  Pallas kernels  299 us (43%)
  matrix products  140 us (20%)
  other arithmetic  67.4 us (10%)
  waiting for transfers between devices  61.8 us (9%)
  starting transfers between devices  60.5 us (9%)
  local copies, waits for them, and re-layouts  50.1 us (7%)
    pallas_call x2, Pallas kernels, middle_call(): pl.pallas_call(body, out_shape=outputs, in_specs=[vmem] * (len(operands)...  188 us
    pallas_call x1, Pallas kernels, first_gathers(): pl.pallas_call(first_gathers, out_shape=(jax.ShapeDtypeStruct((micro, 4,...  59.1 us
    dot_general x12, matrix products, dot_tn(): lax.dot_general(left, right, (((0,), (0,)), ((), ())), preferred_element_...  50 us
    dot_general x6, matrix products, dot_nt(): lax.dot_general(left, right, (((1,), (1,)), ((), ())), preferred_element_...  48.2 us
    ppermute x23, waiting for transfers between devices, step(): lax.ppermute(array, 'dp', perm)  45 us
    dot_general x6, matrix products, dot_nn(): return jnp.dot(left, right, preferred_element_type=F32)  42.1 us
    ppermute x23, starting transfers between devices, step(): lax.ppermute(array, 'dp', perm)  41.5 us
    pallas_call x2, Pallas kernels, attention_call(): pl.pallas_call(functools.partial(body, heads_q, heads_kv), out_shape=out_...  40.9 us
  transfers between devices with their start and end apart: 47, of which 12 were waited for; matrix products, arithmetic and copies ran while one was open for 26% of the time, Pallas kernels for 34%

profile of v4, /device:TPU:8, one launch (start us, length us, event | category | flops | bytes accessed | tf_op | source)
XLA Modules:
  0.0 681.0 jit_solution(4658817658045749554)
XLA Ops:
  9.1 59.1 %shard_map.274 = (bf16[2,4,128,2048]{3,2,1,0:T(8,128)(2,1)}, bf16[8,256,1024]{2,1,0:T(8,128)(2,1)}, bf16[8,256,512]{2,1,0:T(8,128)(2,1)}, bf16[8,16,128]{2,1,0:T(8,128)(2,1)}) custom-call(bf16[2,128,2048]{2,1,0:T(8,128)(2,1)} %shard_map.273.x_ref, bf16[256,1024]{1,0:T(8,128)(2,1)} %pad_maximum_fusion.15.qkv_ref, bf16[256,512]{1,0:T(8,128)(2,1)} %bitcast.154, ...), custom_call_target="tpu_custom_call" | custom-call | tf_op jit(solution)/shard_map/pallas_call | solution.py:803
  99.9 6.0 fusion.114.qkv_ref
  105.9 4.9 collective-permute-done.2
  126.1 20.6 %shard_map.276 = bf16[1024,512]{1,0:T(8,128)(2,1)} custom-call(f32[1024,1024]{1,0:T(8,128)} %fusion.114.qkv_ref, f32[1024,128]{1,0:T(8,128)} %pad_maximum_fusion.16.cos_ref, f32[1024,128]{1,0:T(8,128)} %pad_maximum_fusion.17.sin_ref, s32[1024,3]{1,0:T(8,128)} %copy.66.col_ref, s32[2,3,512]{2,1,0:T(4,128)} %pad_add_fusion.1.row_ref, ...), custom_call_target="tpu_custom_call" | custom-call | flops 1073741824 | bytes 8388608 | tf_op jit(solution)/shard_map/pallas_call | solution.py:171
  160.9 95.6 %shard_map.277 = (f32[2,128,2048]{2,1,0:T(8,128)}, bf16[2,4,128,2048]{3,2,1,0:T(8,128)(2,1)}, bf16[8,256,2304]{2,1,0:T(8,128)(2,1)}) custom-call(bf16[2,512,2048]{2,1,0:T(8,128)(2,1)} %bitcast.146, bf16[2,128,2048]{2,1,0:T(8,128)(2,1)} %shard_map.273.x_ref, f32[1,2048]{1,0:T(1,128)} %bitcast.160, bf16[256,2304]{1,0:T(8,128)(2,1)} %pad_maximum_fusion.7.buf_ref), custom_call_target="tpu_custom_call" | custom-call | tf_op jit(solution)/shard_map/pallas_call | solution.py:820
  270.8 8.8 %fusion.11 = f32[1024,1536]{0,1:T(8,128)S(1)} fusion(bf16[1024,2048]{1,0:T(8,128)(2,1)S(1)} %bitcast.183, bf16[2048,2304]{0,1:T(8,128)(2,1)} %constant_dynamic-update-slice_fusion), kind=kOutput, calls=%fused_computation.20 | convolution fusion | flops 6442450944 | bytes 16777216 | tf_op jit(solution)/shard_map/dot_general | solution.py:34
  279.6 6.5 multiply_convert_fusion.5
  286.2 5.9 convolution_convert_fusion.2
  295.7 6.6 fusion.7
  315.1 6.7 add_convert_fusion.3
  324.0 7.8 %multiply_convert_fusion.2 = (bf16[1024,768]{0,1:T(8,128)(2,1)S(1)}, bf16[1024,768]{0,1:T(8,128)(2,1)S(1)}, bf16[1024,768]{0,1:T(8,128)(2,1)}) fusion(f32[1024,768]{0,1:T(8,128)S(1)} %copy-done.14, f32[1024,768]{0,1:T(8,128)S(1)} %copy-done.15, bf16[1024,2048]{1,0:T(8,128)(2,1)S(1)} %bitcast.150, bf16[2048,2304]{1,0:T(8,128)(2,1)} %bitcast.172), kind=kOutput, calls=%fused_computation.37 | convolution fusion | flops 3233021952 | bytes 18350080 | tf_op jit(solution)/shard_map/dot_general | solution.py:34
  332.1 23.3 %collective-permute-done.15 = bf16[256,2304]{1,0:T(8,128)(2,1)} collective-permute-done((bf16[256,2304]{1,0:T(8,128)(2,1)S(1)}, bf16[256,2304]{1,0:T(8,128)(2,1)}, u32[]{:S(2)}, u32[]{:S(2)}) %collective-permute-start.15) | collective-permute-done | bytes 1179680 | tf_op jit(solution)/shard_map/ppermute | solution.py:613
  355.5 6.7 convolution_convert_fusion.1
  362.2 9.0 %fusion.5 = f32[1024,2048]{1,0:T(8,128)} fusion(bf16[1024,1536]{0,1:T(8,128)(2,1)S(1)} %pad_maximum_fusion.2, bf16[2048,2304]{1,0:T(8,128)(2,1)S(1)} %bitcast.179), kind=kOutput, calls=%fused_computation.14 | convolution fusion | flops 6442450944 | bytes 17825792 | tf_op jit(solution)/shard_map/dot_general | solution.py:38
  380.2 12.8 %add_convert_fusion.1 = bf16[1024,2048]{1,0:T(8,128)(2,1)} fusion(f32[1024,2048]{1,0:T(8,128)} %fusion.5, bf16[2048,2304]{0,1:T(8,128)(2,1)} %constant_dynamic-update-slice_fusion, bf16[1024,768]{0,1:T(8,128)(2,1)} %copy-done.59, bf16[1024,768]{0,1:T(8,128)(2,1)} %copy-done.57), kind=kOutput, calls=%fused_computation.8 | convolution fusion | flops 6452936704 | bytes 22020096 | tf_op jit(solution)/shard_map/dot_general | solution.py:38
  393.0 9.2 %fusion.17 = f32[1024,2048]{1,0:T(8,128)} fusion(bf16[1024,768]{0,1:T(8,128)(2,1)} %get-tuple-element.124, bf16[2048,2304]{1,0:T(8,128)(2,1)} %bitcast.173), kind=kOutput, calls=%fused_computation.45 | convolution fusion | flops 3221225472 | bytes 13107200 | tf_op jit(solution)/shard_map/dot_general | solution.py:38
  402.3 8.2 %add_convert_fusion = bf16[1024,2048]{1,0:T(8,128)(2,1)} fusion(f32[1024,2048]{1,0:T(8,128)} %fusion.17, bf16[1024,768]{0,1:T(8,128)(2,1)S(1)} %copy-done.66, bf16[2048,2304]{0,1:T(8,128)(2,1)} %constant_dynamic-update-slice_fusion), kind=kOutput, calls=%fused_computation.7 | convolution fusion | flops 3225419776 | bytes 17301504 | tf_op jit(solution)/shard_map/dot_general | solution.py:38
  421.5 5.4 add_convert_fusion.2
  429.4 92.1 %shard_map.278 = (f32[2,128,2048]{2,1,0:T(8,128)}, bf16[2,4,128,2048]{3,2,1,0:T(8,128)(2,1)}, f32[1,2048]{1,0:T(1,128)}, f32[256,2304]{1,0:T(8,128)}) custom-call(bf16[2,512,2048]{2,1,0:T(8,128)(2,1)} %bitcast.153, bf16[2,128,2048]{2,1,0:T(8,128)(2,1)} %shard_map.275.g_ref, f32[2,128,2048]{2,1,0:T(8,128)} %get-tuple-element.110.resid_ref, ...), custom_call_target="tpu_custom_call" | custom-call | tf_op jit(solution)/shard_map/pallas_call | solution.py:820
  521.5 6.3 convolution_convert_fusion.3.grad_ref
  540.3 20.3 %shard_map.279 = (bf16[1024,1024]{1,0:T(8,128)(2,1)}, f32[2,2,128]{2,1,0:T(2,128)}) custom-call(f32[1024,1024]{1,0:T(8,128)} %fusion.114.qkv_ref, bf16[1024,512]{1,0:T(8,128)(2,1)} %convolution_convert_fusion.3.grad_ref, f32[1024,128]{1,0:T(8,128)} %pad_maximum_fusion.16.cos_ref, f32[1024,128]{1,0:T(8,128)} %pad_maximum_fusion.17.sin_ref, ...), custom_call_target="tpu_custom_call" | custom-call | flops 2684354560 | bytes 10485760 | tf_op jit(solution)/shard_map/pallas_call | solution.py:171
  577.2 7.0 %collective-permute-done.27 = bf16[256,512]{1,0:T(8,128)(2,1)S(1)} collective-permute-done((bf16[256,512]{1,0:T(8,128)(2,1)S(1)}, bf16[256,512]{1,0:T(8,128)(2,1)S(1)}, u32[]{:S(2)}, u32[]{:S(2)}) %collective-permute-start.27) | collective-permute-done | bytes 262176 | tf_op jit(solution)/shard_map/ppermute | solution.py:613
  588.3 4.5 fusion.115
  626.0 7.2 %collective-permute-done.30 = bf16[2,128,2048]{2,1,0:T(8,128)(2,1)S(1)} collective-permute-done((bf16[2,128,2048]{2,1,0:T(8,128)(2,1)S(1)}, bf16[2,128,2048]{2,1,0:T(8,128)(2,1)S(1)}, u32[]{:S(2)}, u32[]{:S(2)}) %collective-permute-start.30) | collective-permute-done | bytes 1048608 | tf_op jit(solution)/shard_map/ppermute | solution.py:908
  (378 shorter events, 238.0 us)
Async XLA Ops:
  71.0 35.0 %collective-permute-start.1 = (bf16[2,128,2048]{2,1,0:T(8,128)(2,1)}, bf16[2,128,2048]{2,1,0:T(8,128)(2,1)S(1)}, u32[]{:S(2)}, u32[]{:S(2)}) collective-permute-start(bf16[2,128,2048]{2,1,0:T(8,128)(2,1)} %shard_map.275.g_ref), channel_id=1, source_target_pairs={{0,2},{1,3},{2,0},{3,1},{4,6},{5,7},{6,4},{7,5},{8,10},{9,11},{10,... | collective-permute-start | bytes 3145736 | tf_op jit(solution)/shard_map/ppermute | solution.py:897
  72.5 33.4 %collective-permute-start = (bf16[2,128,2048]{2,1,0:T(8,128)(2,1)}, bf16[2,128,2048]{2,1,0:T(8,128)(2,1)S(1)}, u32[]{:S(2)}, u32[]{:S(2)}) collective-permute-start(bf16[2,128,2048]{2,1,0:T(8,128)(2,1)} %shard_map.275.g_ref), channel_id=1, source_target_pairs={{0,1},{1,0},{2,3},{3,2},{4,5},{5,4},{6,7},{7,6},{8,9},{9,8},{10,11... | collective-permute-start | bytes 3145736 | tf_op jit(solution)/shard_map/ppermute | solution.py:896
  83.0 27.9 %collective-permute-start.2 = (bf16[256,2304]{0,1:T(8,128)(2,1)}, bf16[256,2304]{0,1:T(8,128)(2,1)}, u32[]{:S(2)}, u32[]{:S(2)}) collective-permute-start(bf16[256,2304]{0,1:T(8,128)(2,1)} %get-tuple-element.99), channel_id=1, source_target_pairs={{0,8},{4,12},{8,0},{12,4},{16,24},{20,28},{24,16},{28,20},{1,9},{5... | collective-permute-start | bytes 3538952 | tf_op jit(solution)/shard_map/ppermute | solution.py:613
  85.4 28.8 %collective-permute-start.3 = (bf16[256,2304]{0,1:T(8,128)(2,1)}, bf16[256,2304]{0,1:T(8,128)(2,1)}, u32[]{:S(2)}, u32[]{:S(2)}) collective-permute-start(bf16[256,2304]{0,1:T(8,128)(2,1)} %get-tuple-element.99), channel_id=1, source_target_pairs={{8,16},{12,20},{16,8},{20,12},{9,17},{13,21},{17,9},{21,13},{10,18... | collective-permute-start | bytes 3538952 | tf_op jit(solution)/shard_map/ppermute | solution.py:613
  87.4 26.9 %collective-permute-start.4 = (bf16[256,2304]{0,1:T(8,128)(2,1)}, bf16[256,2304]{0,1:T(8,128)(2,1)}, u32[]{:S(2)}, u32[]{:S(2)}) collective-permute-start(bf16[256,2304]{0,1:T(8,128)(2,1)} %get-tuple-element.99), channel_id=1, source_target_pairs={{0,4},{4,0},{8,12},{12,8},{16,20},{20,16},{24,28},{28,24},{1,5},{5... | collective-permute-start | bytes 3538952 | tf_op jit(solution)/shard_map/ppermute | solution.py:613
  114.2 35.0 %collective-permute-start.9 = (bf16[256,2304]{0,1:T(8,128)(2,1)}, bf16[256,2304]{0,1:T(8,128)(2,1)}, u32[]{:S(2)}, u32[]{:S(2)}) collective-permute-start(bf16[256,2304]{0,1:T(8,128)(2,1)} %collective-permute-done.2), channel_id=1, source_target_pairs={{0,4},{4,0},{8,12},{12,8},{16,20},{20,16},{24,28},{28,24},{1,5},{5... | collective-permute-start | bytes 3538952 | tf_op jit(solution)/shard_map/ppermute | solution.py:613
  114.2 35.0 %collective-permute-start.7 = (bf16[256,2304]{0,1:T(8,128)(2,1)}, bf16[256,2304]{0,1:T(8,128)(2,1)}, u32[]{:S(2)}, u32[]{:S(2)}) collective-permute-start(bf16[256,2304]{0,1:T(8,128)(2,1)} %collective-permute-done.2), channel_id=1, source_target_pairs={{8,16},{12,20},{16,8},{20,12},{9,17},{13,21},{17,9},{21,13},{10,18... | collective-permute-start | bytes 3538952 | tf_op jit(solution)/shard_map/ppermute | solution.py:613
  116.4 32.8 %collective-permute-start.8 = (bf16[256,2304]{0,1:T(8,128)(2,1)}, bf16[256,2304]{0,1:T(8,128)(2,1)}, u32[]{:S(2)}, u32[]{:S(2)}) collective-permute-start(bf16[256,2304]{0,1:T(8,128)(2,1)} %collective-permute-done.3), channel_id=1, source_target_pairs={{8,0},{12,4},{16,24},{20,28},{9,1},{13,5},{17,25},{21,29},{10,2},{... | collective-permute-start | bytes 3538952 | tf_op jit(solution)/shard_map/ppermute | solution.py:613
  119.9 29.3 %collective-permute-start.6 = (bf16[128,2048]{1,0:T(8,128)(2,1)}, bf16[128,2048]{1,0:T(8,128)(2,1)}, u32[]{:S(2)}, u32[]{:S(2)}) collective-permute-start(bf16[128,2048]{1,0:T(8,128)(2,1)} %slice_bitcast_fusion.12), channel_id=1, source_target_pairs={{0,1},{1,0},{2,3},{3,2},{4,5},{5,4},{6,7},{7,6},{8,9},{9,8},{10,11... | collective-permute-start | bytes 1572872 | tf_op jit(solution)/shard_map/ppermute | solution.py:901
  121.5 27.7 %collective-permute-start.5 = (bf16[128,2048]{1,0:T(8,128)(2,1)}, bf16[128,2048]{1,0:T(8,128)(2,1)}, u32[]{:S(2)}, u32[]{:S(2)}) collective-permute-start(bf16[128,2048]{1,0:T(8,128)(2,1)} %slice_bitcast_fusion.13), channel_id=1, source_target_pairs={{0,2},{1,3},{2,0},{3,1},{4,6},{5,7},{6,4},{7,5},{8,10},{9,11},{10,... | collective-permute-start | bytes 1572872 | tf_op jit(solution)/shard_map/ppermute | solution.py:900
  149.3 107.3 %collective-permute-start.10 = (bf16[256,2304]{0,1:T(8,128)(2,1)}, bf16[256,2304]{0,1:T(8,128)(2,1)}, u32[]{:S(2)}, u32[]{:S(2)}) collective-permute-start(bf16[256,2304]{0,1:T(8,128)(2,1)} %collective-permute-done.7), channel_id=1, source_target_pairs={{8,0},{12,4},{16,24},{20,28},{9,1},{13,5},{17,25},{21,29},{10,2},{... | collective-permute-start | bytes 3538952 | tf_op jit(solution)/shard_map/ppermute | solution.py:613
  154.8 101.8 %collective-permute-start.11 = (bf16[256,2304]{0,1:T(8,128)(2,1)}, bf16[256,2304]{0,1:T(8,128)(2,1)}, u32[]{:S(2)}, u32[]{:S(2)}) collective-permute-start(bf16[256,2304]{0,1:T(8,128)(2,1)} %get-tuple-element.209), channel_id=1, source_target_pairs={{0,4},{4,0},{8,12},{12,8},{16,20},{20,16},{24,28},{28,24},{1,5},{5... | collective-permute-start | bytes 3538952 | tf_op jit(solution)/shard_map/ppermute | solution.py:613
  321.9 33.5 %collective-permute-start.15 = (bf16[256,2304]{1,0:T(8,128)(2,1)S(1)}, bf16[256,2304]{1,0:T(8,128)(2,1)}, u32[]{:S(2)}, u32[]{:S(2)}) collective-permute-start(bf16[256,2304]{1,0:T(8,128)(2,1)S(1)} %fusion.74), channel_id=1, source_target_pairs={{0,8},{4,12},{24,16},{28,20},{1,9},{5,13},{25,17},{29,21},{2,10},{... | collective-permute-start | bytes 3538952 | tf_op jit(solution)/shard_map/ppermute | solution.py:613
  372.9 37.6 %collective-permute-start.17 = (bf16[256,2304]{1,0:T(8,128)(2,1)S(1)}, bf16[256,2304]{1,0:T(8,128)(2,1)S(1)}, u32[]{:S(2)}, u32[]{:S(2)}) collective-permute-start(bf16[256,2304]{1,0:T(8,128)(2,1)S(1)} %get-tuple-element.204), channel_id=1, source_target_pairs={{8,16},{12,20},{16,8},{20,12},{9,17},{13,21},{17,9},{21,13},{10,18... | collective-permute-start | bytes 3538952 | tf_op jit(solution)/shard_map/ppermute | solution.py:613
  375.3 35.2 %collective-permute-start.16 = (bf16[256,2304]{1,0:T(8,128)(2,1)S(1)}, bf16[256,2304]{1,0:T(8,128)(2,1)S(1)}, u32[]{:S(2)}, u32[]{:S(2)}) collective-permute-start(bf16[256,2304]{1,0:T(8,128)(2,1)S(1)} %get-tuple-element.205), channel_id=1, source_target_pairs={{0,8},{4,12},{24,16},{28,20},{1,9},{5,13},{25,17},{29,21},{2,10},{... | collective-permute-start | bytes 3538952 | tf_op jit(solution)/shard_map/ppermute | solution.py:613
  379.7 39.9 %collective-permute-start.19 = (bf16[1024,768]{1,0:T(8,128)(2,1)}, bf16[1024,768]{1,0:T(8,128)(2,1)S(1)}, u32[]{:S(2)}, u32[]{:S(2)}) collective-permute-start(bf16[1024,768]{1,0:T(8,128)(2,1)} %fusion.59), channel_id=1, source_target_pairs={{0,4},{4,0},{8,12},{12,8},{16,20},{20,16},{24,28},{28,24},{1,5},{5... | collective-permute-start | bytes 4718600 | tf_op jit(solution)/shard_map/ppermute | solution.py:874
  379.7 41.8 %collective-permute-start.18 = (bf16[1024,1536]{1,0:T(8,128)(2,1)}, bf16[1024,1536]{1,0:T(8,128)(2,1)}, u32[]{:S(2)}, u32[]{:S(2)}) collective-permute-start(bf16[1024,1536]{1,0:T(8,128)(2,1)} %convolution_convert_fusion.1), channel_id=1, source_target_pairs={{0,4},{4,0},{8,12},{12,8},{16,20},{20,16},{24,28},{28,24},{1,5},{5... | collective-permute-start | bytes 9437192 | tf_op jit(solution)/shard_map/ppermute | solution.py:874
  411.8 109.6 %collective-permute-start.21 = (bf16[256,2304]{1,0:T(8,128)(2,1)}, bf16[256,2304]{1,0:T(8,128)(2,1)}, u32[]{:S(2)}, u32[]{:S(2)}) collective-permute-start(bf16[256,2304]{1,0:T(8,128)(2,1)} %add_convert_fusion.7), channel_id=1, source_target_pairs={{0,8},{4,12},{8,0},{12,4},{16,24},{20,28},{24,16},{28,20},{1,9},{5... | collective-permute-start | bytes 3538952 | tf_op jit(solution)/shard_map/ppermute | solution.py:613
  415.9 105.6 %collective-permute-start.20 = (bf16[256,2304]{1,0:T(8,128)(2,1)}, bf16[256,2304]{1,0:T(8,128)(2,1)}, u32[]{:S(2)}, u32[]{:S(2)}) collective-permute-start(bf16[256,2304]{1,0:T(8,128)(2,1)} %add_convert_fusion.8), channel_id=1, source_target_pairs={{8,16},{12,20},{16,8},{20,12},{9,17},{13,21},{17,9},{21,13},{10,18... | collective-permute-start | bytes 3538952 | tf_op jit(solution)/shard_map/ppermute | solution.py:613
  533.2 37.1 %collective-permute-start.26 = (bf16[1024,512]{1,0:T(8,128)(2,1)}, bf16[1024,512]{1,0:T(8,128)(2,1)}, u32[]{:S(2)}, u32[]{:S(2)}) collective-permute-start(bf16[1024,512]{1,0:T(8,128)(2,1)} %fusion.68), channel_id=1, source_target_pairs={{0,4},{4,0},{8,12},{12,8},{16,20},{20,16},{24,28},{28,24},{1,5},{5... | collective-permute-start | bytes 3145736 | tf_op jit(solution)/shard_map/ppermute | solution.py:883
  535.9 30.3 %collective-permute-start.22 = (bf16[2,128,2048]{2,1,0:T(8,128)(2,1)}, bf16[2,128,2048]{2,1,0:T(8,128)(2,1)}, u32[]{:S(2)}, u32[]{:S(2)}) collective-permute-start(bf16[2,128,2048]{2,1,0:T(8,128)(2,1)} %pad_maximum_fusion.8), channel_id=1, source_target_pairs={{0,1},{1,0},{2,3},{3,2},{4,5},{5,4},{6,7},{7,6},{8,9},{9,8},{10,11... | collective-permute-start | bytes 3145736 | tf_op jit(solution)/shard_map/ppermute | solution.py:908
  537.5 28.7 %collective-permute-start.24 = (bf16[2,128,2048]{2,1,0:T(8,128)(2,1)}, bf16[2,128,2048]{2,1,0:T(8,128)(2,1)}, u32[]{:S(2)}, u32[]{:S(2)}) collective-permute-start(bf16[2,128,2048]{2,1,0:T(8,128)(2,1)} %pad_maximum_fusion.9), channel_id=1, source_target_pairs={{0,2},{1,3},{2,0},{3,1},{4,6},{5,7},{6,4},{7,5},{8,10},{9,11},{10,... | collective-permute-start | bytes 3145736 | tf_op jit(solution)/shard_map/ppermute | solution.py:909
  621.8 28.2 %collective-permute-start.44 = (f32[4352]{0:T(1024)S(1)}, f32[4352]{0:T(1024)S(1)}, u32[]{:S(2)}, u32[]{:S(2)}) collective-permute-start(f32[4352]{0:T(1024)S(1)} %add.221), channel_id=1, source_target_pairs={{0,16},{4,20},{8,24},{12,28},{16,0},{20,4},{24,8},{28,12},{1,17},{... | collective-permute-start | bytes 52232 | tf_op jit(solution)/shard_map/ppermute | solution.py:787
  624.7 30.5 %collective-permute-start.38 = (bf16[256,1024]{1,0:T(8,128)(2,1)}, bf16[256,1024]{1,0:T(8,128)(2,1)}, u32[]{:S(2)}, u32[]{:S(2)}) collective-permute-start(bf16[256,1024]{1,0:T(8,128)(2,1)} %get-tuple-element.244), channel_id=1, source_target_pairs={{0,8},{4,12},{24,16},{28,20},{1,9},{5,13},{25,17},{29,21},{2,10},{... | collective-permute-start | bytes 1572872 | tf_op jit(solution)/shard_map/ppermute | solution.py:613
  (99 other events, 1115.1 us)

commit v5 on v4

--- a/solution.py
+++ b/solution.py
@@ -11,7 +11,7 @@
 HEAD_SIZE = 128
 EPS = 1e-06
 THETA = 1000000.0
-CHUNKS = 2
+CHUNKS = 3
 F32 = jnp.float32
 BF16 = jnp.bfloat16
 
@@ -728,6 +728,10 @@
         rows = self.free(self.gather_rows(total.astype(BF16)))
         return total, rows, jnp.sum(upstream * unit, axis=(0, 1)), line
 
+    def scatter_line(self, summed):
+        return summed
+        yield
+
     def scatter_here(self, parts):
         job = Job(self.scatter_grads(parts), 0)
         job.step(None)
@@ -876,14 +880,10 @@
         return jnp.concatenate(summed, axis=1)
 
     def scatter_grads(self, parts):
-        away, half = [], parts[0][0].shape[1] // 2
-        for left, right in parts:
-            away.append(dot_tn(left[:, half:], right).astype(BF16))
-        summed = [
-            (dot_tn(left[:, :half], right) + lax.ppermute(array, "dp", CORE).astype(F32)).astype(BF16)
-            for (left, right), array in zip(parts, away)
-        ]
-        own, pair, two, three = jnp.split(jnp.concatenate(summed, axis=1), 4, axis=0)
+        return self.scatter_line(self.scatter_here(parts))
+
+    def scatter_line(self, summed):
+        own, pair, two, three = jnp.split(summed, 4, axis=0)
         (got,) = yield [(three, INWARD)]
         two_sum = add_rounded(two, got)
         got, got_inner = yield [(two, INWARD), (two_sum, INNER)]
@@ -1022,12 +1022,15 @@
     (mixed_bf,) = net.mix(g_steps, mixed_bf)
     attn_part = dot_nt(mixed_bf, w_out_t).astype(BF16).reshape(micro, seq_len, width)
     resid, a2, w_second = net.middle_forward(attn_part, x_own, gain_two, ffn_bufs[1])
+    job_third = rounds.add(net.gather_weights(ffn_bufs[2]), 4)
     (a2,) = rounds.pump(a2.reshape(rows, width))
     w_chunks = [jnp.concatenate(job_first.value, axis=0), w_second.reshape(width, -1)]
     g_all = net.free(g_steps).reshape(rows, width)
 
-    da2, inners = None, []
+    da2, inners, grad_jobs = None, [], []
     for chunk in range(CHUNKS):
+        if chunk == 2:
+            w_chunks.append(jnp.concatenate(job_third.value, axis=0))
         w_chunk = w_chunks[chunk]
         w_gu, w_down_t = w_chunk[:, : 2 * units], w_chunk[:, 2 * units :]
         gate_up = dot_nn(a2, w_gu)
@@ -1045,22 +1048,25 @@
         part_da2 = dot_nt(d_gu, w_gu)
         da2 = part_da2 if da2 is None else da2 + part_da2
         parts = [(a2, d_gu), (g_all, inner)]
-        if chunk == 0:
-            job_grad = rounds.add(net.scatter_grads(parts), 4)
+        if chunk < 2:
+            grad_jobs.append(rounds.add(net.scatter_grads(parts), 4))
     line = net.scatter_here(parts)
     mlp = sum(
         dot_nt(inner, w_chunk[:, 2 * units :]) for inner, w_chunk in zip(inners, w_chunks)
     )
     da2, mlp = rounds.pump(da2.astype(BF16), mlp.astype(BF16))
-    d_resid, d_resid_all, acc_ffn_gain, grad_second = net.middle_backward(
+    d_resid, d_resid_all, acc_ffn_gain, grad_third = net.middle_backward(
         da2.reshape(micro, seq_len, width), g_own, resid, gain_two, line
     )
     (d_resid_all,) = rounds.pump(d_resid_all.reshape(rows, width))
     d_resid_all, mlp = lax.optimization_barrier((d_resid_all, mlp.astype(BF16)))
     mlp_steps = Steps(net.scatter_rows(mlp.reshape(micro, seq_len, width)))
-    job_grad_out = rounds.add(net.scatter_grads([(d_resid_all, mixed_bf)]), 3)
-
-    (d_mixed,) = net.mix(mlp_steps, dot_nn(d_resid_all, w_out_t).astype(BF16))
+    line_out = net.scatter_here([(d_resid_all, mixed_bf)])
+    job_grad_out = rounds.add(net.scatter_line(line_out), 3)
+
+    d_mixed = dot_nn(d_resid_all, w_out_t).astype(BF16)
+    d_mixed, _ = lax.optimization_barrier((d_mixed, line_out))
+    (d_mixed,) = net.mix(mlp_steps, d_mixed)
     d_qkv, head_sums = attention_call(
         attention_backward,
         micro,
@@ -1081,8 +1087,10 @@
     acc_q_gain, acc_k_gain = jnp.sum(head_sums, axis=0)
     (d_qkv,) = net.mix(mlp_steps, d_qkv)
     layer_out = net.from_local((resid + net.free(mlp_steps)).astype(BF16))
-    job_grad_qkv = rounds.add(net.scatter_grads([(a1, d_qkv)]), 4)
-    (da1,) = rounds.pump(dot_nt(d_qkv, w_qkv))
+    line_qkv = net.scatter_here([(a1, d_qkv)])
+    job_grad_qkv = rounds.add(net.scatter_line(line_qkv), 3)
+    da1, _ = lax.optimization_barrier((dot_nt(d_qkv, w_qkv), line_qkv))
+    (da1,) = rounds.pump(da1)
     acc_attn_gain = jnp.sum(da1 * unit_all, axis=0)
     d_normed = net.run(net.scatter_rows(da1.astype(BF16).reshape(micro, seq_len, width)))
     unit_one, recip_one = unit_of(x_own.astype(F32))
@@ -1102,7 +1110,7 @@
     )
     rounds.drain()
     grad_qkv = job_grad_qkv.value
-    grads_ffn = [job_grad.value, grad_second]
+    grads_ffn = [*(job.value for job in grad_jobs), grad_third]
 
     def own_part(start, size):
         return lax.dynamic_slice_in_dim(sums, start + net.me * size, size, 0)

time: 689 us -> 730 us (1.060)
  Pallas kernels: 299 us -> 269 us
  starting transfers between devices: 60.5 us -> 88.1 us
  matrix products: 140 us -> 164 us
  waiting for transfers between devices: 61.8 us -> 85.8 us
    ppermute x23 -> x36, waiting for transfers between devices: 45 us -> 83.4 us  [step(): lax.ppermute(array, 'dp', perm)]
    pallas_call x2, Pallas kernels: 188 us -> 158 us  [middle_call(): pl.pallas_call(body, out_shape=outputs, in_specs=[vmem] * (len(operands)...]
    ppermute x23 -> x36, starting transfers between devices: 41.5 us -> 69.3 us  [step(): lax.ppermute(array, 'dp', perm)]
    dot_general x6 -> x8, matrix products: 48.2 us -> 59.9 us  [dot_nt(): lax.dot_general(left, right, (((1,), (1,)), ((), ())), preferred_element_...]
    unnamed x164 -> x174, local copies, waits for them, and re-layouts: 26.8 us -> 19.8 us
    dot_general x6 -> x8, matrix products: 42.1 us -> 49 us  [dot_nn(): return jnp.dot(left, right, preferred_element_type=F32)]
    dot_general x12 -> x16, matrix products: 50 us -> 55.3 us  [dot_tn(): lax.dot_general(left, right, (((0,), (0,)), ((), ())), preferred_element_...]
    convert_element_type x9 -> x12, other arithmetic: 12.9 us -> 17.1 us  [add_rounded(): return (left.astype(F32) + right.astype(F32)).astype(BF16)]
  transfers between devices with their start and end apart: 47 -> 63, of which waited for: 12 -> 18; matrix products, arithmetic and copies ran while one was open for 26% -> 31% of each run, Pallas kernels for 34% -> 28%
where the time goes in v5:
time: 730 us; the launch traced here: 721 us
  Pallas kernels  269 us (37%)
  matrix products  164 us (22%)
  starting transfers between devices  88.1 us (12%)
  waiting for transfers between devices  85.8 us (12%)
  other arithmetic  67 us (9%)
  local copies, waits for them, and re-layouts  44.9 us (6%)
    pallas_call x2, Pallas kernels, middle_call(): pl.pallas_call(body, out_shape=outputs, in_specs=[vmem] * (len(operands)...  158 us
    ppermute x36, waiting for transfers between devices, step(): lax.ppermute(array, 'dp', perm)  83.4 us
    ppermute x36, starting transfers between devices, step(): lax.ppermute(array, 'dp', perm)  69.3 us
    dot_general x8, matrix products, dot_nt(): lax.dot_general(left, right, (((1,), (1,)), ((), ())), preferred_element_...  59.9 us
    pallas_call x1, Pallas kernels, first_gathers(): pl.pallas_call(first_gathers, out_shape=(jax.ShapeDtypeStruct((micro, 4,...  59.1 us
    dot_general x16, matrix products, dot_tn(): lax.dot_general(left, right, (((0,), (0,)), ((), ())), preferred_element_...  55.3 us
    dot_general x8, matrix products, dot_nn(): return jnp.dot(left, right, preferred_element_type=F32)  49 us
    pallas_call x2, Pallas kernels, attention_call(): pl.pallas_call(functools.partial(body, heads_q, heads_kv), out_shape=out_...  40.7 us
  transfers between devices with their start and end apart: 63, of which 18 were waited for; matrix products, arithmetic and copies ran while one was open for 31% of the time, Pallas kernels for 28%

profile of v5, /device:TPU:8, one launch (start us, length us, event | category | flops | bytes accessed | tf_op | source)
XLA Modules:
  0.0 721.2 jit_solution(6512645943333390270)
XLA Ops:
  8.1 59.1 %shard_map.274 = (bf16[2,4,128,2048]{3,2,1,0:T(8,128)(2,1)}, bf16[8,256,1024]{2,1,0:T(8,128)(2,1)}, bf16[8,256,512]{2,1,0:T(8,128)(2,1)}, bf16[8,16,128]{2,1,0:T(8,128)(2,1)}) custom-call(bf16[2,128,2048]{2,1,0:T(8,128)(2,1)} %shard_map.273.x_ref, bf16[256,1024]{1,0:T(8,128)(2,1)} %pad_maximum_fusion.15.qkv_ref, bf16[256,512]{1,0:T(8,128)(2,1)} %bitcast.164, ...), custom_call_target="tpu_custom_call" | custom-call | tf_op jit(solution)/shard_map/pallas_call | solution.py:807
  102.5 6.1 fusion.140.qkv_ref
  122.0 20.6 %shard_map.276 = bf16[1024,512]{1,0:T(8,128)(2,1)} custom-call(f32[1024,1024]{1,0:T(8,128)} %fusion.140.qkv_ref, f32[1024,128]{1,0:T(8,128)} %pad_maximum_fusion.16.cos_ref, f32[1024,128]{1,0:T(8,128)} %pad_maximum_fusion.17.sin_ref, s32[1024,3]{1,0:T(8,128)} %copy.82.col_ref, s32[2,3,512]{2,1,0:T(4,128)} %pad_add_fusion.1.row_ref, ...), custom_call_target="tpu_custom_call" | custom-call | flops 1073741824 | bytes 8388608 | tf_op jit(solution)/shard_map/pallas_call | solution.py:171
  154.2 78.0 %shard_map.277 = (f32[2,128,2048]{2,1,0:T(8,128)}, bf16[2,4,128,2048]{3,2,1,0:T(8,128)(2,1)}, bf16[8,256,1536]{2,1,0:T(8,128)(2,1)}) custom-call(bf16[2,512,2048]{2,1,0:T(8,128)(2,1)} %bitcast.161, bf16[2,128,2048]{2,1,0:T(8,128)(2,1)} %shard_map.273.x_ref, f32[1,2048]{1,0:T(1,128)} %bitcast.174, bf16[256,1536]{1,0:T(8,128)(2,1)} %pad_maximum_fusion.13.buf_ref), custom_call_target="tpu_custom_call" | custom-call | tf_op jit(solution)/shard_map/pallas_call | solution.py:824
  251.6 6.1 fusion.11
  257.8 6.2 fusion.15
  268.0 5.6 multiply_convert_fusion.7
  274.0 11.3 %collective-permute-done.17 = bf16[256,1536]{0,1:T(8,128)(2,1)S(1)} collective-permute-done((bf16[256,1536]{0,1:T(8,128)(2,1)S(1)}, bf16[256,1536]{0,1:T(8,128)(2,1)S(1)}, u32[]{:S(2)}, u32[]{:S(2)}) %collective-permute-start.17) | collective-permute-done | bytes 786464 | tf_op jit(solution)/shard_map/ppermute | solution.py:613
  299.8 9.0 %fusion.13 = f32[1024,2048]{1,0:T(8,128)} fusion(bf16[1024,1024]{1,0:T(8,128)(2,1)S(1)} %pad_maximum_fusion.1, bf16[2048,1536]{0,1:T(8,128)(2,1)} %copy-done.45), kind=kOutput, calls=%fused_computation.29 | convolution fusion | flops 4294967296 | bytes 14680064 | tf_op jit(solution)/shard_map/dot_general | solution.py:38
  313.0 7.0 multiply_convert_fusion.4
  331.2 6.2 fusion.7
  337.5 14.3 %collective-permute-done.23 = bf16[256,1536]{1,0:T(8,128)(2,1)S(1)} collective-permute-done((bf16[256,1536]{1,0:T(8,128)(2,1)S(1)}, bf16[256,1536]{1,0:T(8,128)(2,1)S(1)}, u32[]{:S(2)}, u32[]{:S(2)}) %collective-permute-start.23) | collective-permute-done | bytes 786464 | tf_op jit(solution)/shard_map/ppermute | solution.py:613
  354.0 7.3 %fusion.48 = f32[1024,2048]{1,0:T(8,128)} fusion(bf16[1024,512]{1,0:T(8,128)(2,1)S(1)} %copy-done.70, bf16[2048,1536]{1,0:T(8,128)(2,1)} %bitcast.183), kind=kOutput, calls=%fused_computation.91 | convolution fusion | flops 2147483648 | bytes 11534336 | tf_op jit(solution)/shard_map/dot_general | solution.py:38
  370.6 9.0 %fusion.9 = f32[1024,2048]{1,0:T(8,128)} fusion(bf16[1024,1024]{1,0:T(8,128)(2,1)S(1)} %pad_maximum_fusion.2, bf16[2048,1536]{1,0:T(8,128)(2,1)} %bitcast.184), kind=kOutput, calls=%fused_computation.25 | convolution fusion | flops 4294967296 | bytes 14680064 | tf_op jit(solution)/shard_map/dot_general | solution.py:38
  412.8 8.8 %add_convert_fusion = bf16[1024,2048]{1,0:T(8,128)(2,1)} fusion(f32[1024,2048]{1,0:T(8,128)S(1)} %fusion.52, f32[1024,2048]{1,0:T(8,128)} %fusion.48, bf16[1024,512]{1,0:T(8,128)(2,1)S(1)} %get-tuple-element.174, bf16[2048,1536]{0,1:T(8,128)(2,1)} %copy-done.26), kind=kOutput, calls=%fused_computation.7 | convolution fusion | flops 2153775104 | bytes 24117248 | tf_op jit(solution)/shard_map/dot_general | solution.py:38
  421.6 11.1 %add_convert_fusion.1 = bf16[1024,2048]{1,0:T(8,128)(2,1)} fusion(f32[1024,2048]{1,0:T(8,128)} %fusion.13, f32[1024,2048]{1,0:T(8,128)} %fusion.9, bf16[1024,1024]{1,0:T(8,128)(2,1)S(1)} %pad_maximum_fusion.3, bf16[2048,1536]{0,1:T(8,128)(2,1)} %copy-done.26), kind=kOutput, calls=%fused_computation.8 | convolution fusion | flops 4301258752 | bytes 27262976 | tf_op jit(solution)/shard_map/dot_general | solution.py:38
  444.3 15.8 %collective-permute-done.31 = bf16[256,1536]{1,0:T(8,128)(2,1)S(1)} collective-permute-done((bf16[256,1536]{1,0:T(8,128)(2,1)S(1)}, bf16[256,1536]{1,0:T(8,128)(2,1)S(1)}, u32[]{:S(2)}, u32[]{:S(2)}) %collective-permute-start.31) | collective-permute-done | bytes 786464 | tf_op jit(solution)/shard_map/ppermute | solution.py:613
  471.2 79.9 %shard_map.278 = (f32[2,128,2048]{2,1,0:T(8,128)}, bf16[2,4,128,2048]{3,2,1,0:T(8,128)(2,1)}, f32[1,2048]{1,0:T(1,128)}, f32[256,1536]{1,0:T(8,128)}) custom-call(bf16[2,512,2048]{2,1,0:T(8,128)(2,1)} %bitcast.160, bf16[2,128,2048]{2,1,0:T(8,128)(2,1)} %shard_map.275.g_ref, f32[2,128,2048]{2,1,0:T(8,128)} %get-tuple-element.139.resid_ref, ...), custom_call_target="tpu_custom_call" | custom-call | tf_op jit(solution)/shard_map/pallas_call | solution.py:824
  551.1 6.3 convolution_convert_fusion.4.grad_ref
  582.2 7.6 %collective-permute-done.40 = bf16[256,1536]{1,0:T(8,128)(2,1)} collective-permute-done((bf16[256,1536]{1,0:T(8,128)(2,1)}, bf16[256,1536]{1,0:T(8,128)(2,1)}, u32[]{:S(2)}, u32[]{:S(2)}) %collective-permute-start.40) | collective-permute-done | bytes 786464 | tf_op jit(solution)/shard_map/ppermute | solution.py:613
  601.6 20.1 %shard_map.279 = (bf16[1024,1024]{1,0:T(8,128)(2,1)}, f32[2,2,128]{2,1,0:T(2,128)}) custom-call(f32[1024,1024]{1,0:T(8,128)} %fusion.140.qkv_ref, bf16[1024,512]{1,0:T(8,128)(2,1)} %convolution_convert_fusion.4.grad_ref, f32[1024,128]{1,0:T(8,128)} %pad_maximum_fusion.16.cos_ref, f32[1024,128]{1,0:T(8,128)} %pad_maximum_fusion.17.sin_ref, ...), custom_call_target="tpu_custom_call" | custom-call | flops 2684354560 | bytes 10485760 | tf_op jit(solution)/shard_map/pallas_call | solution.py:171
  621.8 6.0 fusion.39
  636.2 6.4 fusion.141
  675.4 7.6 %collective-permute-done.51 = bf16[256,1024]{1,0:T(8,128)(2,1)S(1)} collective-permute-done((bf16[256,1024]{1,0:T(8,128)(2,1)S(1)}, bf16[256,1024]{1,0:T(8,128)(2,1)S(1)}, u32[]{:S(2)}, u32[]{:S(2)}) %collective-permute-start.51) | collective-permute-done | bytes 524320 | tf_op jit(solution)/shard_map/ppermute | solution.py:613
  (437 shorter events, 303.5 us)
Async XLA Ops:
  69.9 38.7 %collective-permute-start.1 = (bf16[2,128,2048]{2,1,0:T(8,128)(2,1)}, bf16[2,128,2048]{2,1,0:T(8,128)(2,1)S(1)}, u32[]{:S(2)}, u32[]{:S(2)}) collective-permute-start(bf16[2,128,2048]{2,1,0:T(8,128)(2,1)} %shard_map.275.g_ref), channel_id=1, source_target_pairs={{0,2},{1,3},{2,0},{3,1},{4,6},{5,7},{6,4},{7,5},{8,10},{9,11},{10,... | collective-permute-start | bytes 3145736 | tf_op jit(solution)/shard_map/ppermute | solution.py:897
  71.4 37.2 %collective-permute-start = (bf16[2,128,2048]{2,1,0:T(8,128)(2,1)}, bf16[2,128,2048]{2,1,0:T(8,128)(2,1)S(1)}, u32[]{:S(2)}, u32[]{:S(2)}) collective-permute-start(bf16[2,128,2048]{2,1,0:T(8,128)(2,1)} %shard_map.275.g_ref), channel_id=1, source_target_pairs={{0,1},{1,0},{2,3},{3,2},{4,5},{5,4},{6,7},{7,6},{8,9},{9,8},{10,11... | collective-permute-start | bytes 3145736 | tf_op jit(solution)/shard_map/ppermute | solution.py:896
  108.6 36.4 %collective-permute-start.9 = (bf16[256,1536]{0,1:T(8,128)(2,1)}, bf16[256,1536]{0,1:T(8,128)(2,1)}, u32[]{:S(2)}, u32[]{:S(2)}) collective-permute-start(bf16[256,1536]{0,1:T(8,128)(2,1)} %collective-permute-done.2), channel_id=1, source_target_pairs={{0,4},{4,0},{8,12},{12,8},{16,20},{20,16},{24,28},{28,24},{1,5},{5... | collective-permute-start | bytes 2359304 | tf_op jit(solution)/shard_map/ppermute | solution.py:613
  109.1 35.8 %collective-permute-start.7 = (bf16[256,1536]{0,1:T(8,128)(2,1)}, bf16[256,1536]{0,1:T(8,128)(2,1)}, u32[]{:S(2)}, u32[]{:S(2)}) collective-permute-start(bf16[256,1536]{0,1:T(8,128)(2,1)} %collective-permute-done.2), channel_id=1, source_target_pairs={{8,16},{12,20},{16,8},{20,12},{9,17},{13,21},{17,9},{21,13},{10,18... | collective-permute-start | bytes 2359304 | tf_op jit(solution)/shard_map/ppermute | solution.py:613
  113.9 31.0 %collective-permute-start.8 = (bf16[256,1536]{0,1:T(8,128)(2,1)}, bf16[256,1536]{0,1:T(8,128)(2,1)}, u32[]{:S(2)}, u32[]{:S(2)}) collective-permute-start(bf16[256,1536]{0,1:T(8,128)(2,1)} %collective-permute-done.3), channel_id=1, source_target_pairs={{8,0},{12,4},{16,24},{20,28},{9,1},{13,5},{17,25},{21,29},{10,2},{... | collective-permute-start | bytes 2359304 | tf_op jit(solution)/shard_map/ppermute | solution.py:613
  117.1 27.8 %collective-permute-start.6 = (bf16[128,2048]{1,0:T(8,128)(2,1)}, bf16[128,2048]{1,0:T(8,128)(2,1)}, u32[]{:S(2)}, u32[]{:S(2)}) collective-permute-start(bf16[128,2048]{1,0:T(8,128)(2,1)} %slice_bitcast_fusion.8), channel_id=1, source_target_pairs={{0,1},{1,0},{2,3},{3,2},{4,5},{5,4},{6,7},{7,6},{8,9},{9,8},{10,11... | collective-permute-start | bytes 1572872 | tf_op jit(solution)/shard_map/ppermute | solution.py:901
  117.6 27.3 %collective-permute-start.5 = (bf16[128,2048]{1,0:T(8,128)(2,1)}, bf16[128,2048]{1,0:T(8,128)(2,1)}, u32[]{:S(2)}, u32[]{:S(2)}) collective-permute-start(bf16[128,2048]{1,0:T(8,128)(2,1)} %slice_bitcast_fusion.9), channel_id=1, source_target_pairs={{0,2},{1,3},{2,0},{3,1},{4,6},{5,7},{6,4},{7,5},{8,10},{9,11},{10,... | collective-permute-start | bytes 1572872 | tf_op jit(solution)/shard_map/ppermute | solution.py:900
  145.0 88.9 %collective-permute-start.10 = (bf16[256,1536]{0,1:T(8,128)(2,1)}, bf16[256,1536]{0,1:T(8,128)(2,1)}, u32[]{:S(2)}, u32[]{:S(2)}) collective-permute-start(bf16[256,1536]{0,1:T(8,128)(2,1)} %collective-permute-done.7), channel_id=1, source_target_pairs={{8,0},{12,4},{16,24},{20,28},{9,1},{13,5},{17,25},{21,29},{10,2},{... | collective-permute-start | bytes 2359304 | tf_op jit(solution)/shard_map/ppermute | solution.py:613
  149.7 84.1 %collective-permute-start.11 = (bf16[256,1536]{0,1:T(8,128)(2,1)}, bf16[256,1536]{0,1:T(8,128)(2,1)}, u32[]{:S(2)}, u32[]{:S(2)}) collective-permute-start(bf16[256,1536]{0,1:T(8,128)(2,1)} %get-tuple-element.273), channel_id=1, source_target_pairs={{0,4},{4,0},{8,12},{12,8},{16,20},{20,16},{24,28},{28,24},{1,5},{5... | collective-permute-start | bytes 2359304 | tf_op jit(solution)/shard_map/ppermute | solution.py:613
  233.9 30.2 %collective-permute-start.13 = (bf16[256,1536]{0,1:T(8,128)(2,1)S(1)}, bf16[256,1536]{0,1:T(8,128)(2,1)S(1)}, u32[]{:S(2)}, u32[]{:S(2)}) collective-permute-start(bf16[256,1536]{0,1:T(8,128)(2,1)S(1)} %copy-done.37), channel_id=1, source_target_pairs={{0,8},{4,12},{8,0},{12,4},{16,24},{20,28},{24,16},{28,20},{1,9},{5... | collective-permute-start | bytes 2359304 | tf_op jit(solution)/shard_map/ppermute | solution.py:613
  238.6 25.4 %collective-permute-start.14 = (bf16[256,1536]{0,1:T(8,128)(2,1)S(1)}, bf16[256,1536]{0,1:T(8,128)(2,1)S(1)}, u32[]{:S(2)}, u32[]{:S(2)}) collective-permute-start(bf16[256,1536]{0,1:T(8,128)(2,1)S(1)} %copy-done.37), channel_id=1, source_target_pairs={{8,16},{12,20},{16,8},{20,12},{9,17},{13,21},{17,9},{21,13},{10,18... | collective-permute-start | bytes 2359304 | tf_op jit(solution)/shard_map/ppermute | solution.py:613
  366.2 28.7 %collective-permute-start.30 = (bf16[1024,512]{1,0:T(8,128)(2,1)}, bf16[1024,512]{1,0:T(8,128)(2,1)}, u32[]{:S(2)}, u32[]{:S(2)}) collective-permute-start(bf16[1024,512]{1,0:T(8,128)(2,1)} %fusion.79), channel_id=1, source_target_pairs={{0,4},{4,0},{8,12},{12,8},{16,20},{20,16},{24,28},{28,24},{1,5},{5... | collective-permute-start | bytes 3145736 | tf_op jit(solution)/shard_map/ppermute | solution.py:878
  370.1 62.7 %collective-permute-start.29 = (bf16[1024,1024]{1,0:T(8,128)(2,1)}, bf16[1024,1024]{1,0:T(8,128)(2,1)}, u32[]{:S(2)}, u32[]{:S(2)}) collective-permute-start(bf16[1024,1024]{1,0:T(8,128)(2,1)} %convolution_convert_fusion.2), channel_id=1, source_target_pairs={{0,4},{4,0},{8,12},{12,8},{16,20},{20,16},{24,28},{28,24},{1,5},{5... | collective-permute-start | bytes 6291464 | tf_op jit(solution)/shard_map/ppermute | solution.py:878
  408.4 32.7 %collective-permute-start.33 = (bf16[1024,512]{1,0:T(8,128)(2,1)}, bf16[1024,512]{1,0:T(8,128)(2,1)}, u32[]{:S(2)}, u32[]{:S(2)}) collective-permute-start(bf16[1024,512]{1,0:T(8,128)(2,1)} %fusion.82), channel_id=1, source_target_pairs={{0,4},{4,0},{8,12},{12,8},{16,20},{20,16},{24,28},{28,24},{1,5},{5... | collective-permute-start | bytes 3145736 | tf_op jit(solution)/shard_map/ppermute | solution.py:878
  412.8 52.4 %collective-permute-start.32 = (bf16[1024,1024]{1,0:T(8,128)(2,1)}, bf16[1024,1024]{1,0:T(8,128)(2,1)}, u32[]{:S(2)}, u32[]{:S(2)}) collective-permute-start(bf16[1024,1024]{1,0:T(8,128)(2,1)} %convolution_convert_fusion.1), channel_id=1, source_target_pairs={{0,4},{4,0},{8,12},{12,8},{16,20},{20,16},{24,28},{28,24},{1,5},{5... | collective-permute-start | bytes 6291464 | tf_op jit(solution)/shard_map/ppermute | solution.py:878
  461.5 89.6 %collective-permute-start.35 = (bf16[256,1536]{1,0:T(8,128)(2,1)}, bf16[256,1536]{1,0:T(8,128)(2,1)}, u32[]{:S(2)}, u32[]{:S(2)}) collective-permute-start(bf16[256,1536]{1,0:T(8,128)(2,1)} %get-tuple-element.262), channel_id=1, source_target_pairs={{8,16},{12,20},{16,8},{20,12},{9,17},{13,21},{17,9},{21,13},{10,18... | collective-permute-start | bytes 2359304 | tf_op jit(solution)/shard_map/ppermute | solution.py:613
  463.9 87.2 %collective-permute-start.34 = (bf16[256,1536]{1,0:T(8,128)(2,1)}, bf16[256,1536]{1,0:T(8,128)(2,1)}, u32[]{:S(2)}, u32[]{:S(2)}) collective-permute-start(bf16[256,1536]{1,0:T(8,128)(2,1)} %get-tuple-element.263), channel_id=1, source_target_pairs={{0,8},{4,12},{24,16},{28,20},{1,9},{5,13},{25,17},{29,21},{2,10},{... | collective-permute-start | bytes 2359304 | tf_op jit(solution)/shard_map/ppermute | solution.py:613
  561.1 31.4 %collective-permute-start.37 = (bf16[2,128,2048]{2,1,0:T(8,128)(2,1)}, bf16[2,128,2048]{2,1,0:T(8,128)(2,1)}, u32[]{:S(2)}, u32[]{:S(2)}) collective-permute-start(bf16[2,128,2048]{2,1,0:T(8,128)(2,1)} %pad_maximum_fusion.6), channel_id=1, source_target_pairs={{0,1},{1,0},{2,3},{3,2},{4,5},{5,4},{6,7},{7,6},{8,9},{9,8},{10,11... | collective-permute-start | bytes 3145736 | tf_op jit(solution)/shard_map/ppermute | solution.py:908
  563.6 28.8 %collective-permute-start.38 = (bf16[2,128,2048]{2,1,0:T(8,128)(2,1)}, bf16[2,128,2048]{2,1,0:T(8,128)(2,1)}, u32[]{:S(2)}, u32[]{:S(2)}) collective-permute-start(bf16[2,128,2048]{2,1,0:T(8,128)(2,1)} %pad_maximum_fusion.7), channel_id=1, source_target_pairs={{0,2},{1,3},{2,0},{3,1},{4,6},{5,7},{6,4},{7,5},{8,10},{9,11},{10,... | collective-permute-start | bytes 3145736 | tf_op jit(solution)/shard_map/ppermute | solution.py:909
  580.9 66.0 %collective-permute-start.45 = (bf16[256,512]{1,0:T(8,128)(2,1)}, bf16[256,512]{1,0:T(8,128)(2,1)}, u32[]{:S(2)}, u32[]{:S(2)}) collective-permute-start(bf16[256,512]{1,0:T(8,128)(2,1)} %get-tuple-element.318), channel_id=1, source_target_pairs={{0,8},{4,12},{24,16},{28,20},{1,9},{5,13},{25,17},{29,21},{2,10},{... | collective-permute-start | bytes 786440 | tf_op jit(solution)/shard_map/ppermute | solution.py:613
  592.4 29.3 %collective-permute-start.43 = (bf16[256,512]{1,0:T(8,128)(2,1)}, bf16[256,512]{1,0:T(8,128)(2,1)S(1)}, u32[]{:S(2)}, u32[]{:S(2)}) collective-permute-start(bf16[256,512]{1,0:T(8,128)(2,1)} %get-tuple-element.190), channel_id=1, source_target_pairs={{0,8},{4,12},{24,16},{28,20},{1,9},{5,13},{25,17},{29,21},{2,10},{... | collective-permute-start | bytes 786440 | tf_op jit(solution)/shard_map/ppermute | solution.py:613
  653.8 29.2 %collective-permute-start.47 = (bf16[2,128,2048]{2,1,0:T(8,128)(2,1)S(1)}, bf16[2,128,2048]{2,1,0:T(8,128)(2,1)S(1)}, u32[]{:S(2)}, u32[]{:S(2)}) collective-permute-start(bf16[2,128,2048]{2,1,0:T(8,128)(2,1)S(1)} %pad_maximum_fusion.8), channel_id=1, source_target_pairs={{0,1},{1,0},{2,3},{3,2},{4,5},{5,4},{6,7},{7,6},{8,9},{9,8},{10,11... | collective-permute-start | bytes 3145736 | tf_op jit(solution)/shard_map/ppermute | solution.py:908
  656.0 26.9 %collective-permute-start.48 = (bf16[2,128,2048]{2,1,0:T(8,128)(2,1)S(1)}, bf16[2,128,2048]{2,1,0:T(8,128)(2,1)S(1)}, u32[]{:S(2)}, u32[]{:S(2)}) collective-permute-start(bf16[2,128,2048]{2,1,0:T(8,128)(2,1)S(1)} %pad_maximum_fusion.9), channel_id=1, source_target_pairs={{0,2},{1,3},{2,0},{3,1},{4,6},{5,7},{6,4},{7,5},{8,10},{9,11},{10,... | collective-permute-start | bytes 3145736 | tf_op jit(solution)/shard_map/ppermute | solution.py:909
  670.0 31.1 %collective-permute-start.54 = (bf16[256,1024]{1,0:T(8,128)(2,1)}, bf16[256,1024]{1,0:T(8,128)(2,1)}, u32[]{:S(2)}, u32[]{:S(2)}) collective-permute-start(bf16[256,1024]{1,0:T(8,128)(2,1)} %get-tuple-element.303), channel_id=1, source_target_pairs={{0,8},{4,12},{24,16},{28,20},{1,9},{5,13},{25,17},{29,21},{2,10},{... | collective-permute-start | bytes 1572872 | tf_op jit(solution)/shard_map/ppermute | solution.py:613
  (118 other events, 1454.4 us)

commit v6 on v5

--- a/solution.py
+++ b/solution.py
@@ -11,7 +11,7 @@
 HEAD_SIZE = 128
 EPS = 1e-06
 THETA = 1000000.0
-CHUNKS = 3
+CHUNKS = 2
 F32 = jnp.float32
 BF16 = jnp.bfloat16
 
@@ -158,11 +158,13 @@
     sums_ref[0, 1:2, :] = sum_k
 
 
-def attention_call(body, micro, heads_q, heads_kv, wide, tables, out_shape, out_specs, passes):
-    seq_len = wide[0].shape[0] // micro
+def attention_call(
+    body, micro, heads_q, heads_kv, wide, tables, out_shape, out_specs, passes, first=0
+):
+    seq_len = tables[3].shape[2]
 
     def rows_of(array):
-        return pl.BlockSpec((seq_len, array.shape[1]), lambda i: (i, 0))
+        return pl.BlockSpec((seq_len, array.shape[1]), lambda i: (i + first, 0))
 
     def whole(array):
         return pl.BlockSpec(array.shape, lambda i: (0, 0))
@@ -174,7 +176,7 @@
         grid=(micro,),
         in_specs=[rows_of(array) for array in (*wide, cosine, sine, col)]
         + [
-            pl.BlockSpec((1,) + row.shape[1:], lambda i: (i, 0, 0)),
+            pl.BlockSpec((1,) + row.shape[1:], lambda i: (i + first, 0, 0)),
             whole(gain_q),
             whole(gain_k),
         ],
@@ -1008,29 +1010,33 @@
     unit_all, _ = unit_of(x_bf.astype(F32))
     a1 = (unit_all * gain_one).astype(BF16)
     (qkv,) = net.mix(g_steps, dot_nn(a1, w_qkv))
-    mixed_bf = attention_call(
-        attention_forward,
-        micro,
-        heads_q,
-        heads_kv,
-        (qkv,),
-        tables,
-        jax.ShapeDtypeStruct((rows, q_cols), BF16),
-        pl.BlockSpec((seq_len, q_cols), lambda i: (i, 0)),
-        2,
-    )
-    (mixed_bf,) = net.mix(g_steps, mixed_bf)
+    mixed = []
+    for sequence in range(micro):
+        mixed.append(
+            attention_call(
+                attention_forward,
+                1,
+                heads_q,
+                heads_kv,
+                (qkv,),
+                tables,
+                jax.ShapeDtypeStruct((seq_len, q_cols), BF16),
+                pl.BlockSpec((seq_len, q_cols), lambda i: (i, 0)),
+                2,
+                sequence,
+            )
+        )
+        if sequence == 0:
+            mixed[0], qkv = net.mix(g_steps, mixed[0], qkv)
+    mixed_bf = jnp.concatenate(mixed, axis=0)
     attn_part = dot_nt(mixed_bf, w_out_t).astype(BF16).reshape(micro, seq_len, width)
     resid, a2, w_second = net.middle_forward(attn_part, x_own, gain_two, ffn_bufs[1])
-    job_third = rounds.add(net.gather_weights(ffn_bufs[2]), 4)
     (a2,) = rounds.pump(a2.reshape(rows, width))
     w_chunks = [jnp.concatenate(job_first.value, axis=0), w_second.reshape(width, -1)]
     g_all = net.free(g_steps).reshape(rows, width)
 
     da2, inners, grad_jobs = None, [], []
     for chunk in range(CHUNKS):
-        if chunk == 2:
-            w_chunks.append(jnp.concatenate(job_third.value, axis=0))
         w_chunk = w_chunks[chunk]
         w_gu, w_down_t = w_chunk[:, : 2 * units], w_chunk[:, 2 * units :]
         gate_up = dot_nn(a2, w_gu)
@@ -1048,14 +1054,14 @@
         part_da2 = dot_nt(d_gu, w_gu)
         da2 = part_da2 if da2 is None else da2 + part_da2
         parts = [(a2, d_gu), (g_all, inner)]
-        if chunk < 2:
+        if chunk == 0:
             grad_jobs.append(rounds.add(net.scatter_grads(parts), 4))
     line = net.scatter_here(parts)
     mlp = sum(
         dot_nt(inner, w_chunk[:, 2 * units :]) for inner, w_chunk in zip(inners, w_chunks)
     )
     da2, mlp = rounds.pump(da2.astype(BF16), mlp.astype(BF16))
-    d_resid, d_resid_all, acc_ffn_gain, grad_third = net.middle_backward(
+    d_resid, d_resid_all, acc_ffn_gain, grad_second = net.middle_backward(
         da2.reshape(micro, seq_len, width), g_own, resid, gain_two, line
     )
     (d_resid_all,) = rounds.pump(d_resid_all.reshape(rows, width))
@@ -1110,7 +1116,7 @@
     )
     rounds.drain()
     grad_qkv = job_grad_qkv.value
-    grads_ffn = [*(job.value for job in grad_jobs), grad_third]
+    grads_ffn = [*(job.value for job in grad_jobs), grad_second]
 
     def own_part(start, size):
         return lax.dynamic_slice_in_dim(sums, start + net.me * size, size, 0)

time: 730 us -> 706 us (0.967)
  Pallas kernels: 269 us -> 300 us
  starting transfers between devices: 88.1 us -> 65.5 us
  matrix products: 164 us -> 144 us
  waiting for transfers between devices: 85.8 us -> 68.1 us
    ppermute x36 -> x23, waiting for transfers between devices: 83.4 us -> 51 us  [step(): lax.ppermute(array, 'dp', perm)]
    pallas_call x2, Pallas kernels: 158 us -> 187 us  [middle_call(): pl.pallas_call(body, out_shape=outputs, in_specs=[vmem] * (len(operands)...]
    ppermute x36 -> x23, starting transfers between devices: 69.3 us -> 45 us  [step(): lax.ppermute(array, 'dp', perm)]
    ppermute x2, waiting for transfers between devices: 0.01 us -> 12.5 us  [scatter_rows(): lax.ppermute(jnp.stack([first[1], first[3]]), 'tensor', XNEXT)]
    dot_general x8 -> x6, matrix products: 49 us -> 39.1 us  [dot_nn(): return jnp.dot(left, right, preferred_element_type=F32)]
    dot_general x8 -> x6, matrix products: 59.9 us -> 52.4 us  [dot_nt(): lax.dot_general(left, right, (((1,), (1,)), ((), ())), preferred_element_...]
    unnamed x174 -> x176, local copies, waits for them, and re-layouts: 19.8 us -> 24.1 us
    convert_element_type x12 -> x9, other arithmetic: 17.1 us -> 13.2 us  [add_rounded(): return (left.astype(F32) + right.astype(F32)).astype(BF16)]
  transfers between devices with their start and end apart: 63 -> 47, of which waited for: 18 -> 16; matrix products, arithmetic and copies ran while one was open for 31% -> 26% of each run, Pallas kernels for 28% -> 34%
where the time goes in v6:
time: 706 us; the launch traced here: 697 us
  Pallas kernels  300 us (42%)
  matrix products  144 us (20%)
  waiting for transfers between devices  68.1 us (10%)
  other arithmetic  67 us (9%)
  starting transfers between devices  65.5 us (9%)
  local copies, waits for them, and re-layouts  50.7 us (7%)
    pallas_call x2, Pallas kernels, middle_call(): pl.pallas_call(body, out_shape=outputs, in_specs=[vmem] * (len(operands)...  187 us
    pallas_call x1, Pallas kernels, first_gathers(): pl.pallas_call(first_gathers, out_shape=(jax.ShapeDtypeStruct((micro, 4,...  59.1 us
    dot_general x6, matrix products, dot_nt(): lax.dot_general(left, right, (((1,), (1,)), ((), ())), preferred_element_...  52.4 us
    dot_general x12, matrix products, dot_tn(): lax.dot_general(left, right, (((0,), (0,)), ((), ())), preferred_element_...  52.2 us
    ppermute x23, waiting for transfers between devices, step(): lax.ppermute(array, 'dp', perm)  51 us
    ppermute x23, starting transfers between devices, step(): lax.ppermute(array, 'dp', perm)  45 us
    pallas_call x3, Pallas kernels, attention_call(): pl.pallas_call(functools.partial(body, heads_q, heads_kv), out_shape=out_...  42.8 us
    dot_general x6, matrix products, dot_nn(): return jnp.dot(left, right, preferred_element_type=F32)  39.1 us
  transfers between devices with their start and end apart: 47, of which 16 were waited for; matrix products, arithmetic and copies ran while one was open for 26% of the time, Pallas kernels for 34%

profile of v6, /device:TPU:8, one launch (start us, length us, event | category | flops | bytes accessed | tf_op | source)
XLA Modules:
  0.0 697.4 jit_solution(11691449736094136141)
XLA Ops:
  9.1 59.1 %shard_map.274 = (bf16[2,4,128,2048]{3,2,1,0:T(8,128)(2,1)}, bf16[8,256,1024]{2,1,0:T(8,128)(2,1)}, bf16[8,256,512]{2,1,0:T(8,128)(2,1)}, bf16[8,16,128]{2,1,0:T(8,128)(2,1)}) custom-call(bf16[2,128,2048]{2,1,0:T(8,128)(2,1)} %shard_map.273.x_ref, bf16[256,1024]{1,0:T(8,128)(2,1)} %pad_maximum_fusion.16.qkv_ref, bf16[256,512]{1,0:T(8,128)(2,1)} %bitcast.151, ...), custom_call_target="tpu_custom_call" | custom-call | tf_op jit(solution)/shard_map/pallas_call | solution.py:809
  103.0 6.0 fusion.117.qkv_ref
  122.6 11.3 %shard_map.276 = bf16[512,512]{1,0:T(8,128)(2,1)} custom-call(f32[1024,1024]{1,0:T(8,128)} %fusion.117.qkv_ref, f32[1024,128]{1,0:T(8,128)} %pad_maximum_fusion.17.cos_ref, f32[1024,128]{1,0:T(8,128)} %pad_maximum_fusion.18.sin_ref, s32[1024,3]{1,0:T(8,128)} %copy.67.col_ref, s32[2,3,512]{2,1,0:T(4,128)} %pad_add_fusion.1.row_ref, ...), custom_call_target="tpu_custom_call" | custom-call | flops 536870912 | bytes 8388608 | tf_op jit(solution)/shard_map/pallas_call | solution.py:173
  136.3 7.6 %collective-permute-done.8 = bf16[256,2304]{0,1:T(8,128)(2,1)} collective-permute-done((bf16[256,2304]{0,1:T(8,128)(2,1)}, bf16[256,2304]{0,1:T(8,128)(2,1)}, u32[]{:S(2)}, u32[]{:S(2)}) %collective-permute-start.8) | collective-permute-done | bytes 1179680 | tf_op jit(solution)/shard_map/ppermute | solution.py:615
  158.0 11.3 %shard_map.277 = bf16[512,512]{1,0:T(8,128)(2,1)} custom-call(f32[1024,1024]{1,0:T(8,128)} %fusion.117.qkv_ref, f32[1024,128]{1,0:T(8,128)} %pad_maximum_fusion.17.cos_ref, f32[1024,128]{1,0:T(8,128)} %pad_maximum_fusion.18.sin_ref, s32[1024,3]{1,0:T(8,128)} %copy.67.col_ref, s32[2,3,512]{2,1,0:T(4,128)} %pad_add_fusion.1.row_ref, ...), custom_call_target="tpu_custom_call" | custom-call | flops 536870912 | bytes 8388608 | tf_op jit(solution)/shard_map/pallas_call | solution.py:173
  169.3 6.1 convolution_convert_fusion
  175.4 94.9 %shard_map.278 = (f32[2,128,2048]{2,1,0:T(8,128)}, bf16[2,4,128,2048]{3,2,1,0:T(8,128)(2,1)}, bf16[8,256,2304]{2,1,0:T(8,128)(2,1)}) custom-call(bf16[2,512,2048]{2,1,0:T(8,128)(2,1)} %bitcast.143, bf16[2,128,2048]{2,1,0:T(8,128)(2,1)} %shard_map.273.x_ref, f32[1,2048]{1,0:T(1,128)} %bitcast.159, bf16[256,2304]{1,0:T(8,128)(2,1)} %pad_maximum_fusion.7.buf_ref), custom_call_target="tpu_custom_call" | custom-call | tf_op jit(solution)/shard_map/pallas_call | solution.py:826
  283.7 8.8 %fusion.11 = f32[1024,1536]{0,1:T(8,128)S(1)} fusion(bf16[1024,2048]{1,0:T(8,128)(2,1)S(1)} %bitcast.182, bf16[2048,2304]{0,1:T(8,128)(2,1)} %constant_dynamic-update-slice_fusion), kind=kOutput, calls=%fused_computation.20 | convolution fusion | flops 6442450944 | bytes 16777216 | tf_op jit(solution)/shard_map/dot_general | solution.py:34
  292.5 6.5 multiply_convert_fusion.5
  299.0 5.9 convolution_convert_fusion.2
  308.6 6.6 fusion.7
  328.0 6.7 add_convert_fusion.3
  336.9 7.8 %multiply_convert_fusion.2 = (bf16[1024,768]{0,1:T(8,128)(2,1)S(1)}, bf16[1024,768]{0,1:T(8,128)(2,1)S(1)}, bf16[1024,768]{0,1:T(8,128)(2,1)}) fusion(f32[1024,768]{0,1:T(8,128)S(1)} %copy-done.12, f32[1024,768]{0,1:T(8,128)S(1)} %copy-done.13, bf16[1024,2048]{1,0:T(8,128)(2,1)S(1)} %bitcast.147, bf16[2048,2304]{1,0:T(8,128)(2,1)} %bitcast.171), kind=kOutput, calls=%fused_computation.37 | convolution fusion | flops 3233021952 | bytes 18350080 | tf_op jit(solution)/shard_map/dot_general | solution.py:34
  345.1 23.4 %collective-permute-done.15 = bf16[256,2304]{1,0:T(8,128)(2,1)} collective-permute-done((bf16[256,2304]{1,0:T(8,128)(2,1)S(1)}, bf16[256,2304]{1,0:T(8,128)(2,1)}, u32[]{:S(2)}, u32[]{:S(2)}) %collective-permute-start.15) | collective-permute-done | bytes 1179680 | tf_op jit(solution)/shard_map/ppermute | solution.py:615
  368.4 6.7 convolution_convert_fusion.1
  375.1 9.0 %fusion.5 = f32[1024,2048]{1,0:T(8,128)} fusion(bf16[1024,1536]{0,1:T(8,128)(2,1)S(1)} %pad_maximum_fusion.2, bf16[2048,2304]{1,0:T(8,128)(2,1)S(1)} %bitcast.178), kind=kOutput, calls=%fused_computation.14 | convolution fusion | flops 6442450944 | bytes 17825792 | tf_op jit(solution)/shard_map/dot_general | solution.py:38
  393.2 12.8 %add_convert_fusion.1 = bf16[1024,2048]{1,0:T(8,128)(2,1)} fusion(f32[1024,2048]{1,0:T(8,128)} %fusion.5, bf16[2048,2304]{0,1:T(8,128)(2,1)} %constant_dynamic-update-slice_fusion, bf16[1024,768]{0,1:T(8,128)(2,1)} %copy-done.66, bf16[1024,768]{0,1:T(8,128)(2,1)} %copy-done.64), kind=kOutput, calls=%fused_computation.8 | convolution fusion | flops 6452936704 | bytes 22020096 | tf_op jit(solution)/shard_map/dot_general | solution.py:38
  406.0 9.2 %fusion.17 = f32[1024,2048]{1,0:T(8,128)} fusion(bf16[1024,768]{0,1:T(8,128)(2,1)} %get-tuple-element.128, bf16[2048,2304]{1,0:T(8,128)(2,1)} %bitcast.172), kind=kOutput, calls=%fused_computation.45 | convolution fusion | flops 3221225472 | bytes 13107200 | tf_op jit(solution)/shard_map/dot_general | solution.py:38
  415.2 8.2 %add_convert_fusion = bf16[1024,2048]{1,0:T(8,128)(2,1)} fusion(f32[1024,2048]{1,0:T(8,128)} %fusion.17, bf16[1024,768]{0,1:T(8,128)(2,1)S(1)} %copy-done.72, bf16[2048,2304]{0,1:T(8,128)(2,1)} %constant_dynamic-update-slice_fusion), kind=kOutput, calls=%fused_computation.7 | convolution fusion | flops 3225419776 | bytes 17301504 | tf_op jit(solution)/shard_map/dot_general | solution.py:38
  442.3 92.2 %shard_map.279 = (f32[2,128,2048]{2,1,0:T(8,128)}, bf16[2,4,128,2048]{3,2,1,0:T(8,128)(2,1)}, f32[1,2048]{1,0:T(1,128)}, f32[256,2304]{1,0:T(8,128)}) custom-call(bf16[2,512,2048]{2,1,0:T(8,128)(2,1)} %bitcast.150, bf16[2,128,2048]{2,1,0:T(8,128)(2,1)} %shard_map.275.g_ref, f32[2,128,2048]{2,1,0:T(8,128)} %get-tuple-element.114.resid_ref, ...), custom_call_target="tpu_custom_call" | custom-call | tf_op jit(solution)/shard_map/pallas_call | solution.py:826
  551.4 12.5 %collective-permute-done.22 = bf16[2,128,2048]{2,1,0:T(8,128)(2,1)S(1)} collective-permute-done((bf16[2,128,2048]{2,1,0:T(8,128)(2,1)S(1)}, bf16[2,128,2048]{2,1,0:T(8,128)(2,1)S(1)}, u32[]{:S(2)}, u32[]{:S(2)}) %collective-permute-start.22) | collective-permute-done | bytes 1048608 | tf_op jit(solution)/shard_map/ppermute | solution.py:910
  569.1 20.1 %shard_map.280 = (bf16[1024,1024]{1,0:T(8,128)(2,1)}, f32[2,2,128]{2,1,0:T(2,128)}) custom-call(f32[1024,1024]{1,0:T(8,128)} %fusion.117.qkv_ref, bf16[1024,512]{1,0:T(8,128)(2,1)} %convolution_convert_fusion.3.grad_ref, f32[1024,128]{1,0:T(8,128)} %pad_maximum_fusion.17.cos_ref, f32[1024,128]{1,0:T(8,128)} %pad_maximum_fusion.18.sin_ref, ...), custom_call_target="tpu_custom_call" | custom-call | flops 2684354560 | bytes 10485760 | tf_op jit(solution)/shard_map/pallas_call | solution.py:173
  589.3 6.3 fusion.41
  607.9 7.0 %fusion.118 = f32[1024,2048]{1,0:T(8,128)S(1)} fusion(bf16[1024,1024]{1,0:T(8,128)(2,1)} %get-tuple-element.144, bf16[2048,1024]{1,0:T(8,128)(2,1)} %bitcast.179), kind=kOutput, calls=%fused_computation.255 | convolution fusion | flops 4294967296 | bytes 14680064 | tf_op jit(solution)/shard_map/dot_general | solution.py:38
  (391 shorter events, 248.6 us)
Async XLA Ops:
  70.9 38.1 %collective-permute-start.1 = (bf16[2,128,2048]{2,1,0:T(8,128)(2,1)}, bf16[2,128,2048]{2,1,0:T(8,128)(2,1)S(1)}, u32[]{:S(2)}, u32[]{:S(2)}) collective-permute-start(bf16[2,128,2048]{2,1,0:T(8,128)(2,1)} %shard_map.275.g_ref), channel_id=1, source_target_pairs={{0,2},{1,3},{2,0},{3,1},{4,6},{5,7},{6,4},{7,5},{8,10},{9,11},{10,... | collective-permute-start | bytes 3145736 | tf_op jit(solution)/shard_map/ppermute | solution.py:899
  72.5 36.6 %collective-permute-start = (bf16[2,128,2048]{2,1,0:T(8,128)(2,1)}, bf16[2,128,2048]{2,1,0:T(8,128)(2,1)S(1)}, u32[]{:S(2)}, u32[]{:S(2)}) collective-permute-start(bf16[2,128,2048]{2,1,0:T(8,128)(2,1)} %shard_map.275.g_ref), channel_id=1, source_target_pairs={{0,1},{1,0},{2,3},{3,2},{4,5},{5,4},{6,7},{7,6},{8,9},{9,8},{10,11... | collective-permute-start | bytes 3145736 | tf_op jit(solution)/shard_map/ppermute | solution.py:898
  82.9 27.9 %collective-permute-start.2 = (bf16[256,2304]{0,1:T(8,128)(2,1)}, bf16[256,2304]{0,1:T(8,128)(2,1)}, u32[]{:S(2)}, u32[]{:S(2)}) collective-permute-start(bf16[256,2304]{0,1:T(8,128)(2,1)} %get-tuple-element.102), channel_id=1, source_target_pairs={{0,8},{4,12},{8,0},{12,4},{16,24},{20,28},{24,16},{28,20},{1,9},{5... | collective-permute-start | bytes 3538952 | tf_op jit(solution)/shard_map/ppermute | solution.py:615
  85.4 28.8 %collective-permute-start.3 = (bf16[256,2304]{0,1:T(8,128)(2,1)}, bf16[256,2304]{0,1:T(8,128)(2,1)}, u32[]{:S(2)}, u32[]{:S(2)}) collective-permute-start(bf16[256,2304]{0,1:T(8,128)(2,1)} %get-tuple-element.102), channel_id=1, source_target_pairs={{8,16},{12,20},{16,8},{20,12},{9,17},{13,21},{17,9},{21,13},{10,18... | collective-permute-start | bytes 3538952 | tf_op jit(solution)/shard_map/ppermute | solution.py:615
  87.3 26.9 %collective-permute-start.4 = (bf16[256,2304]{0,1:T(8,128)(2,1)}, bf16[256,2304]{0,1:T(8,128)(2,1)}, u32[]{:S(2)}, u32[]{:S(2)}) collective-permute-start(bf16[256,2304]{0,1:T(8,128)(2,1)} %get-tuple-element.102), channel_id=1, source_target_pairs={{0,4},{4,0},{8,12},{12,8},{16,20},{20,16},{24,28},{28,24},{1,5},{5... | collective-permute-start | bytes 3538952 | tf_op jit(solution)/shard_map/ppermute | solution.py:615
  114.2 29.7 %collective-permute-start.9 = (bf16[256,2304]{0,1:T(8,128)(2,1)}, bf16[256,2304]{0,1:T(8,128)(2,1)}, u32[]{:S(2)}, u32[]{:S(2)}) collective-permute-start(bf16[256,2304]{0,1:T(8,128)(2,1)} %collective-permute-done.2), channel_id=1, source_target_pairs={{0,4},{4,0},{8,12},{12,8},{16,20},{20,16},{24,28},{28,24},{1,5},{5... | collective-permute-start | bytes 3538952 | tf_op jit(solution)/shard_map/ppermute | solution.py:615
  114.2 30.6 %collective-permute-start.7 = (bf16[256,2304]{0,1:T(8,128)(2,1)}, bf16[256,2304]{0,1:T(8,128)(2,1)}, u32[]{:S(2)}, u32[]{:S(2)}) collective-permute-start(bf16[256,2304]{0,1:T(8,128)(2,1)} %collective-permute-done.2), channel_id=1, source_target_pairs={{8,16},{12,20},{16,8},{20,12},{9,17},{13,21},{17,9},{21,13},{10,18... | collective-permute-start | bytes 3538952 | tf_op jit(solution)/shard_map/ppermute | solution.py:615
  116.4 27.5 %collective-permute-start.8 = (bf16[256,2304]{0,1:T(8,128)(2,1)}, bf16[256,2304]{0,1:T(8,128)(2,1)}, u32[]{:S(2)}, u32[]{:S(2)}) collective-permute-start(bf16[256,2304]{0,1:T(8,128)(2,1)} %collective-permute-done.3), channel_id=1, source_target_pairs={{8,0},{12,4},{16,24},{20,28},{9,1},{13,5},{17,25},{21,29},{10,2},{... | collective-permute-start | bytes 3538952 | tf_op jit(solution)/shard_map/ppermute | solution.py:615
  144.8 125.6 %collective-permute-start.10 = (bf16[256,2304]{0,1:T(8,128)(2,1)}, bf16[256,2304]{0,1:T(8,128)(2,1)}, u32[]{:S(2)}, u32[]{:S(2)}) collective-permute-start(bf16[256,2304]{0,1:T(8,128)(2,1)} %collective-permute-done.7), channel_id=1, source_target_pairs={{8,0},{12,4},{16,24},{20,28},{9,1},{13,5},{17,25},{21,29},{10,2},{... | collective-permute-start | bytes 3538952 | tf_op jit(solution)/shard_map/ppermute | solution.py:615
  152.2 118.1 %collective-permute-start.11 = (bf16[256,2304]{0,1:T(8,128)(2,1)}, bf16[256,2304]{0,1:T(8,128)(2,1)}, u32[]{:S(2)}, u32[]{:S(2)}) collective-permute-start(bf16[256,2304]{0,1:T(8,128)(2,1)} %get-tuple-element.215), channel_id=1, source_target_pairs={{0,4},{4,0},{8,12},{12,8},{16,20},{20,16},{24,28},{28,24},{1,5},{5... | collective-permute-start | bytes 3538952 | tf_op jit(solution)/shard_map/ppermute | solution.py:615
  334.9 33.6 %collective-permute-start.15 = (bf16[256,2304]{1,0:T(8,128)(2,1)S(1)}, bf16[256,2304]{1,0:T(8,128)(2,1)}, u32[]{:S(2)}, u32[]{:S(2)}) collective-permute-start(bf16[256,2304]{1,0:T(8,128)(2,1)S(1)} %fusion.74), channel_id=1, source_target_pairs={{0,8},{4,12},{24,16},{28,20},{1,9},{5,13},{25,17},{29,21},{2,10},{... | collective-permute-start | bytes 3538952 | tf_op jit(solution)/shard_map/ppermute | solution.py:615
  385.9 37.5 %collective-permute-start.17 = (bf16[256,2304]{1,0:T(8,128)(2,1)S(1)}, bf16[256,2304]{1,0:T(8,128)(2,1)S(1)}, u32[]{:S(2)}, u32[]{:S(2)}) collective-permute-start(bf16[256,2304]{1,0:T(8,128)(2,1)S(1)} %get-tuple-element.210), channel_id=1, source_target_pairs={{8,16},{12,20},{16,8},{20,12},{9,17},{13,21},{17,9},{21,13},{10,18... | collective-permute-start | bytes 3538952 | tf_op jit(solution)/shard_map/ppermute | solution.py:615
  388.3 35.1 %collective-permute-start.16 = (bf16[256,2304]{1,0:T(8,128)(2,1)S(1)}, bf16[256,2304]{1,0:T(8,128)(2,1)S(1)}, u32[]{:S(2)}, u32[]{:S(2)}) collective-permute-start(bf16[256,2304]{1,0:T(8,128)(2,1)S(1)} %get-tuple-element.211), channel_id=1, source_target_pairs={{0,8},{4,12},{24,16},{28,20},{1,9},{5,13},{25,17},{29,21},{2,10},{... | collective-permute-start | bytes 3538952 | tf_op jit(solution)/shard_map/ppermute | solution.py:615
  392.7 39.8 %collective-permute-start.19 = (bf16[1024,768]{1,0:T(8,128)(2,1)}, bf16[1024,768]{1,0:T(8,128)(2,1)S(1)}, u32[]{:S(2)}, u32[]{:S(2)}) collective-permute-start(bf16[1024,768]{1,0:T(8,128)(2,1)} %fusion.59), channel_id=1, source_target_pairs={{0,4},{4,0},{8,12},{12,8},{16,20},{20,16},{24,28},{28,24},{1,5},{5... | collective-permute-start | bytes 4718600 | tf_op jit(solution)/shard_map/ppermute | solution.py:880
  392.7 41.7 %collective-permute-start.18 = (bf16[1024,1536]{1,0:T(8,128)(2,1)}, bf16[1024,1536]{1,0:T(8,128)(2,1)}, u32[]{:S(2)}, u32[]{:S(2)}) collective-permute-start(bf16[1024,1536]{1,0:T(8,128)(2,1)} %convolution_convert_fusion.1), channel_id=1, source_target_pairs={{0,4},{4,0},{8,12},{12,8},{16,20},{20,16},{24,28},{28,24},{1,5},{5... | collective-permute-start | bytes 9437192 | tf_op jit(solution)/shard_map/ppermute | solution.py:880
  424.7 109.8 %collective-permute-start.21 = (bf16[256,2304]{1,0:T(8,128)(2,1)}, bf16[256,2304]{1,0:T(8,128)(2,1)}, u32[]{:S(2)}, u32[]{:S(2)}) collective-permute-start(bf16[256,2304]{1,0:T(8,128)(2,1)} %add_convert_fusion.7), channel_id=1, source_target_pairs={{0,8},{4,12},{8,0},{12,4},{16,24},{20,28},{24,16},{28,20},{1,9},{5... | collective-permute-start | bytes 3538952 | tf_op jit(solution)/shard_map/ppermute | solution.py:615
  428.8 105.8 %collective-permute-start.20 = (bf16[256,2304]{1,0:T(8,128)(2,1)}, bf16[256,2304]{1,0:T(8,128)(2,1)}, u32[]{:S(2)}, u32[]{:S(2)}) collective-permute-start(bf16[256,2304]{1,0:T(8,128)(2,1)} %add_convert_fusion.8), channel_id=1, source_target_pairs={{8,16},{12,20},{16,8},{20,12},{9,17},{13,21},{17,9},{21,13},{10,18... | collective-permute-start | bytes 3538952 | tf_op jit(solution)/shard_map/ppermute | solution.py:615
  538.3 25.6 %collective-permute-start.22 = (bf16[2,128,2048]{2,1,0:T(8,128)(2,1)S(1)}, bf16[2,128,2048]{2,1,0:T(8,128)(2,1)S(1)}, u32[]{:S(2)}, u32[]{:S(2)}) collective-permute-start(bf16[2,128,2048]{2,1,0:T(8,128)(2,1)S(1)} %pad_maximum_fusion.9), channel_id=1, source_target_pairs={{0,1},{1,0},{2,3},{3,2},{4,5},{5,4},{6,7},{7,6},{8,9},{9,8},{10,11... | collective-permute-start | bytes 3145736 | tf_op jit(solution)/shard_map/ppermute | solution.py:910
  539.0 25.3 %collective-permute-start.25 = (bf16[2,128,2048]{2,1,0:T(8,128)(2,1)S(1)}, bf16[2,128,2048]{2,1,0:T(8,128)(2,1)S(1)}, u32[]{:S(2)}, u32[]{:S(2)}) collective-permute-start(bf16[2,128,2048]{2,1,0:T(8,128)(2,1)S(1)} %pad_maximum_fusion.10), channel_id=1, source_target_pairs={{0,2},{1,3},{2,0},{3,1},{4,6},{5,7},{6,4},{7,5},{8,10},{9,11},{10,... | collective-permute-start | bytes 3145736 | tf_op jit(solution)/shard_map/ppermute | solution.py:911
  549.8 39.4 %collective-permute-start.27 = (bf16[256,512]{1,0:T(8,128)(2,1)}, bf16[256,512]{1,0:T(8,128)(2,1)S(1)}, u32[]{:S(2)}, u32[]{:S(2)}) collective-permute-start(bf16[256,512]{1,0:T(8,128)(2,1)} %get-tuple-element.140), channel_id=1, source_target_pairs={{0,8},{4,12},{24,16},{28,20},{1,9},{5,13},{25,17},{29,21},{2,10},{... | collective-permute-start | bytes 786440 | tf_op jit(solution)/shard_map/ppermute | solution.py:615
  565.6 23.6 %collective-permute-start.26 = (bf16[128,2048]{1,0:T(8,128)(2,1)}, bf16[128,2048]{1,0:T(8,128)(2,1)S(1)}, u32[]{:S(2)}, u32[]{:S(2)}) collective-permute-start(bf16[128,2048]{1,0:T(8,128)(2,1)} %get-tuple-element.236), channel_id=1, source_target_pairs={{0,1},{1,0},{2,3},{3,2},{4,5},{5,4},{6,7},{7,6},{8,9},{9,8},{10,11... | collective-permute-start | bytes 1572872 | tf_op jit(solution)/shard_map/ppermute | solution.py:915
  625.8 29.1 %collective-permute-start.31 = (bf16[2,128,2048]{2,1,0:T(8,128)(2,1)S(1)}, bf16[2,128,2048]{2,1,0:T(8,128)(2,1)S(1)}, u32[]{:S(2)}, u32[]{:S(2)}) collective-permute-start(bf16[2,128,2048]{2,1,0:T(8,128)(2,1)S(1)} %pad_maximum_fusion.11), channel_id=1, source_target_pairs={{0,1},{1,0},{2,3},{3,2},{4,5},{5,4},{6,7},{7,6},{8,9},{9,8},{10,11... | collective-permute-start | bytes 3145736 | tf_op jit(solution)/shard_map/ppermute | solution.py:910
  628.0 26.9 %collective-permute-start.32 = (bf16[2,128,2048]{2,1,0:T(8,128)(2,1)S(1)}, bf16[2,128,2048]{2,1,0:T(8,128)(2,1)S(1)}, u32[]{:S(2)}, u32[]{:S(2)}) collective-permute-start(bf16[2,128,2048]{2,1,0:T(8,128)(2,1)S(1)} %pad_maximum_fusion.12), channel_id=1, source_target_pairs={{0,2},{1,3},{2,0},{3,1},{4,6},{5,7},{6,4},{7,5},{8,10},{9,11},{10,... | collective-permute-start | bytes 3145736 | tf_op jit(solution)/shard_map/ppermute | solution.py:911
  643.5 29.5 %collective-permute-start.38 = (bf16[256,1024]{1,0:T(8,128)(2,1)}, bf16[256,1024]{1,0:T(8,128)(2,1)}, u32[]{:S(2)}, u32[]{:S(2)}) collective-permute-start(bf16[256,1024]{1,0:T(8,128)(2,1)} %get-tuple-element.250), channel_id=1, source_target_pairs={{0,8},{4,12},{24,16},{28,20},{1,9},{5,13},{25,17},{29,21},{2,10},{... | collective-permute-start | bytes 1572872 | tf_op jit(solution)/shard_map/ppermute | solution.py:615
  (105 other events, 1100.7 us)

commit v7 on v4

--- a/solution.py
+++ b/solution.py
@@ -536,12 +536,12 @@
     line.begin(inner)
     kept.start()
     plane.middle()
+    line.middle(inner)
     for i in range(2):
         resid = x_ref[i].astype(F32) + plane.arrive(i)
         resid_ref[i] = resid
         mine[i] = (unit_of(resid)[0] * gain_ref[...]).astype(BF16)
     share.begin()
-    line.middle(inner)
     share.middle()
     line.last(inner)
     share.end()

time: 689 us -> 687 us (level)
  no operation moved by 1% of the time
where the time goes in v7:
time: 687 us; the launch traced here: 679 us
  Pallas kernels  296 us (43%)
  matrix products  140 us (20%)
  other arithmetic  67.4 us (10%)
  starting transfers between devices  61.9 us (9%)
  waiting for transfers between devices  61.2 us (9%)
  local copies, waits for them, and re-layouts  50.1 us (7%)
    pallas_call x2, Pallas kernels, middle_call(): pl.pallas_call(body, out_shape=outputs, in_specs=[vmem] * (len(operands)...  185 us
    pallas_call x1, Pallas kernels, first_gathers(): pl.pallas_call(first_gathers, out_shape=(jax.ShapeDtypeStruct((micro, 4,...  59.1 us
    dot_general x12, matrix products, dot_tn(): lax.dot_general(left, right, (((0,), (0,)), ((), ())), preferred_element_...  49.9 us
    dot_general x6, matrix products, dot_nt(): lax.dot_general(left, right, (((1,), (1,)), ((), ())), preferred_element_...  48.2 us
    ppermute x23, waiting for transfers between devices, step(): lax.ppermute(array, 'dp', perm)  45.8 us
    dot_general x6, matrix products, dot_nn(): return jnp.dot(left, right, preferred_element_type=F32)  42 us
    ppermute x23, starting transfers between devices, step(): lax.ppermute(array, 'dp', perm)  41.4 us
    pallas_call x2, Pallas kernels, attention_call(): pl.pallas_call(functools.partial(body, heads_q, heads_kv), out_shape=out_...  40.9 us
  transfers between devices with their start and end apart: 47, of which 12 were waited for; matrix products, arithmetic and copies ran while one was open for 26% of the time, Pallas kernels for 34%

profile of v7, /device:TPU:8, one launch (start us, length us, event | category | flops | bytes accessed | tf_op | source)
XLA Modules:
  0.0 679.3 jit_solution(519360053920323770)
XLA Ops:
  9.1 59.1 %shard_map.274 = (bf16[2,4,128,2048]{3,2,1,0:T(8,128)(2,1)}, bf16[8,256,1024]{2,1,0:T(8,128)(2,1)}, bf16[8,256,512]{2,1,0:T(8,128)(2,1)}, bf16[8,16,128]{2,1,0:T(8,128)(2,1)}) custom-call(bf16[2,128,2048]{2,1,0:T(8,128)(2,1)} %shard_map.273.x_ref, bf16[256,1024]{1,0:T(8,128)(2,1)} %pad_maximum_fusion.15.qkv_ref, bf16[256,512]{1,0:T(8,128)(2,1)} %bitcast.154, ...), custom_call_target="tpu_custom_call" | custom-call | tf_op jit(solution)/shard_map/pallas_call | solution.py:803
  99.9 6.0 fusion.114.qkv_ref
  105.9 4.9 collective-permute-done.2
  126.1 20.6 %shard_map.276 = bf16[1024,512]{1,0:T(8,128)(2,1)} custom-call(f32[1024,1024]{1,0:T(8,128)} %fusion.114.qkv_ref, f32[1024,128]{1,0:T(8,128)} %pad_maximum_fusion.16.cos_ref, f32[1024,128]{1,0:T(8,128)} %pad_maximum_fusion.17.sin_ref, s32[1024,3]{1,0:T(8,128)} %copy.66.col_ref, s32[2,3,512]{2,1,0:T(4,128)} %pad_add_fusion.1.row_ref, ...), custom_call_target="tpu_custom_call" | custom-call | flops 1073741824 | bytes 8388608 | tf_op jit(solution)/shard_map/pallas_call | solution.py:171
  160.9 93.0 %shard_map.277 = (f32[2,128,2048]{2,1,0:T(8,128)}, bf16[2,4,128,2048]{3,2,1,0:T(8,128)(2,1)}, bf16[8,256,2304]{2,1,0:T(8,128)(2,1)}) custom-call(bf16[2,512,2048]{2,1,0:T(8,128)(2,1)} %bitcast.146, bf16[2,128,2048]{2,1,0:T(8,128)(2,1)} %shard_map.273.x_ref, f32[1,2048]{1,0:T(1,128)} %bitcast.160, bf16[256,2304]{1,0:T(8,128)(2,1)} %pad_maximum_fusion.7.buf_ref), custom_call_target="tpu_custom_call" | custom-call | tf_op jit(solution)/shard_map/pallas_call | solution.py:820
  268.3 8.8 %fusion.11 = f32[1024,1536]{0,1:T(8,128)S(1)} fusion(bf16[1024,2048]{1,0:T(8,128)(2,1)S(1)} %bitcast.183, bf16[2048,2304]{0,1:T(8,128)(2,1)} %constant_dynamic-update-slice_fusion), kind=kOutput, calls=%fused_computation.20 | convolution fusion | flops 6442450944 | bytes 16777216 | tf_op jit(solution)/shard_map/dot_general | solution.py:34
  277.1 6.5 multiply_convert_fusion.5
  283.6 5.9 convolution_convert_fusion.2
  293.2 6.6 fusion.7
  312.5 6.7 add_convert_fusion.3
  321.5 7.8 %multiply_convert_fusion.2 = (bf16[1024,768]{0,1:T(8,128)(2,1)S(1)}, bf16[1024,768]{0,1:T(8,128)(2,1)S(1)}, bf16[1024,768]{0,1:T(8,128)(2,1)}) fusion(f32[1024,768]{0,1:T(8,128)S(1)} %copy-done.14, f32[1024,768]{0,1:T(8,128)S(1)} %copy-done.15, bf16[1024,2048]{1,0:T(8,128)(2,1)S(1)} %bitcast.150, bf16[2048,2304]{1,0:T(8,128)(2,1)} %bitcast.172), kind=kOutput, calls=%fused_computation.37 | convolution fusion | flops 3233021952 | bytes 18350080 | tf_op jit(solution)/shard_map/dot_general | solution.py:34
  329.6 23.3 %collective-permute-done.15 = bf16[256,2304]{1,0:T(8,128)(2,1)} collective-permute-done((bf16[256,2304]{1,0:T(8,128)(2,1)S(1)}, bf16[256,2304]{1,0:T(8,128)(2,1)}, u32[]{:S(2)}, u32[]{:S(2)}) %collective-permute-start.15) | collective-permute-done | bytes 1179680 | tf_op jit(solution)/shard_map/ppermute | solution.py:613
  352.9 6.7 convolution_convert_fusion.1
  359.7 9.0 %fusion.5 = f32[1024,2048]{1,0:T(8,128)} fusion(bf16[1024,1536]{0,1:T(8,128)(2,1)S(1)} %pad_maximum_fusion.2, bf16[2048,2304]{1,0:T(8,128)(2,1)S(1)} %bitcast.179), kind=kOutput, calls=%fused_computation.14 | convolution fusion | flops 6442450944 | bytes 17825792 | tf_op jit(solution)/shard_map/dot_general | solution.py:38
  378.6 12.8 %add_convert_fusion.1 = bf16[1024,2048]{1,0:T(8,128)(2,1)} fusion(f32[1024,2048]{1,0:T(8,128)} %fusion.5, bf16[2048,2304]{0,1:T(8,128)(2,1)} %constant_dynamic-update-slice_fusion, bf16[1024,768]{0,1:T(8,128)(2,1)} %copy-done.59, bf16[1024,768]{0,1:T(8,128)(2,1)} %copy-done.57), kind=kOutput, calls=%fused_computation.8 | convolution fusion | flops 6452936704 | bytes 22020096 | tf_op jit(solution)/shard_map/dot_general | solution.py:38
  391.4 9.2 %fusion.17 = f32[1024,2048]{1,0:T(8,128)} fusion(bf16[1024,768]{0,1:T(8,128)(2,1)} %get-tuple-element.124, bf16[2048,2304]{1,0:T(8,128)(2,1)} %bitcast.173), kind=kOutput, calls=%fused_computation.45 | convolution fusion | flops 3221225472 | bytes 13107200 | tf_op jit(solution)/shard_map/dot_general | solution.py:38
  400.6 8.2 %add_convert_fusion = bf16[1024,2048]{1,0:T(8,128)(2,1)} fusion(f32[1024,2048]{1,0:T(8,128)} %fusion.17, bf16[1024,768]{0,1:T(8,128)(2,1)S(1)} %copy-done.66, bf16[2048,2304]{0,1:T(8,128)(2,1)} %constant_dynamic-update-slice_fusion), kind=kOutput, calls=%fused_computation.7 | convolution fusion | flops 3225419776 | bytes 17301504 | tf_op jit(solution)/shard_map/dot_general | solution.py:38
  419.0 5.4 add_convert_fusion.2
  426.9 92.1 %shard_map.278 = (f32[2,128,2048]{2,1,0:T(8,128)}, bf16[2,4,128,2048]{3,2,1,0:T(8,128)(2,1)}, f32[1,2048]{1,0:T(1,128)}, f32[256,2304]{1,0:T(8,128)}) custom-call(bf16[2,512,2048]{2,1,0:T(8,128)(2,1)} %bitcast.153, bf16[2,128,2048]{2,1,0:T(8,128)(2,1)} %shard_map.275.g_ref, f32[2,128,2048]{2,1,0:T(8,128)} %get-tuple-element.110.resid_ref, ...), custom_call_target="tpu_custom_call" | custom-call | tf_op jit(solution)/shard_map/pallas_call | solution.py:820
  519.0 6.3 convolution_convert_fusion.3.grad_ref
  538.4 20.3 %shard_map.279 = (bf16[1024,1024]{1,0:T(8,128)(2,1)}, f32[2,2,128]{2,1,0:T(2,128)}) custom-call(f32[1024,1024]{1,0:T(8,128)} %fusion.114.qkv_ref, bf16[1024,512]{1,0:T(8,128)(2,1)} %convolution_convert_fusion.3.grad_ref, f32[1024,128]{1,0:T(8,128)} %pad_maximum_fusion.16.cos_ref, f32[1024,128]{1,0:T(8,128)} %pad_maximum_fusion.17.sin_ref, ...), custom_call_target="tpu_custom_call" | custom-call | flops 2684354560 | bytes 10485760 | tf_op jit(solution)/shard_map/pallas_call | solution.py:171
  574.7 7.1 %collective-permute-done.27 = bf16[256,512]{1,0:T(8,128)(2,1)S(1)} collective-permute-done((bf16[256,512]{1,0:T(8,128)(2,1)S(1)}, bf16[256,512]{1,0:T(8,128)(2,1)S(1)}, u32[]{:S(2)}, u32[]{:S(2)}) %collective-permute-start.27) | collective-permute-done | bytes 262176 | tf_op jit(solution)/shard_map/ppermute | solution.py:613
  625.1 6.4 collective-permute-done.30
  668.9 5.1 collective-permute-done.46
  (378 shorter events, 238.9 us)
Async XLA Ops:
  71.0 35.0 %collective-permute-start.1 = (bf16[2,128,2048]{2,1,0:T(8,128)(2,1)}, bf16[2,128,2048]{2,1,0:T(8,128)(2,1)S(1)}, u32[]{:S(2)}, u32[]{:S(2)}) collective-permute-start(bf16[2,128,2048]{2,1,0:T(8,128)(2,1)} %shard_map.275.g_ref), channel_id=1, source_target_pairs={{0,2},{1,3},{2,0},{3,1},{4,6},{5,7},{6,4},{7,5},{8,10},{9,11},{10,... | collective-permute-start | bytes 3145736 | tf_op jit(solution)/shard_map/ppermute | solution.py:897
  72.5 33.4 %collective-permute-start = (bf16[2,128,2048]{2,1,0:T(8,128)(2,1)}, bf16[2,128,2048]{2,1,0:T(8,128)(2,1)S(1)}, u32[]{:S(2)}, u32[]{:S(2)}) collective-permute-start(bf16[2,128,2048]{2,1,0:T(8,128)(2,1)} %shard_map.275.g_ref), channel_id=1, source_target_pairs={{0,1},{1,0},{2,3},{3,2},{4,5},{5,4},{6,7},{7,6},{8,9},{9,8},{10,11... | collective-permute-start | bytes 3145736 | tf_op jit(solution)/shard_map/ppermute | solution.py:896
  83.0 27.9 %collective-permute-start.2 = (bf16[256,2304]{0,1:T(8,128)(2,1)}, bf16[256,2304]{0,1:T(8,128)(2,1)}, u32[]{:S(2)}, u32[]{:S(2)}) collective-permute-start(bf16[256,2304]{0,1:T(8,128)(2,1)} %get-tuple-element.99), channel_id=1, source_target_pairs={{0,8},{4,12},{8,0},{12,4},{16,24},{20,28},{24,16},{28,20},{1,9},{5... | collective-permute-start | bytes 3538952 | tf_op jit(solution)/shard_map/ppermute | solution.py:613
  85.4 28.8 %collective-permute-start.3 = (bf16[256,2304]{0,1:T(8,128)(2,1)}, bf16[256,2304]{0,1:T(8,128)(2,1)}, u32[]{:S(2)}, u32[]{:S(2)}) collective-permute-start(bf16[256,2304]{0,1:T(8,128)(2,1)} %get-tuple-element.99), channel_id=1, source_target_pairs={{8,16},{12,20},{16,8},{20,12},{9,17},{13,21},{17,9},{21,13},{10,18... | collective-permute-start | bytes 3538952 | tf_op jit(solution)/shard_map/ppermute | solution.py:613
  87.4 26.9 %collective-permute-start.4 = (bf16[256,2304]{0,1:T(8,128)(2,1)}, bf16[256,2304]{0,1:T(8,128)(2,1)}, u32[]{:S(2)}, u32[]{:S(2)}) collective-permute-start(bf16[256,2304]{0,1:T(8,128)(2,1)} %get-tuple-element.99), channel_id=1, source_target_pairs={{0,4},{4,0},{8,12},{12,8},{16,20},{20,16},{24,28},{28,24},{1,5},{5... | collective-permute-start | bytes 3538952 | tf_op jit(solution)/shard_map/ppermute | solution.py:613
  114.2 35.0 %collective-permute-start.9 = (bf16[256,2304]{0,1:T(8,128)(2,1)}, bf16[256,2304]{0,1:T(8,128)(2,1)}, u32[]{:S(2)}, u32[]{:S(2)}) collective-permute-start(bf16[256,2304]{0,1:T(8,128)(2,1)} %collective-permute-done.2), channel_id=1, source_target_pairs={{0,4},{4,0},{8,12},{12,8},{16,20},{20,16},{24,28},{28,24},{1,5},{5... | collective-permute-start | bytes 3538952 | tf_op jit(solution)/shard_map/ppermute | solution.py:613
  114.2 35.0 %collective-permute-start.7 = (bf16[256,2304]{0,1:T(8,128)(2,1)}, bf16[256,2304]{0,1:T(8,128)(2,1)}, u32[]{:S(2)}, u32[]{:S(2)}) collective-permute-start(bf16[256,2304]{0,1:T(8,128)(2,1)} %collective-permute-done.2), channel_id=1, source_target_pairs={{8,16},{12,20},{16,8},{20,12},{9,17},{13,21},{17,9},{21,13},{10,18... | collective-permute-start | bytes 3538952 | tf_op jit(solution)/shard_map/ppermute | solution.py:613
  116.4 32.8 %collective-permute-start.8 = (bf16[256,2304]{0,1:T(8,128)(2,1)}, bf16[256,2304]{0,1:T(8,128)(2,1)}, u32[]{:S(2)}, u32[]{:S(2)}) collective-permute-start(bf16[256,2304]{0,1:T(8,128)(2,1)} %collective-permute-done.3), channel_id=1, source_target_pairs={{8,0},{12,4},{16,24},{20,28},{9,1},{13,5},{17,25},{21,29},{10,2},{... | collective-permute-start | bytes 3538952 | tf_op jit(solution)/shard_map/ppermute | solution.py:613
  119.9 29.3 %collective-permute-start.6 = (bf16[128,2048]{1,0:T(8,128)(2,1)}, bf16[128,2048]{1,0:T(8,128)(2,1)}, u32[]{:S(2)}, u32[]{:S(2)}) collective-permute-start(bf16[128,2048]{1,0:T(8,128)(2,1)} %slice_bitcast_fusion.12), channel_id=1, source_target_pairs={{0,1},{1,0},{2,3},{3,2},{4,5},{5,4},{6,7},{7,6},{8,9},{9,8},{10,11... | collective-permute-start | bytes 1572872 | tf_op jit(solution)/shard_map/ppermute | solution.py:901
  121.5 27.7 %collective-permute-start.5 = (bf16[128,2048]{1,0:T(8,128)(2,1)}, bf16[128,2048]{1,0:T(8,128)(2,1)}, u32[]{:S(2)}, u32[]{:S(2)}) collective-permute-start(bf16[128,2048]{1,0:T(8,128)(2,1)} %slice_bitcast_fusion.13), channel_id=1, source_target_pairs={{0,2},{1,3},{2,0},{3,1},{4,6},{5,7},{6,4},{7,5},{8,10},{9,11},{10,... | collective-permute-start | bytes 1572872 | tf_op jit(solution)/shard_map/ppermute | solution.py:900
  149.3 104.8 %collective-permute-start.10 = (bf16[256,2304]{0,1:T(8,128)(2,1)}, bf16[256,2304]{0,1:T(8,128)(2,1)}, u32[]{:S(2)}, u32[]{:S(2)}) collective-permute-start(bf16[256,2304]{0,1:T(8,128)(2,1)} %collective-permute-done.7), channel_id=1, source_target_pairs={{8,0},{12,4},{16,24},{20,28},{9,1},{13,5},{17,25},{21,29},{10,2},{... | collective-permute-start | bytes 3538952 | tf_op jit(solution)/shard_map/ppermute | solution.py:613
  154.8 99.2 %collective-permute-start.11 = (bf16[256,2304]{0,1:T(8,128)(2,1)}, bf16[256,2304]{0,1:T(8,128)(2,1)}, u32[]{:S(2)}, u32[]{:S(2)}) collective-permute-start(bf16[256,2304]{0,1:T(8,128)(2,1)} %get-tuple-element.209), channel_id=1, source_target_pairs={{0,4},{4,0},{8,12},{12,8},{16,20},{20,16},{24,28},{28,24},{1,5},{5... | collective-permute-start | bytes 3538952 | tf_op jit(solution)/shard_map/ppermute | solution.py:613
  319.4 33.6 %collective-permute-start.15 = (bf16[256,2304]{1,0:T(8,128)(2,1)S(1)}, bf16[256,2304]{1,0:T(8,128)(2,1)}, u32[]{:S(2)}, u32[]{:S(2)}) collective-permute-start(bf16[256,2304]{1,0:T(8,128)(2,1)S(1)} %fusion.74), channel_id=1, source_target_pairs={{0,8},{4,12},{24,16},{28,20},{1,9},{5,13},{25,17},{29,21},{2,10},{... | collective-permute-start | bytes 3538952 | tf_op jit(solution)/shard_map/ppermute | solution.py:613
  370.4 38.5 %collective-permute-start.17 = (bf16[256,2304]{1,0:T(8,128)(2,1)S(1)}, bf16[256,2304]{1,0:T(8,128)(2,1)S(1)}, u32[]{:S(2)}, u32[]{:S(2)}) collective-permute-start(bf16[256,2304]{1,0:T(8,128)(2,1)S(1)} %get-tuple-element.204), channel_id=1, source_target_pairs={{8,16},{12,20},{16,8},{20,12},{9,17},{13,21},{17,9},{21,13},{10,18... | collective-permute-start | bytes 3538952 | tf_op jit(solution)/shard_map/ppermute | solution.py:613
  373.7 35.2 %collective-permute-start.16 = (bf16[256,2304]{1,0:T(8,128)(2,1)S(1)}, bf16[256,2304]{1,0:T(8,128)(2,1)S(1)}, u32[]{:S(2)}, u32[]{:S(2)}) collective-permute-start(bf16[256,2304]{1,0:T(8,128)(2,1)S(1)} %get-tuple-element.205), channel_id=1, source_target_pairs={{0,8},{4,12},{24,16},{28,20},{1,9},{5,13},{25,17},{29,21},{2,10},{... | collective-permute-start | bytes 3538952 | tf_op jit(solution)/shard_map/ppermute | solution.py:613
  378.1 39.0 %collective-permute-start.19 = (bf16[1024,768]{1,0:T(8,128)(2,1)}, bf16[1024,768]{1,0:T(8,128)(2,1)S(1)}, u32[]{:S(2)}, u32[]{:S(2)}) collective-permute-start(bf16[1024,768]{1,0:T(8,128)(2,1)} %fusion.59), channel_id=1, source_target_pairs={{0,4},{4,0},{8,12},{12,8},{16,20},{20,16},{24,28},{28,24},{1,5},{5... | collective-permute-start | bytes 4718600 | tf_op jit(solution)/shard_map/ppermute | solution.py:874
  378.1 40.9 %collective-permute-start.18 = (bf16[1024,1536]{1,0:T(8,128)(2,1)}, bf16[1024,1536]{1,0:T(8,128)(2,1)}, u32[]{:S(2)}, u32[]{:S(2)}) collective-permute-start(bf16[1024,1536]{1,0:T(8,128)(2,1)} %convolution_convert_fusion.1), channel_id=1, source_target_pairs={{0,4},{4,0},{8,12},{12,8},{16,20},{20,16},{24,28},{28,24},{1,5},{5... | collective-permute-start | bytes 9437192 | tf_op jit(solution)/shard_map/ppermute | solution.py:874
  410.2 108.8 %collective-permute-start.21 = (bf16[256,2304]{1,0:T(8,128)(2,1)}, bf16[256,2304]{1,0:T(8,128)(2,1)}, u32[]{:S(2)}, u32[]{:S(2)}) collective-permute-start(bf16[256,2304]{1,0:T(8,128)(2,1)} %add_convert_fusion.7), channel_id=1, source_target_pairs={{0,8},{4,12},{8,0},{12,4},{16,24},{20,28},{24,16},{28,20},{1,9},{5... | collective-permute-start | bytes 3538952 | tf_op jit(solution)/shard_map/ppermute | solution.py:613
  414.2 104.7 %collective-permute-start.20 = (bf16[256,2304]{1,0:T(8,128)(2,1)}, bf16[256,2304]{1,0:T(8,128)(2,1)}, u32[]{:S(2)}, u32[]{:S(2)}) collective-permute-start(bf16[256,2304]{1,0:T(8,128)(2,1)} %add_convert_fusion.8), channel_id=1, source_target_pairs={{8,16},{12,20},{16,8},{20,12},{9,17},{13,21},{17,9},{21,13},{10,18... | collective-permute-start | bytes 3538952 | tf_op jit(solution)/shard_map/ppermute | solution.py:613
  530.7 37.1 %collective-permute-start.26 = (bf16[1024,512]{1,0:T(8,128)(2,1)}, bf16[1024,512]{1,0:T(8,128)(2,1)}, u32[]{:S(2)}, u32[]{:S(2)}) collective-permute-start(bf16[1024,512]{1,0:T(8,128)(2,1)} %fusion.68), channel_id=1, source_target_pairs={{0,4},{4,0},{8,12},{12,8},{16,20},{20,16},{24,28},{28,24},{1,5},{5... | collective-permute-start | bytes 3145736 | tf_op jit(solution)/shard_map/ppermute | solution.py:883
  533.4 31.0 %collective-permute-start.22 = (bf16[2,128,2048]{2,1,0:T(8,128)(2,1)}, bf16[2,128,2048]{2,1,0:T(8,128)(2,1)}, u32[]{:S(2)}, u32[]{:S(2)}) collective-permute-start(bf16[2,128,2048]{2,1,0:T(8,128)(2,1)} %pad_maximum_fusion.8), channel_id=1, source_target_pairs={{0,1},{1,0},{2,3},{3,2},{4,5},{5,4},{6,7},{7,6},{8,9},{9,8},{10,11... | collective-permute-start | bytes 3145736 | tf_op jit(solution)/shard_map/ppermute | solution.py:908
  536.0 28.4 %collective-permute-start.24 = (bf16[2,128,2048]{2,1,0:T(8,128)(2,1)}, bf16[2,128,2048]{2,1,0:T(8,128)(2,1)}, u32[]{:S(2)}, u32[]{:S(2)}) collective-permute-start(bf16[2,128,2048]{2,1,0:T(8,128)(2,1)} %pad_maximum_fusion.9), channel_id=1, source_target_pairs={{0,2},{1,3},{2,0},{3,1},{4,6},{5,7},{6,4},{7,5},{8,10},{9,11},{10,... | collective-permute-start | bytes 3145736 | tf_op jit(solution)/shard_map/ppermute | solution.py:909
  620.3 28.5 %collective-permute-start.44 = (f32[4352]{0:T(1024)S(1)}, f32[4352]{0:T(1024)S(1)}, u32[]{:S(2)}, u32[]{:S(2)}) collective-permute-start(f32[4352]{0:T(1024)S(1)} %add.221), channel_id=1, source_target_pairs={{0,16},{4,20},{8,24},{12,28},{16,0},{20,4},{24,8},{28,12},{1,17},{... | collective-permute-start | bytes 52232 | tf_op jit(solution)/shard_map/ppermute | solution.py:787
  623.8 30.2 %collective-permute-start.38 = (bf16[256,1024]{1,0:T(8,128)(2,1)}, bf16[256,1024]{1,0:T(8,128)(2,1)}, u32[]{:S(2)}, u32[]{:S(2)}) collective-permute-start(bf16[256,1024]{1,0:T(8,128)(2,1)} %get-tuple-element.244), channel_id=1, source_target_pairs={{0,8},{4,12},{24,16},{28,20},{1,9},{5,13},{25,17},{29,21},{2,10},{... | collective-permute-start | bytes 1572872 | tf_op jit(solution)/shard_map/ppermute | solution.py:613
  (99 other events, 1118.7 us)
